TPU v7x, 32 devices: a whole 2x2x4 slice. The times are simulated.
32 devices in a mesh: dp: 16 (over z, x, core), tp: 2 (over y).
Axes of the slice: x: 2, y: 2, z: 4, core: 2. Of those that a mesh axis runs over, the one named last changes fastest.
Arguments:
- layer_in: bfloat16 [16384, 768], P(('dp', 'tp')), may hold values from -6 to 6
- lengths: int32 [128, 17], P('dp'), may hold values from 0 to 77, as said below
- attn_gain: float32 [768], replicated, may hold values from 0.25 to 1.75
- attn_shift: float32 [768], replicated, may hold values from -2 to 2
- qkv_weight: bfloat16 [768, 3, 768], P(None, None, 'tp'), may hold values from -0.21875 to 0.21875
- qv_bias: float32 [2, 768], P(None, 'tp'), may hold values from -3 to 3
- out_weight: bfloat16 [768, 768], P('tp'), may hold values from -0.875 to 0.875
- out_bias: float32 [768], replicated, may hold values from -2 to 2
- mlp_gain: float32 [768], replicated, may hold values from 0.25 to 1.75
- mlp_shift: float32 [768], replicated, may hold values from -2 to 2
- up_weight: bfloat16 [768, 3072], P(None, 'tp'), may hold values from -0.21875 to 0.21875
- up_bias: float32 [3072], P('tp'), may hold values from -3 to 3
- down_weight: bfloat16 [3072, 768], P('tp'), may hold values from -0.15625 to 0.15625
- down_bias: float32 [768], replicated, may hold values from -2 to 2
- cotangent: bfloat16 [16384, 768], P(('dp', 'tp')), may hold values from -6 to 6
Outputs:
- layer_out: bfloat16 [16384, 768], P(('dp', 'tp'))
- in_grad: bfloat16 [16384, 768], P(('dp', 'tp'))
- attn_gain_grad: float32 [768], replicated
- attn_shift_grad: float32 [768], replicated
- qkv_weight_grad: float32 [768, 3, 768], P(None, None, 'tp')
- qv_bias_grad: float32 [2, 768], P(None, 'tp')
- out_weight_grad: float32 [768, 768], P('tp')
- out_bias_grad: float32 [768], replicated
- mlp_gain_grad: float32 [768], replicated
- mlp_shift_grad: float32 [768], replicated
- up_weight_grad: float32 [768, 3072], P(None, 'tp')
- up_bias_grad: float32 [3072], P('tp')
- down_weight_grad: float32 [3072, 768], P('tp')
- down_bias_grad: float32 [768], replicated
Inputs may be any that keep to these rules, and one draw needn't show every extreme that they name: Row r's captions take lengths[r, 0], lengths[r, 1], ... tokens in order from slot 0; each entry is 0 or between 8 and 77; after a 0 all entries of the row are 0; a row's entries sum to at most 128, and its slots from that sum on are padding.
All inputs are finite; a program needn't handle non-finite values.
Results may differ from a plain program's by a relative error of at most 0.017.
Values may be sent and summed in bfloat16 or wider, within the bound.
No kernel may reach another device: no remote copies, remote signals or barrier semaphores. Data moves between devices by JAX's collectives and lax.ppermute only.
A program may use at most 128 MiB of HBM per device.

v0:
```python
import math

import jax
import jax.numpy as jnp
from jax import lax
from jax.experimental import pallas as pl
from jax.experimental.pallas import tpu as pltpu
from jax.sharding import PartitionSpec as P

HEAD = 64
SEQ = 128
UNITS = 4
EPS = 1e-05
SCALE = 1.0 / math.sqrt(HEAD)
F32 = jnp.float32
BF16 = jnp.bfloat16

VM = pl.BlockSpec(memory_space=pltpu.VMEM)
SM = pl.BlockSpec(memory_space=pltpu.SMEM)
HB = pl.BlockSpec(memory_space=pl.ANY)

NEAR_FIRST, FAR_FIRST = (0, 2, 1, 3), (0, 1, 2, 3)
TP_BIT, CORE_BIT, NEAR_BIT, FAR_BIT, FIRST_REST = 0, 1, 2, 3, 4
TP, CORE, NEAR, FAR = (1 << bit for bit in (TP_BIT, CORE_BIT, NEAR_BIT, FAR_BIT))


def nn(a, b):
    return lax.dot_general(a, b, (((1,), (0,)), ((), ())), preferred_element_type=F32)


def nt(a, b):
    return lax.dot_general(a, b, (((1,), (1,)), ((), ())), preferred_element_type=F32)


def tn(a, b):
    return lax.dot_general(a, b, (((0,), (0,)), ((), ())), preferred_element_type=F32)


def normalize(values):
    center = values - jnp.mean(values, axis=-1, keepdims=True)
    inv = lax.rsqrt(jnp.mean(center * center, axis=-1, keepdims=True) + EPS)
    return center * inv, inv


def norm_back(values, grad, gain):
    normed, inv = normalize(values)
    scaled = grad * gain
    mean_g = jnp.mean(scaled, axis=-1, keepdims=True)
    mean_gn = jnp.mean(scaled * normed, axis=-1, keepdims=True)
    part = inv * (scaled - mean_g - normed * mean_gn)
    gain_sum = jnp.sum(grad * normed, axis=0, keepdims=True)
    shift_sum = jnp.sum(grad, axis=0, keepdims=True)
    return part, gain_sum, shift_sum


def row_mask(lens, row):
    at_k = lax.broadcasted_iota(jnp.int32, (SEQ, 1), 0)
    at_q = lax.broadcasted_iota(jnp.int32, (1, SEQ), 1)
    total = jnp.int32(0)
    seg_q = jnp.zeros((1, SEQ), jnp.int32)
    seg_k = jnp.zeros((SEQ, 1), jnp.int32)
    for entry in range(lens.shape[1]):
        total = total + lens[row, entry]
        seg_q = seg_q + jnp.where(at_q >= total, 1, 0)
        seg_k = seg_k + jnp.where(at_k >= total, 1, 0)
    allowed = (seg_q == seg_k) & (at_k <= at_q) & ((at_k < total) | (at_k == at_q))
    valid = jnp.where(at_k < total, 1.0, 0.0).astype(F32)
    return jnp.concatenate([allowed, allowed], axis=1), valid


def low_lanes():
    return lax.broadcasted_iota(jnp.int32, (SEQ, 2 * HEAD), 1) < HEAD


def stack_pair(pair, low):
    zero = jnp.zeros_like(pair)
    return jnp.concatenate([jnp.where(low, pair, zero), jnp.where(low, zero, pair)], axis=0)


def pair_probs(q_stack, keys, allowed2):
    scores = jnp.where(allowed2, nt(keys, q_stack) * SCALE, -1e30)
    weights = jnp.exp(scores - jnp.max(scores, axis=0, keepdims=True))
    return weights * (1.0 / jnp.sum(weights, axis=0, keepdims=True))


class Copies:
    def __init__(self, sems):
        self.sems = sems
        self.count = 0

    def start(self, src, dst):
        made = pltpu.make_async_copy(src, dst, self.sems.at[self.count])
        self.count += 1
        made.start()
        return made


def wait(*copies):
    for made in copies:
        made.wait()


def blocks(count, size=SEQ):
    return [slice(i * size, (i + 1) * size) for i in range(count)]


def over_rows(tokens, body, start):
    at = lambda i: pl.ds(pl.multiple_of(i * SEQ, SEQ), SEQ)
    return lax.fori_loop(0, tokens // SEQ, lambda i, carry: body(at(i), carry), start)


def project(nrm, w, bias, qkv):
    width = w.shape[2]
    for part in range(3):
        value = nn(nrm[...], w[part])
        if part != 1:
            value = value + bias[pl.ds(part // 2, 1), :]
        qkv[:, part * width : (part + 1) * width] = value.astype(BF16)


def attend(lens, ids, qkv, att):
    width = att.shape[1]
    rows = att.shape[0] // SEQ
    low = low_lanes()
    @pl.loop(0, rows, unroll=2)
    def _(row):
        at = pl.ds(pl.multiple_of(row * SEQ, SEQ), SEQ)
        allowed2, valid = row_mask(lens, ids[0] * rows + row)
        for first in range(0, width, 2 * HEAD):
            q = qkv[at, first : first + 2 * HEAD]
            k = qkv[at, width + first : width + first + 2 * HEAD]
            v = qkv[at, 2 * width + first : 2 * width + first + 2 * HEAD]
            probs = pair_probs(stack_pair(q, low), k, allowed2)
            both = tn(probs.astype(BF16), v)
            out = jnp.where(low, both[:SEQ], both[SEQ:]) * valid
            att[at, first : first + 2 * HEAD] = out.astype(BF16)


def own_fwd_kernel(lens, ids, x_hbm, vecs, w_hbm, bias, nrm_hbm, qkv_hbm, att, x, w, nrm, qkv, sems):
    copies = Copies(sems)
    x_in = copies.start(x_hbm, x)
    w_in = copies.start(w_hbm, w)
    wait(x_in)

    def norm_rows(at, carry):
        normed, _ = normalize(x[at, :].astype(F32))
        nrm[at, :] = (normed * vecs[0:1, :] + vecs[1:2, :]).astype(BF16)
        return carry

    over_rows(x.shape[0], norm_rows, 0)
    nrm_out = copies.start(nrm, nrm_hbm)
    wait(w_in)
    project(nrm, w, bias, qkv)
    qkv_out = copies.start(qkv, qkv_hbm)
    attend(lens, ids, qkv, att)
    wait(nrm_out, qkv_out)


def unit_block(part, rows, width, first=0):
    return pl.ds(first + (part // 2) * rows, rows), pl.ds((part % 2) * width, width)


def fetch_weights(copies, ids, mine_parts, sib_parts, w, wo):
    core, mine = ids[1], ids[2]
    width = w.shape[2]
    part_rows = w.shape[1] // (2 * UNITS)
    to_w, to_wo = [], []
    for side, parts in ((core, mine_parts), (1 - core, sib_parts)):
        for step, unit_ref in enumerate(parts):
            unit = jnp.bitwise_xor(mine, step)
            at_w = pl.ds(pl.multiple_of((side * UNITS + unit) * part_rows, part_rows), part_rows)
            at_o = pl.ds(pl.multiple_of(unit * part_rows, part_rows), part_rows)
            cols = pl.ds(pl.multiple_of(side * width, width), width)
            for part in range(3):
                to_w.append(copies.start(unit_ref.at[unit_block(part, part_rows, width)], w.at[part, at_w, :]))
            if wo is not None:
                to_wo.append(copies.start(unit_ref.at[unit_block(3, part_rows, width)], wo.at[at_o, cols]))
    return to_w, to_wo


def fetch_output_weight(copies, ids, mine_parts, sib_parts, wo):
    core, mine = ids[1], ids[2]
    width = wo.shape[0]
    part_rows = width // UNITS
    made = []
    for side, parts in ((core, mine_parts), (1 - core, sib_parts)):
        for step, unit_ref in enumerate(parts):
            at_o = pl.ds(pl.multiple_of(jnp.bitwise_xor(mine, step) * part_rows, part_rows), part_rows)
            cols = pl.ds(pl.multiple_of(side * width, width), width)
            made.append(copies.start(unit_ref.at[unit_block(3, part_rows, width)], wo.at[at_o, cols]))
    return made


def other_fwd_kernel(lens, ids, x_hbm, nrm_hbm, bias, att_own_hbm, wo_own_hbm, vecs, *refs):
    mine_parts, sib_parts = refs[:4], refs[4:8]
    qkv_hbm, att_hbm, mid_hbm, nm = refs[8:12]
    x, nrm, att_own, wo_own, w, wo, qkv, att, mid, sems = refs[12:]
    copies = Copies(sems)
    nrm_in = copies.start(nrm_hbm, nrm)
    to_w, to_wo = fetch_weights(copies, ids, mine_parts, sib_parts, w, wo)
    late = [copies.start(x_hbm, x), copies.start(att_own_hbm, att_own), copies.start(wo_own_hbm, wo_own)]
    wait(nrm_in, *to_w)
    project(nrm, w, bias, qkv)
    qkv_out = copies.start(qkv, qkv_hbm)
    attend(lens, ids, qkv, att)
    att_out = copies.start(att, att_hbm)
    wait(*to_wo, *late)
    mid[...] = nn(att_own[...], wo_own[...]) + nn(att[...], wo[...])

    def norm_rows(at, carry):
        value = x[at, :].astype(F32) + mid[at, :] + vecs[2:3, :]
        mid[at, :] = value
        normed, _ = normalize(value)
        nm[at, :] = (normed * vecs[3:4, :] + vecs[4:5, :]).astype(BF16)
        return carry

    over_rows(x.shape[0], norm_rows, 0)
    mid_out = copies.start(mid, mid_hbm)
    wait(qkv_out, att_out, mid_out)


def gelu_parts(pre):
    bell = jnp.exp(-0.5 * pre * pre)
    t = 1.0 / (1.0 + (0.3275911 * math.sqrt(0.5)) * jnp.abs(pre))
    poly = 1.061405429 * t - 1.453152027
    poly = poly * t + 1.421413741
    poly = poly * t - 0.284496736
    poly = poly * t + 0.254829592
    tail = 0.5 * (poly * t) * bell
    cdf = jnp.where(pre >= 0, 1.0 - tail, tail)
    return pre * cdf, cdf + pre * bell * (1.0 / math.sqrt(2.0 * math.pi))


def mlp_kernel(own, *refs):
    ids, nm_a, nm_b, ct_a, ct_b, bias = refs[:6]
    if own:
        up_hbm, down_hbm = refs[6:8]
        out_hbm, dnm_hbm, keep_a, send_a, keep_b, send_b, bias_g = refs[8:15]
        scratch = refs[15:]
    else:
        units, (out_prev, dnm_prev) = refs[6:10], refs[10:12]
        out_own_hbm, out_sib_hbm, dnm_own_hbm, dnm_sib_hbm, keep_a, send_a, keep_b, send_b, bias_g = refs[12:21]
        scratch = refs[21:]
    up, down, nm, ct, pre, dact, act, pg, gu, gd, sems = scratch[:11]
    core, mine = ids[1], ids[2]
    hidden = up.shape[1]
    tokens = nm_a.shape[0]
    unit_rows = up.shape[0] // UNITS
    copies = Copies(sems)
    copy = copies.start
    halves = (pl.ds(0, tokens), pl.ds(tokens, tokens))

    def unit_at(step):
        start = jnp.bitwise_xor(mine, step) * unit_rows
        return pl.ds(pl.multiple_of(start, unit_rows), unit_rows)

    at = pl.ds(pl.multiple_of(core * hidden, hidden), hidden)
    if own:
        ups = [copy(up_hbm.at[:, at], up)]
    else:
        ups = [copy(unit.at[pl.ds(0, unit_rows)], up.at[unit_at(i), :]) for i, unit in enumerate(units)]
    nms = [copy(nm_a, nm.at[halves[0]])]
    if own:
        downs = [copy(down_hbm.at[at, :], down)]
    else:
        downs = [copy(unit.at[pl.ds(unit_rows, unit_rows)], down.at[unit_at(i), :]) for i, unit in enumerate(units)]
    cts = [copy(ct_a, ct.at[halves[0]])]
    nms.append(copy(nm_b, nm.at[halves[1]]))
    cts.append(copy(ct_b, ct.at[halves[1]]))
    if not own:
        prev_out, prev_dnm, dnm_own, dnm_sib, out_own, out_sib = scratch[11:17]
        lates = [copy(dnm_prev, prev_dnm), copy(out_prev, prev_out)]
    else:
        dnm, out = scratch[11:13]

    piece = 16

    def half_step(half, total):
        rows = pl.ds(pl.multiple_of(half * tokens, tokens), tokens)
        for i in range(2):
            pl.when(half == i)(lambda: wait(nms[i], *(ups if i == 0 else ())))
        pre[...] = nn(nm[rows, :], up[...])
        for i in range(2):
            pl.when(half == i)(lambda: wait(cts[i], *(downs if i == 0 else ())))
        dact[...] = nt(ct[rows, :], down[...])

        def elementwise(step, total):
            at = pl.ds(pl.multiple_of(step * piece, piece), piece)
            to = pl.ds(pl.multiple_of(half * tokens + step * piece, piece), piece)
            value, slope = gelu_parts(pre[at, :] + bias[...])
            act[to, :] = value.astype(BF16)
            back = (dact[at, :] * slope).astype(BF16)
            pg[to, :] = back
            return total + jnp.sum(back.astype(F32), axis=0, keepdims=True)

        return lax.fori_loop(0, tokens // piece, elementwise, total, unroll=2)

    bias_sum = lax.fori_loop(0, 2, half_step, jnp.zeros((1, hidden), F32))
    bias_g[...] = bias_sum
    writes = []
    if own:
        dnm[...] = nt(pg[...], up[...]).astype(BF16)
        writes.append(copy(dnm, dnm_hbm))
        out[...] = nn(act[...], down[...]).astype(BF16)
        writes.append(copy(out, out_hbm))
    else:
        wait(*lates)
        total = nt(pg[...], up[...])
        dnm_own[...] = total[:tokens] + prev_dnm[:tokens, :].astype(F32)
        dnm_sib[...] = (total[tokens:] + prev_dnm[tokens:, :].astype(F32)).astype(BF16)
        writes += [copy(dnm_own, dnm_own_hbm), copy(dnm_sib, dnm_sib_hbm)]
        total = nn(act[...], down[...])
        out_own[...] = total[:tokens] + prev_out[:tokens, :].astype(F32)
        out_sib[...] = (total[tokens:] + prev_out[tokens:, :].astype(F32)).astype(BF16)
        writes += [copy(out_own, out_own_hbm), copy(out_sib, out_sib_hbm)]
    for source, grad, order, targets in (
        (gd, lambda: tn(act[...], ct[...]), NEAR_FIRST, (keep_b, send_b)),
        (gu, lambda: tn(nm[...], pg[...]), NEAR_FIRST, (keep_a, send_a)),
    ):
        source[...] = grad().astype(BF16)
        for place, step in enumerate(order):
            to = targets[place // 2].at[pl.ds((place % 2) * unit_rows, unit_rows)]
            writes.append(copy(source.at[unit_at(step), :], to))
    wait(*writes)


def attend_back(lens, ids, qkv, datt, dqkv):
    width = datt.shape[1]
    rows = datt.shape[0] // SEQ
    low = low_lanes()

    @pl.loop(0, rows)
    def _(row):
        allowed2, valid = row_mask(lens, ids[0] * rows + row)
        at = pl.ds(pl.multiple_of(row * SEQ, SEQ), SEQ)
        for first in range(0, width, 2 * HEAD):
            q_cols = slice(first, first + 2 * HEAD)
            k_cols = slice(width + first, width + first + 2 * HEAD)
            v_cols = slice(2 * width + first, 2 * width + first + 2 * HEAD)
            k = qkv[at, k_cols]
            q_stack = stack_pair(qkv[at, q_cols], low)
            grad = (datt[at, q_cols].astype(F32) * valid).astype(BF16)
            g_stack = stack_pair(grad, low)
            probs = pair_probs(q_stack, k, allowed2)
            dqkv[at, v_cols] = nn(probs.astype(BF16), g_stack).astype(BF16)
            prob_grad = nt(qkv[at, v_cols], g_stack)
            inner = jnp.sum(probs * prob_grad, axis=0, keepdims=True)
            score_grad = (probs * (prob_grad - inner)).astype(BF16)
            both = tn(score_grad, k)
            dqkv[at, q_cols] = (jnp.where(low, both[:SEQ], both[SEQ:]) * SCALE).astype(BF16)
            dqkv[at, k_cols] = (nn(score_grad, q_stack) * SCALE).astype(BF16)


def weight_grads(copies, ids, nrm, dqkv, dw, dwo, order, keep, send):
    core, mine = ids[1], ids[2]
    width = dw.shape[2]
    part_rows = dw.shape[1] // (2 * UNITS)
    made = []
    for part in (3, 2, 1, 0):
        if part < 3:
            dw[part] = tn(nrm[...], dqkv[:, part * width : (part + 1) * width]).astype(BF16)
        for place in range(UNITS):
            unit = jnp.bitwise_xor(mine, order[place])
            for side, target in ((1 - core, send), (core, keep)):
                at_w = pl.ds(pl.multiple_of((side * UNITS + unit) * part_rows, part_rows), part_rows)
                at_o = pl.ds(pl.multiple_of(unit * part_rows, part_rows), part_rows)
                cols = pl.ds(pl.multiple_of(side * width, width), width)
                source = dw.at[part, at_w, :] if part < 3 else dwo.at[at_o, cols]
                made.append(copies.start(source, target.at[unit_block(part, part_rows, width, 2 * place * part_rows)]))
    return made


def bias_sums(dqkv):
    width = dqkv.shape[1] // 3
    ones = jnp.ones((8, dqkv.shape[0]), BF16)
    return [nn(ones, dqkv[:, first : first + width])[0:1] for first in (0, 2 * width)]


def normed_grad(dqkv, w):
    width = w.shape[2]
    total = nt(dqkv[:, :width], w[0])
    for part in range(1, 3):
        total = total + nt(dqkv[:, part * width : (part + 1) * width], w[part])
    return total


def other_back_kernel(lens, ids, dnm_own_hbm, dnm_sib_hbm, ct_hbm, mid_hbm, vecs, qkv_hbm, att_hbm, nrm_hbm, *refs):
    mine_parts, sib_parts = refs[:4], refs[4:8]
    mg_hbm, dqkv_hbm, keep, send, sums = refs[8:13]
    dnm_own, dnm_sib, ct, mid, qkv, att, nrm, wo, mg, ml, datt, dqkv, dw, dwo, sems = refs[13:]
    copies = Copies(sems)
    first_in = [
        copies.start(dnm_own_hbm, dnm_own), copies.start(dnm_sib_hbm, dnm_sib),
        copies.start(ct_hbm, ct), copies.start(mid_hbm, mid),
    ]
    to_wo = fetch_output_weight(copies, ids, mine_parts, sib_parts, wo)
    qkv_in, att_in, nrm_in = copies.start(qkv_hbm, qkv), copies.start(att_hbm, att), copies.start(nrm_hbm, nrm)
    wait(*first_in)

    def back_rows(at, totals):
        grad = dnm_own[at, :] + dnm_sib[at, :].astype(F32)
        part, gain_sum, shift_sum = norm_back(mid[at, :], grad, vecs[3:4, :])
        out_grad = ct[at, :].astype(F32)
        value = out_grad + part
        mg[at, :] = value
        ml[at, :] = value.astype(BF16)
        adds = (gain_sum, shift_sum, jnp.sum(value, axis=0, keepdims=True), jnp.sum(out_grad, axis=0, keepdims=True))
        return tuple(total + add for total, add in zip(totals, adds))

    totals = over_rows(mid.shape[0], back_rows, (jnp.zeros((1, mid.shape[1]), F32),) * 4)
    sums[...] = jnp.concatenate(list(totals) + [jnp.zeros((4, mid.shape[1]), F32)])
    mg_out = copies.start(mg, mg_hbm)
    wait(*to_wo, qkv_in, att_in)
    datt[...] = nt(ml[...], wo[...]).astype(BF16)
    dwo[...] = tn(att[...], ml[...]).astype(BF16)
    attend_back(lens, ids, qkv, datt, dqkv)
    wait(nrm_in)
    dqkv_out = copies.start(dqkv, dqkv_hbm)
    outs = weight_grads(copies, ids, nrm, dqkv, dw, dwo, NEAR_FIRST, keep, send)
    wait(mg_out, dqkv_out, *outs)


def own_back_kernel(
    lens, ids, mg_hbm, wo_hbm, qkv_hbm, att_hbm, nrm_hbm, dqkv_hbm, keep, send,
    mg, wo, qkv, att, nrm, ml, datt, dqkv, dw, dwo, sems,
):
    copies = Copies(sems)
    mg_in, wo_in = copies.start(mg_hbm, mg), copies.start(wo_hbm, wo)
    att_in, qkv_in, nrm_in = copies.start(att_hbm, att), copies.start(qkv_hbm, qkv), copies.start(nrm_hbm, nrm)
    wait(mg_in)
    ml[...] = mg[...].astype(BF16)
    wait(wo_in, att_in, qkv_in)
    datt[...] = nt(ml[...], wo[...]).astype(BF16)
    dwo[...] = tn(att[...], ml[...]).astype(BF16)
    attend_back(lens, ids, qkv, datt, dqkv)
    dqkv_out = copies.start(dqkv, dqkv_hbm)
    wait(nrm_in)
    outs = weight_grads(copies, ids, nrm, dqkv, dw, dwo, NEAR_FIRST, keep, send)
    wait(dqkv_out, *outs)


def input_grad_kernel(ids, dqkv_a_hbm, dqkv_b_hbm, mg_hbm, x_hbm, vecs, w_hbm, sums, ub_own, ub_other, *refs):
    mine_parts, sib_parts = refs[:4], refs[4:8]
    in_grad, vec = refs[8:10]
    dqkv_a, dqkv_b, mg, x, w_own, w_other, dn, sems = refs[10:]
    half, core = ids[0], ids[1]
    copies = Copies(sems)
    own_in = [copies.start(dqkv_a_hbm, dqkv_a), copies.start(w_hbm, w_own)]
    other_in, _ = fetch_weights(copies, ids, mine_parts, sib_parts, w_other, None)
    other_in.append(copies.start(dqkv_b_hbm, dqkv_b))
    late = [copies.start(mg_hbm, mg), copies.start(x_hbm, x)]
    width = w_own.shape[2]
    wait(*own_in)
    dn[...] = normed_grad(dqkv_a, w_own)
    wait(*other_in)
    dn[...] += normed_grad(dqkv_b, w_other)
    wait(*late)

    def back_rows(at, totals):
        part, gain_sum, shift_sum = norm_back(x[at, :].astype(F32), dn[at, :], vecs[0:1, :])
        in_grad[at, :] = (mg[at, :] + part).astype(BF16)
        return totals[0] + gain_sum, totals[1] + shift_sum

    totals = over_rows(x.shape[0], back_rows, (jnp.zeros((1, x.shape[1]), F32),) * 2)
    vec[...] = jnp.zeros_like(vec)
    for i in range(2):
        vec[i : i + 1, :] = totals[i]
    vec[2:6, :] = sums[0:4, :]
    for dqkv, side in ((dqkv_a, half), (dqkv_b, 1 - half)):
        for i, value in enumerate(bias_sums(dqkv)):
            vec[6 + i : 7 + i, pl.ds(pl.multiple_of(side * width, width), width)] = value
    vec[pl.ds(8 + 2 * half + core, 1), :] = ub_own[...]
    vec[pl.ds(8 + 2 * (1 - half) + core, 1), :] = ub_other[...]


def layer_out_kernel(mid_hbm, own_hbm, sib_hbm, bias, out, mid, own, sib, sems):
    copies = Copies(sems)
    wait(copies.start(mid_hbm, mid), copies.start(own_hbm, own), copies.start(sib_hbm, sib))

    def rows(at, carry):
        out[at, :] = (mid[at, :] + own[at, :] + sib[at, :].astype(F32) + bias[...]).astype(BF16)
        return carry

    over_rows(out.shape[0], rows, 0)


class Placing:
    def __init__(self, ids, copies):
        self.core, self.mine = ids[1], ids[2]
        self.copies = copies
        self.work, self.outs = [], []

    def take(self, refs, narrow, wide, targets):
        for i, ref in enumerate(refs):
            side = self.core if i < UNITS else 1 - self.core
            unit = jnp.bitwise_xor(self.mine, i % UNITS)
            self.work.append((self.copies.start(ref, narrow.at[i]), narrow, wide, i, targets(side, unit)))

    def finish(self):
        for arrived, narrow, wide, i, targets in self.work:
            arrived.wait()
            wide[i] = narrow[i].astype(F32)
            for block, target in targets:
                self.outs.append(self.copies.start(wide.at[i, block[0], block[1]], target))
        wait(*self.outs)


def mlp_targets(out, down_first, rows, width):
    def targets(side, unit):
        base, start = pl.multiple_of(side * width, width), pl.multiple_of(unit * rows, rows)
        if down_first:
            target = out.at[pl.ds(pl.multiple_of(base + start, rows), rows), :]
        else:
            target = out.at[pl.ds(start, rows), pl.ds(base, width)]
        return [((pl.ds(0, rows), pl.ds(0, width)), target)]

    return targets


def attn_targets(w, wo):
    width = w.shape[2]
    rows = w.shape[1] // (2 * UNITS)

    def targets(side, unit):
        at_w = pl.ds(pl.multiple_of((side * UNITS + unit) * rows, rows), rows)
        at_o = pl.ds(pl.multiple_of(unit * rows, rows), rows)
        cols = pl.ds(pl.multiple_of(side * width, width), width)
        places = [w.at[part, at_w, :] for part in range(3)] + [wo.at[at_o, cols]]
        return [(unit_block(part, rows, width), place) for part, place in enumerate(places)]

    return targets


def place_mlp_kernel(down_first, ids, *refs):
    units, (out, narrow, wide, sems) = refs[:8], refs[8:]
    placing = Placing(ids, Copies(sems))
    placing.take(units, narrow, wide, mlp_targets(out, down_first, *units[0].shape))
    placing.finish()


def place_down_kernel(*refs):
    place_mlp_kernel(True, *refs)


def place_two_kernel(ids, *refs):
    up_units, attn_units = refs[:8], refs[8:16]
    up, w, wo, narrow_u, wide_u, narrow_a, wide_a, sems = refs[16:]
    placing = Placing(ids, Copies(sems))
    placing.take(up_units, narrow_u, wide_u, mlp_targets(up, False, *up_units[0].shape))
    placing.take(attn_units, narrow_a, wide_a, attn_targets(w, wo))
    placing.finish()


def vmem(*buffers, sems):
    return [pltpu.VMEM(shape, dtype) for shape, dtype in buffers] + [pltpu.SemaphoreType.DMA((sems,))]


def call(kernel, outs, in_specs, name, scratch=(), out_specs=None, limit=60, gflop=1.0):
    return pl.pallas_call(
        kernel,
        out_shape=tuple(jax.ShapeDtypeStruct(shape, dtype) for shape, dtype in outs),
        in_specs=in_specs,
        out_specs=tuple(VM for _ in outs) if out_specs is None else tuple(out_specs),
        scratch_shapes=list(scratch),
        name=name,
        cost_estimate=pl.CostEstimate(flops=int(gflop * 1e9), bytes_accessed=8 << 20, transcendentals=0),
        compiler_params=pltpu.CompilerParams(vmem_limit_bytes=limit * 1024 * 1024),
    )


def build(mesh):
    devices = mesh.shape["dp"] * mesh.shape["tp"]
    bits = devices.bit_length() - 1

    def swap(value, mask):
        return lax.ppermute(value, ("dp", "tp"), [(i, i ^ mask) for i in range(devices)])

    def after(value, *deps):
        return lax.optimization_barrier((value, deps))[0]

    def share(unit):
        return [unit] + [swap(unit, mask) for mask in (NEAR, FAR, NEAR | FAR)]

    def add(*terms):
        total = terms[0].astype(F32)
        for term in terms[1:]:
            total = total + term.astype(F32)
        return total

    last = []

    def turn(*values):
        return lax.optimization_barrier((values, last[-1]))[0]

    def note(value):
        last.append(value)
        return value

    def due(*values):
        values = turn(*values)
        note(values[-1])
        return values

    def total(parts, *terms):
        cut = lambda v, part: v if part is None else v[v.shape[0] * part[0] // 4 : v.shape[0] * part[1] // 4]
        return note(add(*[cut(term, part) for term, part in zip(turn(*terms), parts)]).astype(BF16))

    def on_device(
        layer_in, lengths, attn_gain, attn_shift, qkv_weight, qv_bias, out_weight, out_bias,
        mlp_gain, mlp_shift, up_weight, up_bias, down_weight, down_bias, cotangent,
    ):
        tokens, wide = layer_in.shape
        width = qkv_weight.shape[2]
        hidden = up_weight.shape[1] // 2
        flat = lax.axis_index("dp") * 2 + lax.axis_index("tp")
        half = lax.axis_index("tp")
        core = (flat >> CORE_BIT) & 1
        mine = ((flat >> FAR_BIT) & 1) * 2 + ((flat >> NEAR_BIT) & 1)
        ids = jnp.stack([half, core, mine]).astype(jnp.int32)
        row = lambda v: v.reshape(1, -1)
        none = jnp.zeros_like(out_bias)
        vecs = jnp.stack([attn_gain, attn_shift, out_bias, mlp_gain, mlp_shift, none, none, none])
        w_own = jnp.transpose(qkv_weight, (1, 0, 2))

        part_rows = wide // (2 * UNITS)
        unit_w = lax.dynamic_slice(w_own, (0, (core * UNITS + mine) * part_rows, 0), (3, part_rows, width))
        unit_o = lax.dynamic_slice(out_weight, (mine * part_rows, core * width), (part_rows, width))
        attn_unit = jnp.concatenate(
            [jnp.concatenate([unit_w[0], unit_w[1]], axis=1), jnp.concatenate([unit_w[2], unit_o], axis=1)]
        )
        attn_unit = swap(attn_unit, TP)

        acts = (tokens, 3 * width)
        one = (tokens, wide)
        head = (tokens, width)
        w_shape, wo_shape = (3, wide, width), (width, wide)
        nrm, qkv_own, att_own = call(
            own_fwd_kernel,
            [(one, BF16), (acts, BF16), (head, BF16)],
            [SM, SM, HB, VM, HB, VM],
            "attn_own_fwd",
            gflop=0.5,
            scratch=vmem((one, BF16), (w_shape, BF16), (one, BF16), (acts, BF16), sems=4),
            out_specs=[HB, HB, VM],
        )(lengths, ids, layer_in, vecs, w_own, qv_bias)
        attn_parts = share(after(attn_unit, att_own))
        unit_rows = hidden // UNITS
        up_late, down_late, bias_late, up_bias_late = after((up_weight, down_weight, qv_bias, up_bias), att_own)
        mlp_unit = jnp.concatenate(
            [
                lax.dynamic_slice(up_late, (mine * unit_rows, core * hidden), (unit_rows, hidden)),
                lax.dynamic_slice(down_late, (core * hidden + mine * unit_rows, 0), (unit_rows, wide)),
            ]
        )
        mlp_unit = swap(mlp_unit, TP)
        small = jnp.concatenate([bias_late.reshape(-1), up_bias_late])
        small_other = swap(small.reshape(-1, 128), TP).reshape(-1)
        ct_sib = swap(cotangent, CORE)
        bias_other = small_other[: 2 * width].reshape(2, width)
        up_bias_own = lax.dynamic_slice(up_bias, (core * hidden,), (hidden,))
        up_bias_other = lax.dynamic_slice(small_other, (2 * width + core * hidden,), (hidden,))
        attn_sib = [swap(part, CORE) for part in attn_parts]
        qkv_other, att_other, mid, nm = call(
            other_fwd_kernel,
            [(acts, BF16), (head, BF16), (one, F32), (one, BF16)],
            [SM, SM, HB, HB, VM, HB, HB, VM] + [HB] * 8,
            "attn_other_fwd",
            gflop=6,
            scratch=vmem(
                (one, BF16), (one, BF16), (head, BF16), (wo_shape, BF16), (w_shape, BF16), (wo_shape, BF16),
                (acts, BF16), (head, BF16), (one, F32), sems=40,
            ),
            out_specs=[HB, HB, HB, VM],
        )(
            lengths, ids, layer_in, after(nrm, mlp_unit), bias_other, att_own, out_weight, vecs,
            *attn_parts, *attn_sib,
        )
        mlp_near, mlp_far = swap(mlp_unit, NEAR), swap(mlp_unit, FAR)

        mlp_near, mlp_far, nm = after((mlp_near, mlp_far, nm))
        mlp_parts = [mlp_unit, mlp_near, mlp_far, swap(mlp_unit, NEAR | FAR)]
        nm_sib = swap(nm, CORE)
        tall, square = (2 * tokens, wide), (wide, hidden)
        scratch = [
            (square, BF16), (square, BF16), (tall, BF16), (tall, BF16), ((tokens, hidden), F32), ((tokens, hidden), F32),
            ((2 * tokens, hidden), BF16), ((2 * tokens, hidden), BF16), (square, BF16), (square, BF16),
        ]

        def mlp_scratch(*more):
            buffers = vmem(*scratch, *more, sems=40)
            return buffers[:10] + buffers[-1:] + buffers[10:-1]

        both = (2 * tokens, wide)
        pair = (2 * unit_rows, hidden)
        out_a, dnm_a, keep_own, send_own, b_own_lo, b_own_hi, ub_own = call(
            lambda *r: mlp_kernel(True, *r),
            [(both, BF16), (both, BF16), *[(pair, BF16)] * 4, ((1, hidden), F32)],
            [SM] + [HB] * 4 + [VM] + [HB] * 2,
            "mlp_own",
            gflop=1,
            scratch=mlp_scratch((tall, BF16), (tall, BF16)),
            out_specs=[HB] * 6 + [VM],
        )(ids, nm, nm_sib, cotangent, ct_sib, row(up_bias_own), up_weight, down_weight)
        out_own, out_sib, dnm_own, dnm_sib, keep_other, send_other, b_other_lo, b_other_hi, ub_other = call(
            lambda *r: mlp_kernel(False, *r),
            [
                (one, F32), (one, BF16), (one, F32), (one, BF16), *[(pair, BF16)] * 4,
                ((1, hidden), F32),
            ],
            [SM] + [HB] * 4 + [VM] + [HB] * 6,
            "mlp_other",
            gflop=12,
            scratch=mlp_scratch((tall, BF16), (tall, BF16), (one, F32), (one, BF16), (one, F32), (one, BF16)),
            out_specs=[HB] * 8 + [VM],
        )(ids, nm, nm_sib, cotangent, ct_sib, row(up_bias_other), *mlp_parts, out_a, dnm_a)
        grad_units = (2 * UNITS * part_rows, 2 * width)
        whole, low_half, high_half, first, second = None, (0, 2), (2, 4), (0, 1), (1, 2)
        a_own = swap(send_own, NEAR)
        note(ub_other)
        a_own, dnm_sib, out_sib, send_other, b_other_hi, b_other_lo = turn(
            a_own, dnm_sib, out_sib, send_other, b_other_hi, b_other_lo
        )
        dnm_got = swap(dnm_sib, CORE)
        a_own2 = swap(total((high_half, high_half), keep_own, a_own), FAR)
        a_other = swap(send_other, NEAR)
        b_hi = swap(b_other_hi, TP)
        mg, dqkv_other, keep_o, send_o, sums_mid = call(
            other_back_kernel,
            [(one, F32), (acts, BF16), (grad_units, BF16), (grad_units, BF16), ((8, wide), F32)],
            [SM, SM, HB, HB, HB, HB, VM, HB, HB, HB] + [HB] * 8,
            "attn_other_back",
            gflop=10,
            scratch=vmem(
                (one, F32), (one, BF16), (one, BF16), (one, F32), (acts, BF16), (head, BF16), (one, BF16),
                (wo_shape, BF16), (one, F32), (one, BF16), (head, BF16), (acts, BF16),
                (w_shape, BF16), (wo_shape, BF16), sems=60,
            ),
            out_specs=[HB] * 4 + [VM],
        )(
            lengths, ids, dnm_own, dnm_got, cotangent, mid, vecs, qkv_other, att_other, nrm,
            *attn_parts, *attn_sib,
        )
        note(sums_mid)
        out_got = swap(turn(out_sib)[0], CORE)
        a_other, a_own2, b_hi, send_o = turn(a_other, a_own2, b_hi, send_o)
        o_sib = swap(send_o, CORE)
        a_other2 = swap(total((high_half, high_half), keep_other, a_other), FAR)
        o1 = swap(total((high_half, high_half), keep_o, o_sib), NEAR)
        b_lo = swap(b_other_lo, TP)
        mg_now, = turn(mg)
        dqkv_own, keep_s, send_s = call(
            own_back_kernel,
            [(acts, BF16), (grad_units, BF16), (grad_units, BF16)],
            [SM, SM] + [HB] * 5,
            "attn_own_back",
            gflop=10,
            scratch=vmem(
                (one, F32), (wo_shape, BF16), (acts, BF16), (head, BF16), (one, BF16),
                (one, BF16), (head, BF16), (acts, BF16), (w_shape, BF16), (wo_shape, BF16), sems=48,
            ),
            out_specs=[HB] * 3,
        )(lengths, ids, mg_now, out_weight, qkv_own, att_own, nrm)
        note(dqkv_own)
        a_other2, o1, b_lo, send_s = turn(a_other2, o1, b_lo, send_s)
        s_sib = swap(send_s, CORE)
        a_back = swap(total((low_half, low_half, whole), keep_other, a_other, a_other2), TP)
        s1 = swap(total((high_half, high_half), keep_s, s_sib), NEAR)
        o2 = swap(total((second, second, high_half), keep_o, o_sib, o1), FAR)
        b1 = swap(total((whole, whole), b_own_hi, b_hi), NEAR)
        a_unit = total((low_half, low_half, whole, whole), keep_own, a_own, a_own2, a_back)
        a_more = swap(a_unit, 1 << FIRST_REST)
        in_grad, vec = call(
            input_grad_kernel,
            [(one, BF16), ((16, wide), F32)],
            [SM, HB, HB, HB, HB, VM, HB, VM, VM, VM] + [HB] * 8,
            "input_grad",
            gflop=0.01,
            scratch=vmem(
                (acts, BF16), (acts, BF16), (one, F32), (one, BF16), (w_shape, BF16), (w_shape, BF16), (one, F32),
                sems=32,
            ),
        )(
            ids, dqkv_own, dqkv_other, *turn(mg), layer_in, vecs, w_own, sums_mid, ub_own, ub_other,
            *attn_parts, *attn_sib,
        )
        note(vec)

        def step(value, bit):
            mine, got = turn(value, swap(value, 1 << bit))
            return note(mine + got)

        def rest(unit, got):
            unit = total((whole, whole), unit, got)
            for bit in range(FIRST_REST + 1, bits):
                unit = total((whole, whole), unit, swap(unit, 1 << bit))
            return unit

        def step_with(value, got):
            mine, got = turn(value, got)
            return note(mine + got)

        s2 = swap(total((second, second, high_half), keep_s, s_sib, s1), FAR)
        o_back = swap(total((first, first, low_half, whole), keep_o, o_sib, o1, o2), TP)
        vec = step(vec, CORE_BIT)
        a_unit = rest(a_unit, a_more)
        a_near, a_far = swap(a_unit, NEAR), swap(a_unit, FAR)
        for bit in range(FIRST_REST, bits):
            vec = step(vec, bit)
        s_unit = total((first, first, low_half, whole, whole), keep_s, s_sib, s1, s2, o_back)
        s_more = swap(s_unit, 1 << FIRST_REST)
        vec_tp = swap(vec, TP)
        b2 = swap(total((high_half, high_half, high_half), b_own_lo, b_lo, b1), FAR)
        layer_out, = call(
            layer_out_kernel,
            [(one, BF16)],
            [HB, HB, HB, VM],
            "layer_out",
            gflop=0.01,
            scratch=vmem((one, F32), (one, F32), (one, BF16), sems=3),
        )(mid, out_own, *turn(out_got), row(down_bias))
        note(layer_out)
        a_near, a_far, vec_tp, b2, s_more = due(a_near, a_far, vec_tp, b2, s_more)
        s_unit = rest(s_unit, s_more)
        s_units = share(s_unit)
        b_unit = total((low_half, low_half, low_half, whole), b_own_lo, b_lo, b1, b2)
        b_more = swap(b_unit, 1 << FIRST_REST)
        a_corner = swap(a_far, NEAR)
        vec = note(vec + vec_tp)
        *s_units, a_corner, b_more = due(*s_units, a_corner, b_more)
        b_unit = rest(b_unit, b_more)
        b_units = share(b_unit)
        vec_near = swap(vec, NEAR)
        a_units = [a_unit, a_near, a_far, a_corner]
        a_sib = [swap(value, CORE) for value in turn(*a_units)]
        s_sib = [swap(value, CORE) for value in turn(*s_units)]
        up_grad, qkv_grad, out_grad = call(
            place_two_kernel,
            [((wide, 2 * hidden), F32), ((3, wide, width), F32), ((width, wide), F32)],
            [SM] + [HB] * 16,
            "place_two",
            gflop=0.01,
            scratch=vmem(
                ((8, unit_rows, hidden), BF16), ((8, unit_rows, hidden), F32),
                ((8, 2 * part_rows, 2 * width), BF16), ((8, 2 * part_rows, 2 * width), F32), sems=56,
            ),
            out_specs=[HB] * 3,
            limit=32,
        )(ids, *turn(*a_units, *a_sib, *s_units, *s_sib))
        note(out_grad)
        vec = step_with(vec, vec_near)
        vec_far = swap(vec, FAR)
        *b_units, vec_far = due(*b_units, vec_far)
        b_sib = [swap(value, CORE) for value in b_units]
        vec = vec + vec_far
        down_grad, = call(
            place_down_kernel,
            [((2 * hidden, wide), F32)],
            [SM] + [HB] * 8,
            "place_down",
            scratch=vmem(((8, unit_rows, wide), BF16), ((8, unit_rows, wide), F32), sems=16),
            out_specs=[HB],
            limit=24,
        )(ids, *b_units, *b_sib)
        one_of = lambda i: vec[i]
        qvb = lax.dynamic_slice(vec, (6, half * width), (2, width))
        ub = lax.dynamic_slice(vec, (8 + 2 * half, 0), (2, hidden)).reshape(2 * hidden)
        return (
            layer_out, in_grad, one_of(0), one_of(1), jnp.transpose(qkv_grad, (1, 0, 2)), qvb,
            out_grad, one_of(4), one_of(2), one_of(3), up_grad, ub, down_grad, one_of(5),
        )

    return on_device


def solution(mesh):
    tokens, vector = P(("dp", "tp"), None), P()
    in_specs = (
        tokens, P("dp", None), vector, vector, P(None, None, "tp"), P(None, "tp"), P("tp", None), vector,
        vector, vector, P(None, "tp"), P("tp"), P("tp", None), vector, tokens,
    )
    out_specs = (
        tokens, tokens, vector, vector, P(None, None, "tp"), P(None, "tp"), P("tp", None), vector,
        vector, vector, P(None, "tp"), P("tp"), P("tp", None), vector,
    )
    return jax.shard_map(build(mesh), mesh=mesh, in_specs=in_specs, out_specs=out_specs, check_vma=False)
```

profile of v0, /device:TPU:1, one launch (start us, length us, event | category | flops | bytes accessed | tf_op | source)
XLA Modules:
  0.0 237.0 jit_solution(18413311137245606904)
XLA Ops:
  2.7 2.1 collective-permute-start.2
  6.1 7.1 %attn_own_fwd.1 = (bf16[512,768]{1,0:T(8,128)(2,1)}, bf16[512,1152]{1,0:T(8,128)(2,1)}, bf16[512,384]{1,0:T(8,128)(2,1)}) custom-call(s32[8,17]{1,0:T(8,128)} %lens.7, s32[3]{0:T(128)} %pad_add_fusion.ids.r_0_.refs_0_, bf16[512,768]{1,0:T(8,128)(2,1)} %x_hbm.5, f32[8,768]{1,0:T(8,128)} %stack.43.vecs, bf16[3,768,384]{2,1,0:T(8,128)(2,1)} %bitcast.16, ...), custom_call_target="tpu_custom_call" | custom-call | flops 500000000 | bytes 8388608 | tf_op jit(solution)/shard_map/attn_own_fwd/pallas_call | solution.py:637
  18.7 10.0 %collective-permute-done.1 = f32[18,128]{1,0:T(8,128)S(1)} collective-permute-done((f32[18,128]{1,0:T(8,128)S(1)}, f32[18,128]{1,0:T(8,128)S(1)}, u32[]{:S(2)}, u32[]{:S(2)}) %collective-permute-start.1) | collective-permute-done | bytes 9248 | tf_op jit(solution)/shard_map/ppermute | solution.py:576
  28.7 1.8 collective-permute-start.6
  35.5 10.3 %attn_other_fwd.1 = (bf16[512,1152]{1,0:T(8,128)(2,1)}, bf16[512,384]{1,0:T(8,128)(2,1)}, f32[512,768]{1,0:T(8,128)}, bf16[512,768]{1,0:T(8,128)(2,1)}) custom-call(s32[8,17]{1,0:T(8,128)} %lens.7, s32[3]{0:T(128)} %pad_add_fusion.ids.r_0_.refs_0_, bf16[512,768]{1,0:T(8,128)(2,1)} %x_hbm.5, bf16[512,768]{1,0:T(8,128)(2,1)} %get-tuple-element.172.nrm_hbm, ...), custom_call_target="tpu_custom_call" | custom-call | flops 6000000000 | bytes 8388608 | tf_op jit(solution)/shard_map/attn_other_fwd/pallas_call | solution.py:663
  54.0 17.0 %mlp_own.1 = (bf16[1024,768]{1,0:T(8,128)(2,1)}, bf16[1024,768]{1,0:T(8,128)(2,1)}, bf16[384,768]{1,0:T(8,128)(2,1)}, bf16[384,768]{1,0:T(8,128)(2,1)}, bf16[384...) custom-call(s32[3]{0:T(128)} %pad_add_fusion.ids.r_0_.refs_0_, ...), custom_call_target="tpu_custom_call" | custom-call | flops 1000000000 | bytes 8388608 | tf_op jit(solution)/shard_map/mlp_own/pallas_call | solution.py:695
  73.1 17.1 %mlp_other.1 = (f32[512,768]{1,0:T(8,128)}, bf16[512,768]{1,0:T(8,128)(2,1)}, f32[512,768]{1,0:T(8,128)}, bf16[512,768]{1,0:T(8,128)(2,1)}, bf16[384,768]{1,0:T(...) custom-call(s32[3]{0:T(128)} %pad_add_fusion.ids.r_0_.refs_0_, ...), custom_call_target="tpu_custom_call" | custom-call | flops 12000000000 | bytes 8388608 | tf_op jit(solution)/shard_map/mlp_other/pallas_call | solution.py:704
  93.9 14.4 %attn_other_back.1 = (f32[512,768]{1,0:T(8,128)}, bf16[512,1152]{1,0:T(8,128)(2,1)}, bf16[768,768]{1,0:T(8,128)(2,1)}, bf16[768,768]{1,0:T(8,128)(2,1)}, f32[8,768]{1,0:T(8,128)}) custom-call(s32[8,17]{1,0:T(8,128)} %lens.7, s32[3]{0:T(128)} %pad_add_fusion.ids.r_0_.refs_0_, f32[512,768]{1,0:T(8,128)} %get-tuple-element.192.dnm_own_hbm, ...), custom_call_target="tpu_custom_call" | custom-call | flops 10000000000 | bytes 8388608 | tf_op jit(solution)/shard_map/attn_other_back/pallas_call | solution.py:727
  115.2 11.9 %attn_own_back.1 = (bf16[512,1152]{1,0:T(8,128)(2,1)}, bf16[768,768]{1,0:T(8,128)(2,1)}, bf16[768,768]{1,0:T(8,128)(2,1)}) custom-call(s32[8,17]{1,0:T(8,128)} %lens.7, s32[3]{0:T(128)} %pad_add_fusion.ids.r_0_.refs_0_, f32[512,768]{1,0:T(8,128)} %get-tuple-element.243.mg_hbm, bf16[384,768]{1,0:T(8,128)(2,1)} %wo_hbm.1, ...), custom_call_target="tpu_custom_call" | custom-call | flops 10000000000 | bytes 8388608 | tf_op jit(solution)/shard_map/attn_own_back/pallas_call | solution.py:751
  134.7 2.0 add_convert_fusion.12
  138.1 1.6 collective-permute-done.28
  139.9 2.4 %collective-permute-start.34 = (bf16[192,768]{1,0:T(8,128)(2,1)S(1)}, bf16[192,768]{1,0:T(8,128)(2,1)S(1)}, u32[]{:S(2)}, u32[]{:S(2)}) collective-permute-start(bf16[192,768]{1,0:T(8,128)(2,1)S(1)} %add_convert_fusion.11), channel_id=1, source_target_pairs={{0,16},{1,17},{2,18},{3,19},{4,20},{5,21},{6,22},{7,23},{8,24},{9,... | collective-permute-start | bytes 884744 | tf_op jit(solution)/shard_map/ppermute | solution.py:576
  143.5 8.8 %input_grad.1 = (bf16[512,768]{1,0:T(8,128)(2,1)}, f32[16,768]{1,0:T(8,128)}) custom-call(s32[3]{0:T(128)} %pad_add_fusion.ids.r_0_.refs_0_, bf16[512,1152]{1,0:T(8,128)(2,1)} %get-tuple-element.219.dqkv_a_hbm, bf16[512,1152]{1,0:T(8,128)(2,1)} %get-tuple-element.237.dqkv_b_hbm, f32[512,768]{1,0:T(8,128)} %get-tuple-element.243.mg_hbm, ...), custom_call_target="tpu_custom_call" | custom-call | flops 10000000 | bytes 8388608 | tf_op jit(solution)/shard_map/input_grad/pallas_call | solution.py:772
  158.5 6.2 %collective-permute-done.33 = f32[16,768]{1,0:T(8,128)S(1)} collective-permute-done((f32[16,768]{1,0:T(8,128)S(1)}, f32[16,768]{1,0:T(8,128)S(1)}, u32[]{:S(2)}, u32[]{:S(2)}) %collective-permute-start.33) | collective-permute-done | bytes 49184 | tf_op jit(solution)/shard_map/ppermute | solution.py:576
  165.0 1.6 collective-permute-start.36
  169.1 2.8 %collective-permute-start.39 = (bf16[192,768]{1,0:T(8,128)(2,1)S(1)}, bf16[192,768]{1,0:T(8,128)(2,1)S(1)}, u32[]{:S(2)}, u32[]{:S(2)}) collective-permute-start(bf16[192,768]{1,0:T(8,128)(2,1)S(1)} %add_convert_fusion.7), channel_id=1, source_target_pairs={{0,16},{1,17},{2,18},{3,19},{4,20},{5,21},{6,22},{7,23},{8,24},{9,... | collective-permute-start | bytes 884744 | tf_op jit(solution)/shard_map/ppermute | solution.py:576
  173.7 3.9 %layer_out.1 = bf16[512,768]{1,0:T(8,128)(2,1)} custom-call(f32[512,768]{1,0:T(8,128)} %get-tuple-element.176.mid_hbm, f32[512,768]{1,0:T(8,128)} %get-tuple-element.183.own_hbm, bf16[512,768]{1,0:T(8,128)(2,1)} %collective-permute-done.17.sib_hbm, f32[1,768]{1,0:T(1,128)} %reshape.60.bias), custom_call_target="tpu_custom_call" | custom-call | flops 10000000 | bytes 8388608 | tf_op jit(solution)/shard_map/layer_out/pallas_call | solution.py:813
  177.7 7.1 %collective-permute-done.38 = bf16[192,768]{1,0:T(8,128)(2,1)S(1)} collective-permute-done((bf16[192,768]{1,0:T(8,128)(2,1)S(1)}, bf16[192,768]{1,0:T(8,128)(2,1)S(1)}, u32[]{:S(2)}, u32[]{:S(2)}) %collective-permute-start.38) | collective-permute-done | bytes 294944 | tf_op jit(solution)/shard_map/ppermute | solution.py:576
  191.4 8.2 %collective-permute-done.45 = bf16[192,768]{1,0:T(8,128)(2,1)S(1)} collective-permute-done((bf16[192,768]{1,0:T(8,128)(2,1)S(1)}, bf16[192,768]{1,0:T(8,128)(2,1)S(1)}, u32[]{:S(2)}, u32[]{:S(2)}) %collective-permute-start.45) | collective-permute-done | bytes 294944 | tf_op jit(solution)/shard_map/ppermute | solution.py:576
  199.6 7.7 %collective-permute-done.43.refs_11_ = bf16[192,768]{1,0:T(8,128)(2,1)S(1)} collective-permute-done((bf16[192,768]{1,0:T(8,128)(2,1)S(1)}, bf16[192,768]{1,0:T(8,128)(2,1)S(1)}, u32[]{:S(2)}, u32[]{:S(2)}) %collective-permute-start.43) | collective-permute-done | bytes 294944 | tf_op jit(solution)/shard_map/ppermute | solution.py:576
  207.4 3.1 %collective-permute-start.50 = (bf16[192,768]{1,0:T(8,128)(2,1)S(1)}, bf16[192,768]{1,0:T(8,128)(2,1)S(1)}, u32[]{:S(2)}, u32[]{:S(2)}) collective-permute-start(bf16[192,768]{1,0:T(8,128)(2,1)S(1)} %add_convert_fusion.5.refs_8_), channel_id=1, source_target_pairs={{0,2},{1,3},{2,0},{3,1},{4,6},{5,7},{6,4},{7,5},{8,10},{9,11},{10,... | collective-permute-start | bytes 884744 | tf_op jit(solution)/shard_map/ppermute | solution.py:576
  216.8 5.7 %place_two.1 = (f32[768,1536]{1,0:T(8,128)}, f32[3,768,384]{2,1,0:T(8,128)}, f32[384,768]{1,0:T(8,128)}) custom-call(s32[3]{0:T(128)S(1)} %copy-done, bf16[192,768]{1,0:T(8,128)(2,1)S(1)} %add_convert_fusion.8.refs_0_, bf16[192,768]{1,0:T(8,128)(2,1)S(1)} %collective-permute-done.35.refs_1_, bf16[192,768]{1,0:T(8,128)(2,1)S(1)} %collective-permute-done.36.refs_2_, ...), custom_call_target="tpu_custom_call" | custom-call | flops 10000000 | bytes 8388608 | tf_op jit(solution)/shard_map/place_two/pallas_call | solution.py:836
  223.7 5.0 %collective-permute-done.56.refs_4_ = bf16[192,768]{1,0:T(8,128)(2,1)S(1)} collective-permute-done((bf16[192,768]{1,0:T(8,128)(2,1)S(1)}, bf16[192,768]{1,0:T(8,128)(2,1)S(1)}, u32[]{:S(2)}, u32[]{:S(2)}) %collective-permute-start.56) | collective-permute-done | bytes 294944 | tf_op jit(solution)/shard_map/ppermute | solution.py:576
  233.5 3.4 %place_down.1 = f32[1536,768]{1,0:T(8,128)} custom-call(s32[3]{0:T(128)S(1)} %copy-done, bf16[192,768]{1,0:T(8,128)(2,1)S(1)} %add_convert_fusion.3.refs_1_, bf16[192,768]{1,0:T(8,128)(2,1)S(1)} %collective-permute-done.54.refs_2_, bf16[192,768]{1,0:T(8,128)(2,1)S(1)} %collective-permute-done.55.refs_3_, ...), custom_call_target="tpu_custom_call" | custom-call | flops 1000000000 | bytes 8388608 | tf_op jit(solution)/shard_map/place_down/pallas_call | solution.py:855
  (235 shorter events, 74.3 us)
Async XLA Ops:
  14.4 17.1 %collective-permute-start = (bf16[384,768]{1,0:T(8,128)(2,1)S(1)}, bf16[384,768]{1,0:T(8,128)(2,1)}, u32[]{:S(2)}, u32[]{:S(2)}) collective-permute-start(bf16[384,768]{1,0:T(8,128)(2,1)S(1)} %pad_maximum_fusion), channel_id=1, source_target_pairs={{0,1},{1,0},{2,3},{3,2},{4,5},{5,4},{6,7},{7,6},{8,9},{9,8},{10,11... | collective-permute-start | bytes 1769480 | tf_op jit(solution)/shard_map/ppermute | solution.py:576
  14.5 16.0 %collective-permute-start.3 = (bf16[192,768]{1,0:T(8,128)(2,1)S(1)}, bf16[192,768]{1,0:T(8,128)(2,1)S(1)}, u32[]{:S(2)}, u32[]{:S(2)}) collective-permute-start(bf16[192,768]{1,0:T(8,128)(2,1)S(1)} %collective-permute-done.2.refs_0_), channel_id=1, source_target_pairs={{0,4},{1,5},{2,6},{3,7},{4,0},{5,1},{6,2},{7,3},{8,12},{9,13},{10,... | collective-permute-start | bytes 884744 | tf_op jit(solution)/shard_map/ppermute | solution.py:576
  15.9 14.7 %collective-permute-start.4 = (bf16[192,768]{1,0:T(8,128)(2,1)S(1)}, bf16[192,768]{1,0:T(8,128)(2,1)S(1)}, u32[]{:S(2)}, u32[]{:S(2)}) collective-permute-start(bf16[192,768]{1,0:T(8,128)(2,1)S(1)} %collective-permute-done.2.refs_0_), channel_id=1, source_target_pairs={{0,8},{1,9},{2,10},{3,11},{4,12},{5,13},{6,14},{7,15},{8,0},{9,1},... | collective-permute-start | bytes 884744 | tf_op jit(solution)/shard_map/ppermute | solution.py:576
  31.5 15.2 %collective-permute-start.10 = (bf16[384,768]{1,0:T(8,128)(2,1)}, bf16[384,768]{1,0:T(8,128)(2,1)}, u32[]{:S(2)}, u32[]{:S(2)}) collective-permute-start(bf16[384,768]{1,0:T(8,128)(2,1)} %collective-permute-done.r_6_), channel_id=1, source_target_pairs={{0,4},{1,5},{2,6},{3,7},{4,0},{5,1},{6,2},{7,3},{8,12},{9,13},{10,... | collective-permute-start | bytes 1769480 | tf_op jit(solution)/shard_map/ppermute | solution.py:576
  32.9 14.9 %collective-permute-start.11 = (bf16[384,768]{1,0:T(8,128)(2,1)}, bf16[384,768]{1,0:T(8,128)(2,1)}, u32[]{:S(2)}, u32[]{:S(2)}) collective-permute-start(bf16[384,768]{1,0:T(8,128)(2,1)} %collective-permute-done.r_6_), channel_id=1, source_target_pairs={{0,8},{1,9},{2,10},{3,11},{4,12},{5,13},{6,14},{7,15},{8,0},{9,1},... | collective-permute-start | bytes 1769480 | tf_op jit(solution)/shard_map/ppermute | solution.py:576
  34.8 17.4 %collective-permute-start.13 = (bf16[512,768]{1,0:T(8,128)(2,1)S(1)}, bf16[512,768]{1,0:T(8,128)(2,1)S(1)}, u32[]{:S(2)}, u32[]{:S(2)}) collective-permute-start(bf16[512,768]{1,0:T(8,128)(2,1)S(1)} %copy-done.4), channel_id=1, source_target_pairs={{0,2},{1,3},{2,0},{3,1},{4,6},{5,7},{6,4},{7,5},{8,10},{9,11},{10,... | collective-permute-start | bytes 2359304 | tf_op jit(solution)/shard_map/ppermute | solution.py:576
  48.9 23.4 %collective-permute-start.14 = (bf16[384,768]{1,0:T(8,128)(2,1)}, bf16[384,768]{1,0:T(8,128)(2,1)S(1)}, u32[]{:S(2)}, u32[]{:S(2)}) collective-permute-start(bf16[384,768]{1,0:T(8,128)(2,1)} %collective-permute-done.r_6_), channel_id=1, source_target_pairs={{0,12},{1,13},{2,14},{3,15},{4,8},{5,9},{6,10},{7,11},{8,4},{9,5},... | collective-permute-start | bytes 1769480 | tf_op jit(solution)/shard_map/ppermute | solution.py:576
  71.0 19.2 %collective-permute-start.15 = (bf16[384,768]{1,0:T(8,128)(2,1)}, bf16[384,768]{1,0:T(8,128)(2,1)S(1)}, u32[]{:S(2)}, u32[]{:S(2)}) collective-permute-start(bf16[384,768]{1,0:T(8,128)(2,1)} %get-tuple-element.184), channel_id=1, source_target_pairs={{0,4},{1,5},{2,6},{3,7},{4,0},{5,1},{6,2},{7,3},{8,12},{9,13},{10,... | collective-permute-start | bytes 1769480 | tf_op jit(solution)/shard_map/ppermute | solution.py:576
  91.0 17.4 %collective-permute-start.19 = (bf16[192,768]{1,0:T(8,128)(2,1)S(1)}, bf16[192,768]{1,0:T(8,128)(2,1)S(1)}, u32[]{:S(2)}, u32[]{:S(2)}) collective-permute-start(bf16[192,768]{1,0:T(8,128)(2,1)S(1)} %add_convert_fusion.15), channel_id=1, source_target_pairs={{0,8},{1,9},{2,10},{3,11},{4,12},{5,13},{6,14},{7,15},{8,0},{9,1},... | collective-permute-start | bytes 884744 | tf_op jit(solution)/shard_map/ppermute | solution.py:576
  91.2 17.2 %collective-permute-start.18 = (bf16[384,768]{1,0:T(8,128)(2,1)}, bf16[384,768]{1,0:T(8,128)(2,1)S(1)}, u32[]{:S(2)}, u32[]{:S(2)}) collective-permute-start(bf16[384,768]{1,0:T(8,128)(2,1)} %get-tuple-element.200), channel_id=1, source_target_pairs={{0,4},{1,5},{2,6},{3,7},{4,0},{5,1},{6,2},{7,3},{8,12},{9,13},{10,... | collective-permute-start | bytes 1769480 | tf_op jit(solution)/shard_map/ppermute | solution.py:576
  91.4 17.0 %collective-permute-start.20 = (bf16[384,768]{1,0:T(8,128)(2,1)}, bf16[384,768]{1,0:T(8,128)(2,1)S(1)}, u32[]{:S(2)}, u32[]{:S(2)}) collective-permute-start(bf16[384,768]{1,0:T(8,128)(2,1)} %get-tuple-element.205), channel_id=1, source_target_pairs={{0,1},{1,0},{2,3},{3,2},{4,5},{5,4},{6,7},{7,6},{8,9},{9,8},{10,11... | collective-permute-start | bytes 1769480 | tf_op jit(solution)/shard_map/ppermute | solution.py:576
  109.0 18.1 %collective-permute-start.24 = (bf16[384,768]{1,0:T(8,128)(2,1)}, bf16[384,768]{1,0:T(8,128)(2,1)}, u32[]{:S(2)}, u32[]{:S(2)}) collective-permute-start(bf16[384,768]{1,0:T(8,128)(2,1)} %get-tuple-element.214), channel_id=1, source_target_pairs={{0,1},{1,0},{2,3},{3,2},{4,5},{5,4},{6,7},{7,6},{8,9},{9,8},{10,11... | collective-permute-start | bytes 1769480 | tf_op jit(solution)/shard_map/ppermute | solution.py:576
  110.1 17.0 %collective-permute-start.21 = (bf16[192,768]{1,0:T(8,128)(2,1)S(1)}, bf16[192,768]{1,0:T(8,128)(2,1)}, u32[]{:S(2)}, u32[]{:S(2)}) collective-permute-start(bf16[192,768]{1,0:T(8,128)(2,1)S(1)} %add_convert_fusion.14), channel_id=1, source_target_pairs={{0,8},{1,9},{2,10},{3,11},{4,12},{5,13},{6,14},{7,15},{8,0},{9,1},... | collective-permute-start | bytes 884744 | tf_op jit(solution)/shard_map/ppermute | solution.py:576
  113.9 14.7 %collective-permute-start.23 = (bf16[384,768]{1,0:T(8,128)(2,1)S(1)}, bf16[384,768]{1,0:T(8,128)(2,1)}, u32[]{:S(2)}, u32[]{:S(2)}) collective-permute-start(bf16[384,768]{1,0:T(8,128)(2,1)S(1)} %add_convert_fusion.2), channel_id=1, source_target_pairs={{0,4},{1,5},{2,6},{3,7},{4,0},{5,1},{6,2},{7,3},{8,12},{9,13},{10,... | collective-permute-start | bytes 1769480 | tf_op jit(solution)/shard_map/ppermute | solution.py:576
  133.5 20.1 %collective-permute-start.27 = (bf16[384,768]{1,0:T(8,128)(2,1)}, bf16[384,768]{1,0:T(8,128)(2,1)}, u32[]{:S(2)}, u32[]{:S(2)}) collective-permute-start(bf16[384,768]{1,0:T(8,128)(2,1)} %add_convert_fusion.1), channel_id=1, source_target_pairs={{0,4},{1,5},{2,6},{3,7},{4,0},{5,1},{6,2},{7,3},{8,12},{9,13},{10,... | collective-permute-start | bytes 1769480 | tf_op jit(solution)/shard_map/ppermute | solution.py:576
  136.7 18.0 %collective-permute-start.30 = (bf16[192,768]{1,0:T(8,128)(2,1)}, bf16[192,768]{1,0:T(8,128)(2,1)}, u32[]{:S(2)}, u32[]{:S(2)}) collective-permute-start(bf16[192,768]{1,0:T(8,128)(2,1)} %add_convert_fusion.12), channel_id=1, source_target_pairs={{0,8},{1,9},{2,10},{3,11},{4,12},{5,13},{6,14},{7,15},{8,0},{9,1},... | collective-permute-start | bytes 884744 | tf_op jit(solution)/shard_map/ppermute | solution.py:576
  139.9 18.5 %collective-permute-start.34 = (bf16[192,768]{1,0:T(8,128)(2,1)S(1)}, bf16[192,768]{1,0:T(8,128)(2,1)S(1)}, u32[]{:S(2)}, u32[]{:S(2)}) collective-permute-start(bf16[192,768]{1,0:T(8,128)(2,1)S(1)} %add_convert_fusion.11), channel_id=1, source_target_pairs={{0,16},{1,17},{2,18},{3,19},{4,20},{5,21},{6,22},{7,23},{8,24},{9,... | collective-permute-start | bytes 884744 | tf_op jit(solution)/shard_map/ppermute | solution.py:576
  142.2 25.6 %collective-permute-start.26 = (bf16[384,768]{1,0:T(8,128)(2,1)S(1)}, bf16[384,768]{1,0:T(8,128)(2,1)}, u32[]{:S(2)}, u32[]{:S(2)}) collective-permute-start(bf16[384,768]{1,0:T(8,128)(2,1)S(1)} %add_convert_fusion), channel_id=1, source_target_pairs={{0,4},{1,5},{2,6},{3,7},{4,0},{5,1},{6,2},{7,3},{8,12},{9,13},{10,... | collective-permute-start | bytes 1769480 | tf_op jit(solution)/shard_map/ppermute | solution.py:576
  157.7 14.2 %collective-permute-start.17 = (bf16[512,768]{1,0:T(8,128)(2,1)S(1)}, bf16[512,768]{1,0:T(8,128)(2,1)}, u32[]{:S(2)}, u32[]{:S(2)}) collective-permute-start(bf16[512,768]{1,0:T(8,128)(2,1)S(1)} %copy-done.34), channel_id=1, source_target_pairs={{0,2},{1,3},{2,0},{3,1},{4,6},{5,7},{6,4},{7,5},{8,10},{9,11},{10,... | collective-permute-start | bytes 2359304 | tf_op jit(solution)/shard_map/ppermute | solution.py:576
  169.0 15.8 %collective-permute-start.38 = (bf16[192,768]{1,0:T(8,128)(2,1)S(1)}, bf16[192,768]{1,0:T(8,128)(2,1)S(1)}, u32[]{:S(2)}, u32[]{:S(2)}) collective-permute-start(bf16[192,768]{1,0:T(8,128)(2,1)S(1)} %add_convert_fusion.6), channel_id=1, source_target_pairs={{0,8},{1,9},{2,10},{3,11},{4,12},{5,13},{6,14},{7,15},{8,0},{9,1},... | collective-permute-start | bytes 884744 | tf_op jit(solution)/shard_map/ppermute | solution.py:576
  169.1 15.7 %collective-permute-start.39 = (bf16[192,768]{1,0:T(8,128)(2,1)S(1)}, bf16[192,768]{1,0:T(8,128)(2,1)S(1)}, u32[]{:S(2)}, u32[]{:S(2)}) collective-permute-start(bf16[192,768]{1,0:T(8,128)(2,1)S(1)} %add_convert_fusion.7), channel_id=1, source_target_pairs={{0,16},{1,17},{2,18},{3,19},{4,20},{5,21},{6,22},{7,23},{8,24},{9,... | collective-permute-start | bytes 884744 | tf_op jit(solution)/shard_map/ppermute | solution.py:576
  184.9 14.7 %collective-permute-start.41 = (bf16[192,768]{1,0:T(8,128)(2,1)S(1)}, bf16[192,768]{1,0:T(8,128)(2,1)S(1)}, u32[]{:S(2)}, u32[]{:S(2)}) collective-permute-start(bf16[192,768]{1,0:T(8,128)(2,1)S(1)} %add_convert_fusion.5.refs_8_), channel_id=1, source_target_pairs={{0,4},{1,5},{2,6},{3,7},{4,0},{5,1},{6,2},{7,3},{8,12},{9,13},{10,... | collective-permute-start | bytes 884744 | tf_op jit(solution)/shard_map/ppermute | solution.py:576
  190.2 17.1 %collective-permute-start.43 = (bf16[192,768]{1,0:T(8,128)(2,1)S(1)}, bf16[192,768]{1,0:T(8,128)(2,1)S(1)}, u32[]{:S(2)}, u32[]{:S(2)}) collective-permute-start(bf16[192,768]{1,0:T(8,128)(2,1)S(1)} %add_convert_fusion.5.refs_8_), channel_id=1, source_target_pairs={{0,12},{1,13},{2,14},{3,15},{4,8},{5,9},{6,10},{7,11},{8,4},{9,5},... | collective-permute-start | bytes 884744 | tf_op jit(solution)/shard_map/ppermute | solution.py:576
  190.9 16.4 %collective-permute-start.44 = (bf16[192,768]{1,0:T(8,128)(2,1)S(1)}, bf16[192,768]{1,0:T(8,128)(2,1)S(1)}, u32[]{:S(2)}, u32[]{:S(2)}) collective-permute-start(bf16[192,768]{1,0:T(8,128)(2,1)S(1)} %collective-permute-done.36.refs_2_), channel_id=1, source_target_pairs={{0,4},{1,5},{2,6},{3,7},{4,0},{5,1},{6,2},{7,3},{8,12},{9,13},{10,... | collective-permute-start | bytes 884744 | tf_op jit(solution)/shard_map/ppermute | solution.py:576
  (76 other events, 517.4 us)
where the time goes:
time: 238 us; the launch traced here: 237 us
  Pallas kernels  99.6 us (42%)
  starting transfers between devices  57.7 us (24%)
  waiting for transfers between devices  52.3 us (22%)
  local copies, waits for them, and re-layouts  13.4 us (6%)
  other arithmetic  12.6 us (5%)
    ppermute x62, starting transfers between devices, swap(): lax.ppermute(value, ('dp', 'tp'), [(i, i ^ mask) for i in range(devices)])  57.7 us
    ppermute x62, waiting for transfers between devices, swap(): lax.ppermute(value, ('dp', 'tp'), [(i, i ^ mask) for i in range(devices)])  52.3 us
    pallas_call x1, Pallas kernels, on_device(): call(lambda *r: mlp_kernel(False, *r), [(one, F32), (one, BF16), (one, F3...  17.1 us
    pallas_call x1, Pallas kernels, on_device(): call(lambda *r: mlp_kernel(True, *r), [(both, BF16), (both, BF16), *[(pai...  17 us
    pallas_call x1, Pallas kernels, on_device(): call(other_back_kernel, [(one, F32), (acts, BF16), (grad_units, BF16), (g...  14.4 us
    pallas_call x1, Pallas kernels, on_device(): call(own_back_kernel, [(acts, BF16), (grad_units, BF16), (grad_units, BF1...  11.9 us
    convert_element_type x16, other arithmetic, total(): add(*[cut(term, part) for term, part in zip(turn(*terms), parts)])  11.9 us
    pallas_call x1, Pallas kernels, on_device(): call(other_fwd_kernel, [(acts, BF16), (head, BF16), (one, F32), (one, BF1...  10.3 us
  transfers between devices with their start and end apart: 62, of which 15 were waited for; matrix products, arithmetic and copies ran while one was open for 8% of the time, Pallas kernels for 41%

commit v1 on v0

--- a/solution.py
+++ b/solution.py
@@ -114,7 +114,7 @@
     for part in range(3):
         value = nn(nrm[...], w[part])
         if part != 1:
-            value = value + bias[pl.ds(part // 2, 1), :]
+            value = value + bias[part // 2]
         qkv[:, part * width : (part + 1) * width] = value.astype(BF16)
 
 
@@ -150,7 +150,7 @@
     over_rows(x.shape[0], norm_rows, 0)
     nrm_out = copies.start(nrm, nrm_hbm)
     wait(w_in)
-    project(nrm, w, bias, qkv)
+    project(nrm, w, [bias[0:1, :], bias[1:2, :]], qkv)
     qkv_out = copies.start(qkv, qkv_hbm)
     attend(lens, ids, qkv, att)
     wait(nrm_out, qkv_out)
@@ -200,7 +200,8 @@
     to_w, to_wo = fetch_weights(copies, ids, mine_parts, sib_parts, w, wo)
     late = [copies.start(x_hbm, x), copies.start(att_own_hbm, att_own), copies.start(wo_own_hbm, wo_own)]
     wait(nrm_in, *to_w)
-    project(nrm, w, bias, qkv)
+    half = w.shape[2]
+    project(nrm, w, [bias[0:1, :half], bias[0:1, half:]], qkv)
     qkv_out = copies.start(qkv, qkv_hbm)
     attend(lens, ids, qkv, att)
     att_out = copies.start(att, att_hbm)
@@ -222,17 +223,17 @@
 def gelu_parts(pre):
     bell = jnp.exp(-0.5 * pre * pre)
     t = 1.0 / (1.0 + (0.3275911 * math.sqrt(0.5)) * jnp.abs(pre))
-    poly = 1.061405429 * t - 1.453152027
-    poly = poly * t + 1.421413741
-    poly = poly * t - 0.284496736
-    poly = poly * t + 0.254829592
-    tail = 0.5 * (poly * t) * bell
+    poly = 0.5307027145 * t - 0.7265760135
+    poly = poly * t + 0.7107068705
+    poly = poly * t - 0.142248368
+    poly = poly * t + 0.127414796
+    tail = poly * t * bell
     cdf = jnp.where(pre >= 0, 1.0 - tail, tail)
     return pre * cdf, cdf + pre * bell * (1.0 / math.sqrt(2.0 * math.pi))
 
 
 def mlp_kernel(own, *refs):
-    ids, nm_a, nm_b, ct_a, ct_b, bias = refs[:6]
+    ids, nm_a, nm_b, ct_a, ct_b, biases = refs[:6]
     if own:
         up_hbm, down_hbm = refs[6:8]
         out_hbm, dnm_hbm, keep_a, send_a, keep_b, send_b, bias_g = refs[8:15]
@@ -273,7 +274,7 @@
     else:
         dnm, out = scratch[11:13]
 
-    piece = 16
+    piece = 32
 
     def half_step(half, total):
         rows = pl.ds(pl.multiple_of(half * tokens, tokens), tokens)
@@ -287,14 +288,15 @@
         def elementwise(step, total):
             at = pl.ds(pl.multiple_of(step * piece, piece), piece)
             to = pl.ds(pl.multiple_of(half * tokens + step * piece, piece), piece)
-            value, slope = gelu_parts(pre[at, :] + bias[...])
+            value, slope = gelu_parts(pre[at, :] + bias)
             act[to, :] = value.astype(BF16)
             back = (dact[at, :] * slope).astype(BF16)
             pg[to, :] = back
             return total + jnp.sum(back.astype(F32), axis=0, keepdims=True)
 
-        return lax.fori_loop(0, tokens // piece, elementwise, total, unroll=2)
-
+        return lax.fori_loop(0, tokens // piece, elementwise, total)
+
+    bias = biases[pl.ds((6 if own else 1 + core), 1), :]
     bias_sum = lax.fori_loop(0, 2, half_step, jnp.zeros((1, hidden), F32))
     bias_g[...] = bias_sum
     writes = []
@@ -473,12 +475,12 @@
     vec[pl.ds(8 + 2 * (1 - half) + core, 1), :] = ub_other[...]
 
 
-def layer_out_kernel(mid_hbm, own_hbm, sib_hbm, bias, out, mid, own, sib, sems):
+def layer_out_kernel(mid_hbm, own_hbm, sib_hbm, vecs, out, mid, own, sib, sems):
     copies = Copies(sems)
     wait(copies.start(mid_hbm, mid), copies.start(own_hbm, own), copies.start(sib_hbm, sib))
 
     def rows(at, carry):
-        out[at, :] = (mid[at, :] + own[at, :] + sib[at, :].astype(F32) + bias[...]).astype(BF16)
+        out[at, :] = (mid[at, :] + own[at, :] + sib[at, :].astype(F32) + vecs[5:6, :]).astype(BF16)
         return carry
 
     over_rows(out.shape[0], rows, 0)
@@ -617,9 +619,8 @@
         core = (flat >> CORE_BIT) & 1
         mine = ((flat >> FAR_BIT) & 1) * 2 + ((flat >> NEAR_BIT) & 1)
         ids = jnp.stack([half, core, mine]).astype(jnp.int32)
-        row = lambda v: v.reshape(1, -1)
-        none = jnp.zeros_like(out_bias)
-        vecs = jnp.stack([attn_gain, attn_shift, out_bias, mlp_gain, mlp_shift, none, none, none])
+        up_bias_own = lax.dynamic_slice(up_bias, (core * hidden,), (hidden,))
+        vecs = jnp.stack([attn_gain, attn_shift, out_bias, mlp_gain, mlp_shift, down_bias, up_bias_own, up_bias_own])
         w_own = jnp.transpose(qkv_weight, (1, 0, 2))
 
         part_rows = wide // (2 * UNITS)
@@ -654,11 +655,8 @@
         )
         mlp_unit = swap(mlp_unit, TP)
         small = jnp.concatenate([bias_late.reshape(-1), up_bias_late])
-        small_other = swap(small.reshape(-1, 128), TP).reshape(-1)
+        small_other = swap(small.reshape(3, wide), TP)
         ct_sib = swap(cotangent, CORE)
-        bias_other = small_other[: 2 * width].reshape(2, width)
-        up_bias_own = lax.dynamic_slice(up_bias, (core * hidden,), (hidden,))
-        up_bias_other = lax.dynamic_slice(small_other, (2 * width + core * hidden,), (hidden,))
         attn_sib = [swap(part, CORE) for part in attn_parts]
         qkv_other, att_other, mid, nm = call(
             other_fwd_kernel,
@@ -672,7 +670,7 @@
             ),
             out_specs=[HB, HB, HB, VM],
         )(
-            lengths, ids, layer_in, after(nrm, mlp_unit), bias_other, att_own, out_weight, vecs,
+            lengths, ids, layer_in, after(nrm, mlp_unit), small_other, att_own, out_weight, vecs,
             *attn_parts, *attn_sib,
         )
         mlp_near, mlp_far = swap(mlp_unit, NEAR), swap(mlp_unit, FAR)
@@ -700,7 +698,7 @@
             gflop=1,
             scratch=mlp_scratch((tall, BF16), (tall, BF16)),
             out_specs=[HB] * 6 + [VM],
-        )(ids, nm, nm_sib, cotangent, ct_sib, row(up_bias_own), up_weight, down_weight)
+        )(ids, nm, nm_sib, cotangent, ct_sib, vecs, up_weight, down_weight)
         out_own, out_sib, dnm_own, dnm_sib, keep_other, send_other, b_other_lo, b_other_hi, ub_other = call(
             lambda *r: mlp_kernel(False, *r),
             [
@@ -712,7 +710,7 @@
             gflop=12,
             scratch=mlp_scratch((tall, BF16), (tall, BF16), (one, F32), (one, BF16), (one, F32), (one, BF16)),
             out_specs=[HB] * 8 + [VM],
-        )(ids, nm, nm_sib, cotangent, ct_sib, row(up_bias_other), *mlp_parts, out_a, dnm_a)
+        )(ids, nm, nm_sib, cotangent, ct_sib, small_other, *mlp_parts, out_a, dnm_a)
         grad_units = (2 * UNITS * part_rows, 2 * width)
         whole, low_half, high_half, first, second = None, (0, 2), (2, 4), (0, 1), (1, 2)
         a_own = swap(send_own, NEAR)
@@ -817,7 +815,7 @@
             "layer_out",
             gflop=0.01,
             scratch=vmem((one, F32), (one, F32), (one, BF16), sems=3),
-        )(mid, out_own, *turn(out_got), row(down_bias))
+        )(mid, out_own, *turn(out_got), vecs)
         note(layer_out)
         a_near, a_far, vec_tp, b2, s_more = due(a_near, a_far, vec_tp, b2, s_more)
         s_unit = rest(s_unit, s_more)
@@ -849,8 +847,12 @@
         note(out_grad)
         vec = step_with(vec, vec_near)
         vec_far = swap(vec, FAR)
-        *b_units, vec_far = due(*b_units, vec_far)
-        b_sib = [swap(value, CORE) for value in b_units]
+        *b_three, b_corner = b_units
+        b_three = due(*b_three)
+        b_sib = [swap(value, CORE) for value in b_three]
+        *b_sib, vec_far, b_corner = due(*b_sib, vec_far, b_corner)
+        b_sib.append(swap(b_corner, CORE))
+        b_units = [*b_three, b_corner]
         vec = vec + vec_far
         down_grad, = call(
             place_down_kernel,

time: 238 us -> 235 us (0.987)
  local copies, waits for them, and re-layouts: 13.4 us -> 10.6 us
    unnamed x74 -> x78, local copies, waits for them, and re-layouts: 4.6 us -> 4.96 us
  transfers between devices with their start and end apart: 62 -> 62, of which waited for: 15 -> 16; matrix products, arithmetic and copies ran while one was open for 8% -> 7% of each run, Pallas kernels for 41% -> 41%
where the time goes in v1:
time: 235 us; the launch traced here: 234 us
  Pallas kernels  99.1 us (42%)
  starting transfers between devices  56.9 us (24%)
  waiting for transfers between devices  53.4 us (23%)
  other arithmetic  12.6 us (5%)
  local copies, waits for them, and re-layouts  10.6 us (5%)
    ppermute x62, starting transfers between devices, swap(): lax.ppermute(value, ('dp', 'tp'), [(i, i ^ mask) for i in range(devices)])  56.9 us
    ppermute x62, waiting for transfers between devices, swap(): lax.ppermute(value, ('dp', 'tp'), [(i, i ^ mask) for i in range(devices)])  53.4 us
    pallas_call x1, Pallas kernels, on_device(): call(lambda *r: mlp_kernel(False, *r), [(one, F32), (one, BF16), (one, F3...  16.9 us
    pallas_call x1, Pallas kernels, on_device(): call(lambda *r: mlp_kernel(True, *r), [(both, BF16), (both, BF16), *[(pai...  16.7 us
    pallas_call x1, Pallas kernels, on_device(): call(other_back_kernel, [(one, F32), (acts, BF16), (grad_units, BF16), (g...  14.4 us
    pallas_call x1, Pallas kernels, on_device(): call(own_back_kernel, [(acts, BF16), (grad_units, BF16), (grad_units, BF1...  11.9 us
    convert_element_type x16, other arithmetic, total(): add(*[cut(term, part) for term, part in zip(turn(*terms), parts)])  11.9 us
    pallas_call x1, Pallas kernels, on_device(): call(other_fwd_kernel, [(acts, BF16), (head, BF16), (one, F32), (one, BF1...  10.3 us
  transfers between devices with their start and end apart: 62, of which 16 were waited for; matrix products, arithmetic and copies ran while one was open for 7% of the time, Pallas kernels for 41%

profile of v1, /device:TPU:1, one launch (start us, length us, event | category | flops | bytes accessed | tf_op | source)
XLA Modules:
  0.0 234.1 jit_solution(5183777867159718400)
XLA Ops:
  2.7 2.1 collective-permute-start.2
  6.2 7.1 %attn_own_fwd.1 = (bf16[512,768]{1,0:T(8,128)(2,1)}, bf16[512,1152]{1,0:T(8,128)(2,1)}, bf16[512,384]{1,0:T(8,128)(2,1)}) custom-call(s32[8,17]{1,0:T(8,128)} %lens.7, s32[3]{0:T(128)} %pad_add_fusion.ids.r_0_.refs_0_, bf16[512,768]{1,0:T(8,128)(2,1)} %x_hbm.5, f32[8,768]{1,0:T(8,128)} %stack.48.vecs.r_5_, bf16[3,768,384]{2,1,0:T(8,128)(2,1)} %bitcast.13, ...), custom_call_target="tpu_custom_call" | custom-call | flops 500000000 | bytes 8388608 | tf_op jit(solution)/shard_map/attn_own_fwd/pallas_call | solution.py:638
  18.8 10.0 %collective-permute-done.1.bias.r_5_ = f32[3,768]{1,0:T(4,128)S(1)} collective-permute-done((f32[3,768]{1,0:T(4,128)S(1)}, f32[3,768]{1,0:T(4,128)S(1)}, u32[]{:S(2)}, u32[]{:S(2)}) %collective-permute-start.1) | collective-permute-done | bytes 9248 | tf_op jit(solution)/shard_map/ppermute | solution.py:578
  35.8 10.3 %attn_other_fwd.1 = (bf16[512,1152]{1,0:T(8,128)(2,1)}, bf16[512,384]{1,0:T(8,128)(2,1)}, f32[512,768]{1,0:T(8,128)}, bf16[512,768]{1,0:T(8,128)(2,1)}) custom-call(s32[8,17]{1,0:T(8,128)} %lens.7, s32[3]{0:T(128)} %pad_add_fusion.ids.r_0_.refs_0_, bf16[512,768]{1,0:T(8,128)(2,1)} %x_hbm.5, bf16[512,768]{1,0:T(8,128)(2,1)} %get-tuple-element.175.nrm_hbm, ...), custom_call_target="tpu_custom_call" | custom-call | flops 6000000000 | bytes 8388608 | tf_op jit(solution)/shard_map/attn_other_fwd/pallas_call | solution.py:661
  52.6 16.7 %mlp_own.1 = (bf16[1024,768]{1,0:T(8,128)(2,1)}, bf16[1024,768]{1,0:T(8,128)(2,1)}, bf16[384,768]{1,0:T(8,128)(2,1)}, bf16[384,768]{1,0:T(8,128)(2,1)}, bf16[384...) custom-call(s32[3]{0:T(128)} %pad_add_fusion.ids.r_0_.refs_0_, ...), custom_call_target="tpu_custom_call" | custom-call | flops 1000000000 | bytes 8388608 | tf_op jit(solution)/shard_map/mlp_own/pallas_call | solution.py:693
  71.0 16.9 %mlp_other.1 = (f32[512,768]{1,0:T(8,128)}, bf16[512,768]{1,0:T(8,128)(2,1)}, f32[512,768]{1,0:T(8,128)}, bf16[512,768]{1,0:T(8,128)(2,1)}, bf16[384,768]{1,0:T(...) custom-call(s32[3]{0:T(128)} %pad_add_fusion.ids.r_0_.refs_0_, ...), custom_call_target="tpu_custom_call" | custom-call | flops 12000000000 | bytes 8388608 | tf_op jit(solution)/shard_map/mlp_other/pallas_call | solution.py:702
  92.4 14.4 %attn_other_back.1 = (f32[512,768]{1,0:T(8,128)}, bf16[512,1152]{1,0:T(8,128)(2,1)}, bf16[768,768]{1,0:T(8,128)(2,1)}, bf16[768,768]{1,0:T(8,128)(2,1)}, f32[8,768]{1,0:T(8,128)}) custom-call(s32[8,17]{1,0:T(8,128)} %lens.7, s32[3]{0:T(128)} %pad_add_fusion.ids.r_0_.refs_0_, f32[512,768]{1,0:T(8,128)} %get-tuple-element.195.dnm_own_hbm, ...), custom_call_target="tpu_custom_call" | custom-call | flops 10000000000 | bytes 8388608 | tf_op jit(solution)/shard_map/attn_other_back/pallas_call | solution.py:725
  113.5 11.9 %attn_own_back.1 = (bf16[512,1152]{1,0:T(8,128)(2,1)}, bf16[768,768]{1,0:T(8,128)(2,1)}, bf16[768,768]{1,0:T(8,128)(2,1)}) custom-call(s32[8,17]{1,0:T(8,128)} %lens.7, s32[3]{0:T(128)} %pad_add_fusion.ids.r_0_.refs_0_, f32[512,768]{1,0:T(8,128)} %get-tuple-element.246.mg_hbm, bf16[384,768]{1,0:T(8,128)(2,1)} %wo_hbm.1, ...), custom_call_target="tpu_custom_call" | custom-call | flops 10000000000 | bytes 8388608 | tf_op jit(solution)/shard_map/attn_own_back/pallas_call | solution.py:749
  125.4 2.0 collective-permute-done.23
  135.7 2.8 %collective-permute-done.28 = bf16[192,768]{1,0:T(8,128)(2,1)S(1)} collective-permute-done((bf16[192,768]{1,0:T(8,128)(2,1)S(1)}, bf16[192,768]{1,0:T(8,128)(2,1)S(1)}, u32[]{:S(2)}, u32[]{:S(2)}) %collective-permute-start.28) | collective-permute-done | bytes 294944 | tf_op jit(solution)/shard_map/ppermute | solution.py:578
  138.7 2.4 %collective-permute-start.34 = (bf16[192,768]{1,0:T(8,128)(2,1)S(1)}, bf16[192,768]{1,0:T(8,128)(2,1)S(1)}, u32[]{:S(2)}, u32[]{:S(2)}) collective-permute-start(bf16[192,768]{1,0:T(8,128)(2,1)S(1)} %add_convert_fusion.11), channel_id=1, source_target_pairs={{0,16},{1,17},{2,18},{3,19},{4,20},{5,21},{6,22},{7,23},{8,24},{9,... | collective-permute-start | bytes 884744 | tf_op jit(solution)/shard_map/ppermute | solution.py:578
  141.7 8.8 %input_grad.1 = (bf16[512,768]{1,0:T(8,128)(2,1)}, f32[16,768]{1,0:T(8,128)}) custom-call(s32[3]{0:T(128)} %pad_add_fusion.ids.r_0_.refs_0_, bf16[512,1152]{1,0:T(8,128)(2,1)} %get-tuple-element.222.dqkv_a_hbm, bf16[512,1152]{1,0:T(8,128)(2,1)} %get-tuple-element.240.dqkv_b_hbm, f32[512,768]{1,0:T(8,128)} %get-tuple-element.246.mg_hbm, ...), custom_call_target="tpu_custom_call" | custom-call | flops 10000000 | bytes 8388608 | tf_op jit(solution)/shard_map/input_grad/pallas_call | solution.py:770
  156.1 6.2 %collective-permute-done.33 = f32[16,768]{1,0:T(8,128)S(1)} collective-permute-done((f32[16,768]{1,0:T(8,128)S(1)}, f32[16,768]{1,0:T(8,128)S(1)}, u32[]{:S(2)}, u32[]{:S(2)}) %collective-permute-start.33) | collective-permute-done | bytes 49184 | tf_op jit(solution)/shard_map/ppermute | solution.py:578
  167.1 2.8 %collective-permute-start.39 = (bf16[192,768]{1,0:T(8,128)(2,1)S(1)}, bf16[192,768]{1,0:T(8,128)(2,1)S(1)}, u32[]{:S(2)}, u32[]{:S(2)}) collective-permute-start(bf16[192,768]{1,0:T(8,128)(2,1)S(1)} %add_convert_fusion.7), channel_id=1, source_target_pairs={{0,16},{1,17},{2,18},{3,19},{4,20},{5,21},{6,22},{7,23},{8,24},{9,... | collective-permute-start | bytes 884744 | tf_op jit(solution)/shard_map/ppermute | solution.py:578
  171.1 4.0 %layer_out.1 = bf16[512,768]{1,0:T(8,128)(2,1)} custom-call(f32[512,768]{1,0:T(8,128)} %get-tuple-element.179.mid_hbm, f32[512,768]{1,0:T(8,128)} %get-tuple-element.186.own_hbm, bf16[512,768]{1,0:T(8,128)(2,1)} %collective-permute-done.17.sib_hbm, f32[8,768]{1,0:T(8,128)} %stack.48.vecs.r_5_), custom_call_target="tpu_custom_call" | custom-call | flops 10000000 | bytes 8388608 | tf_op jit(solution)/shard_map/layer_out/pallas_call | solution.py:811
  175.2 7.6 %collective-permute-done.38 = bf16[192,768]{1,0:T(8,128)(2,1)S(1)} collective-permute-done((bf16[192,768]{1,0:T(8,128)(2,1)S(1)}, bf16[192,768]{1,0:T(8,128)(2,1)S(1)}, u32[]{:S(2)}, u32[]{:S(2)}) %collective-permute-start.38) | collective-permute-done | bytes 294944 | tf_op jit(solution)/shard_map/ppermute | solution.py:578
  184.9 2.0 collective-permute-start.45
  189.6 7.5 %collective-permute-done.45 = bf16[192,768]{1,0:T(8,128)(2,1)S(1)} collective-permute-done((bf16[192,768]{1,0:T(8,128)(2,1)S(1)}, bf16[192,768]{1,0:T(8,128)(2,1)S(1)}, u32[]{:S(2)}, u32[]{:S(2)}) %collective-permute-start.45) | collective-permute-done | bytes 294944 | tf_op jit(solution)/shard_map/ppermute | solution.py:578
  197.1 8.3 %collective-permute-done.43.refs_11_ = bf16[192,768]{1,0:T(8,128)(2,1)S(1)} collective-permute-done((bf16[192,768]{1,0:T(8,128)(2,1)S(1)}, bf16[192,768]{1,0:T(8,128)(2,1)S(1)}, u32[]{:S(2)}, u32[]{:S(2)}) %collective-permute-start.43) | collective-permute-done | bytes 294944 | tf_op jit(solution)/shard_map/ppermute | solution.py:578
  205.5 3.0 %collective-permute-start.50 = (bf16[192,768]{1,0:T(8,128)(2,1)S(1)}, bf16[192,768]{1,0:T(8,128)(2,1)S(1)}, u32[]{:S(2)}, u32[]{:S(2)}) collective-permute-start(bf16[192,768]{1,0:T(8,128)(2,1)S(1)} %add_convert_fusion.5.refs_8_), channel_id=1, source_target_pairs={{0,2},{1,3},{2,0},{3,1},{4,6},{5,7},{6,4},{7,5},{8,10},{9,11},{10,... | collective-permute-start | bytes 884744 | tf_op jit(solution)/shard_map/ppermute | solution.py:578
  214.4 5.7 %place_two.1 = (f32[768,1536]{1,0:T(8,128)}, f32[3,768,384]{2,1,0:T(8,128)}, f32[384,768]{1,0:T(8,128)}) custom-call(s32[3]{0:T(128)S(1)} %copy-done, bf16[192,768]{1,0:T(8,128)(2,1)S(1)} %add_convert_fusion.8.refs_0_, bf16[192,768]{1,0:T(8,128)(2,1)S(1)} %collective-permute-done.35.refs_1_, bf16[192,768]{1,0:T(8,128)(2,1)S(1)} %collective-permute-done.36.refs_2_, ...), custom_call_target="tpu_custom_call" | custom-call | flops 10000000 | bytes 8388608 | tf_op jit(solution)/shard_map/place_two/pallas_call | solution.py:834
  220.5 2.1 collective-permute-start.56
  224.2 2.2 collective-permute-done.60.refs_4_
  230.6 3.4 %place_down.1 = f32[1536,768]{1,0:T(8,128)} custom-call(s32[3]{0:T(128)S(1)} %copy-done, bf16[192,768]{1,0:T(8,128)(2,1)S(1)} %add_convert_fusion.3.refs_1_, bf16[192,768]{1,0:T(8,128)(2,1)S(1)} %collective-permute-done.54.refs_2_, bf16[192,768]{1,0:T(8,128)(2,1)S(1)} %collective-permute-done.55.refs_3_, ...), custom_call_target="tpu_custom_call" | custom-call | flops 1000000000 | bytes 8388608 | tf_op jit(solution)/shard_map/place_down/pallas_call | solution.py:857
  (234 shorter events, 72.3 us)
Async XLA Ops:
  14.6 17.1 %collective-permute-start = (bf16[384,768]{1,0:T(8,128)(2,1)S(1)}, bf16[384,768]{1,0:T(8,128)(2,1)}, u32[]{:S(2)}, u32[]{:S(2)}) collective-permute-start(bf16[384,768]{1,0:T(8,128)(2,1)S(1)} %pad_maximum_fusion), channel_id=1, source_target_pairs={{0,1},{1,0},{2,3},{3,2},{4,5},{5,4},{6,7},{7,6},{8,9},{9,8},{10,11... | collective-permute-start | bytes 1769480 | tf_op jit(solution)/shard_map/ppermute | solution.py:578
  14.7 16.0 %collective-permute-start.3 = (bf16[192,768]{1,0:T(8,128)(2,1)S(1)}, bf16[192,768]{1,0:T(8,128)(2,1)S(1)}, u32[]{:S(2)}, u32[]{:S(2)}) collective-permute-start(bf16[192,768]{1,0:T(8,128)(2,1)S(1)} %collective-permute-done.2.refs_0_), channel_id=1, source_target_pairs={{0,4},{1,5},{2,6},{3,7},{4,0},{5,1},{6,2},{7,3},{8,12},{9,13},{10,... | collective-permute-start | bytes 884744 | tf_op jit(solution)/shard_map/ppermute | solution.py:578
  16.1 14.7 %collective-permute-start.4 = (bf16[192,768]{1,0:T(8,128)(2,1)S(1)}, bf16[192,768]{1,0:T(8,128)(2,1)S(1)}, u32[]{:S(2)}, u32[]{:S(2)}) collective-permute-start(bf16[192,768]{1,0:T(8,128)(2,1)S(1)} %collective-permute-done.2.refs_0_), channel_id=1, source_target_pairs={{0,8},{1,9},{2,10},{3,11},{4,12},{5,13},{6,14},{7,15},{8,0},{9,1},... | collective-permute-start | bytes 884744 | tf_op jit(solution)/shard_map/ppermute | solution.py:578
  31.7 15.2 %collective-permute-start.10 = (bf16[384,768]{1,0:T(8,128)(2,1)}, bf16[384,768]{1,0:T(8,128)(2,1)S(1)}, u32[]{:S(2)}, u32[]{:S(2)}) collective-permute-start(bf16[384,768]{1,0:T(8,128)(2,1)} %collective-permute-done.r_6_), channel_id=1, source_target_pairs={{0,4},{1,5},{2,6},{3,7},{4,0},{5,1},{6,2},{7,3},{8,12},{9,13},{10,... | collective-permute-start | bytes 1769480 | tf_op jit(solution)/shard_map/ppermute | solution.py:578
  33.0 14.9 %collective-permute-start.11 = (bf16[384,768]{1,0:T(8,128)(2,1)}, bf16[384,768]{1,0:T(8,128)(2,1)}, u32[]{:S(2)}, u32[]{:S(2)}) collective-permute-start(bf16[384,768]{1,0:T(8,128)(2,1)} %collective-permute-done.r_6_), channel_id=1, source_target_pairs={{0,8},{1,9},{2,10},{3,11},{4,12},{5,13},{6,14},{7,15},{8,0},{9,1},... | collective-permute-start | bytes 1769480 | tf_op jit(solution)/shard_map/ppermute | solution.py:578
  34.3 16.5 %collective-permute-start.13 = (bf16[512,768]{1,0:T(8,128)(2,1)S(1)}, bf16[512,768]{1,0:T(8,128)(2,1)S(1)}, u32[]{:S(2)}, u32[]{:S(2)}) collective-permute-start(bf16[512,768]{1,0:T(8,128)(2,1)S(1)} %copy-done.4), channel_id=1, source_target_pairs={{0,2},{1,3},{2,0},{3,1},{4,6},{5,7},{6,4},{7,5},{8,10},{9,11},{10,... | collective-permute-start | bytes 2359304 | tf_op jit(solution)/shard_map/ppermute | solution.py:578
  49.1 21.1 %collective-permute-start.14 = (bf16[384,768]{1,0:T(8,128)(2,1)}, bf16[384,768]{1,0:T(8,128)(2,1)S(1)}, u32[]{:S(2)}, u32[]{:S(2)}) collective-permute-start(bf16[384,768]{1,0:T(8,128)(2,1)} %collective-permute-done.r_6_), channel_id=1, source_target_pairs={{0,12},{1,13},{2,14},{3,15},{4,8},{5,9},{6,10},{7,11},{8,4},{9,5},... | collective-permute-start | bytes 1769480 | tf_op jit(solution)/shard_map/ppermute | solution.py:578
  69.3 18.5 %collective-permute-start.15 = (bf16[384,768]{1,0:T(8,128)(2,1)}, bf16[384,768]{1,0:T(8,128)(2,1)S(1)}, u32[]{:S(2)}, u32[]{:S(2)}) collective-permute-start(bf16[384,768]{1,0:T(8,128)(2,1)} %get-tuple-element.187), channel_id=1, source_target_pairs={{0,4},{1,5},{2,6},{3,7},{4,0},{5,1},{6,2},{7,3},{8,12},{9,13},{10,... | collective-permute-start | bytes 1769480 | tf_op jit(solution)/shard_map/ppermute | solution.py:578
  88.6 18.3 %collective-permute-start.19 = (bf16[192,768]{1,0:T(8,128)(2,1)S(1)}, bf16[192,768]{1,0:T(8,128)(2,1)S(1)}, u32[]{:S(2)}, u32[]{:S(2)}) collective-permute-start(bf16[192,768]{1,0:T(8,128)(2,1)S(1)} %add_convert_fusion.15), channel_id=1, source_target_pairs={{0,8},{1,9},{2,10},{3,11},{4,12},{5,13},{6,14},{7,15},{8,0},{9,1},... | collective-permute-start | bytes 884744 | tf_op jit(solution)/shard_map/ppermute | solution.py:578
  89.5 17.4 %collective-permute-start.18 = (bf16[384,768]{1,0:T(8,128)(2,1)}, bf16[384,768]{1,0:T(8,128)(2,1)S(1)}, u32[]{:S(2)}, u32[]{:S(2)}) collective-permute-start(bf16[384,768]{1,0:T(8,128)(2,1)} %get-tuple-element.203), channel_id=1, source_target_pairs={{0,4},{1,5},{2,6},{3,7},{4,0},{5,1},{6,2},{7,3},{8,12},{9,13},{10,... | collective-permute-start | bytes 1769480 | tf_op jit(solution)/shard_map/ppermute | solution.py:578
  90.2 16.6 %collective-permute-start.20 = (bf16[384,768]{1,0:T(8,128)(2,1)}, bf16[384,768]{1,0:T(8,128)(2,1)S(1)}, u32[]{:S(2)}, u32[]{:S(2)}) collective-permute-start(bf16[384,768]{1,0:T(8,128)(2,1)} %get-tuple-element.208), channel_id=1, source_target_pairs={{0,1},{1,0},{2,3},{3,2},{4,5},{5,4},{6,7},{7,6},{8,9},{9,8},{10,11... | collective-permute-start | bytes 1769480 | tf_op jit(solution)/shard_map/ppermute | solution.py:578
  107.8 17.6 %collective-permute-start.24 = (bf16[384,768]{1,0:T(8,128)(2,1)}, bf16[384,768]{1,0:T(8,128)(2,1)}, u32[]{:S(2)}, u32[]{:S(2)}) collective-permute-start(bf16[384,768]{1,0:T(8,128)(2,1)} %get-tuple-element.217), channel_id=1, source_target_pairs={{0,1},{1,0},{2,3},{3,2},{4,5},{5,4},{6,7},{7,6},{8,9},{9,8},{10,11... | collective-permute-start | bytes 1769480 | tf_op jit(solution)/shard_map/ppermute | solution.py:578
  108.1 17.3 %collective-permute-start.21 = (bf16[192,768]{1,0:T(8,128)(2,1)S(1)}, bf16[192,768]{1,0:T(8,128)(2,1)}, u32[]{:S(2)}, u32[]{:S(2)}) collective-permute-start(bf16[192,768]{1,0:T(8,128)(2,1)S(1)} %add_convert_fusion.14), channel_id=1, source_target_pairs={{0,8},{1,9},{2,10},{3,11},{4,12},{5,13},{6,14},{7,15},{8,0},{9,1},... | collective-permute-start | bytes 884744 | tf_op jit(solution)/shard_map/ppermute | solution.py:578
  112.7 14.7 %collective-permute-start.23 = (bf16[384,768]{1,0:T(8,128)(2,1)S(1)}, bf16[384,768]{1,0:T(8,128)(2,1)}, u32[]{:S(2)}, u32[]{:S(2)}) collective-permute-start(bf16[384,768]{1,0:T(8,128)(2,1)S(1)} %add_convert_fusion.2), channel_id=1, source_target_pairs={{0,4},{1,5},{2,6},{3,7},{4,0},{5,1},{6,2},{7,3},{8,12},{9,13},{10,... | collective-permute-start | bytes 1769480 | tf_op jit(solution)/shard_map/ppermute | solution.py:578
  132.3 19.6 %collective-permute-start.27 = (bf16[384,768]{1,0:T(8,128)(2,1)}, bf16[384,768]{1,0:T(8,128)(2,1)}, u32[]{:S(2)}, u32[]{:S(2)}) collective-permute-start(bf16[384,768]{1,0:T(8,128)(2,1)} %add_convert_fusion.1), channel_id=1, source_target_pairs={{0,4},{1,5},{2,6},{3,7},{4,0},{5,1},{6,2},{7,3},{8,12},{9,13},{10,... | collective-permute-start | bytes 1769480 | tf_op jit(solution)/shard_map/ppermute | solution.py:578
  134.9 18.0 %collective-permute-start.30 = (bf16[192,768]{1,0:T(8,128)(2,1)}, bf16[192,768]{1,0:T(8,128)(2,1)}, u32[]{:S(2)}, u32[]{:S(2)}) collective-permute-start(bf16[192,768]{1,0:T(8,128)(2,1)} %add_convert_fusion.12), channel_id=1, source_target_pairs={{0,8},{1,9},{2,10},{3,11},{4,12},{5,13},{6,14},{7,15},{8,0},{9,1},... | collective-permute-start | bytes 884744 | tf_op jit(solution)/shard_map/ppermute | solution.py:578
  138.7 17.2 %collective-permute-start.34 = (bf16[192,768]{1,0:T(8,128)(2,1)S(1)}, bf16[192,768]{1,0:T(8,128)(2,1)S(1)}, u32[]{:S(2)}, u32[]{:S(2)}) collective-permute-start(bf16[192,768]{1,0:T(8,128)(2,1)S(1)} %add_convert_fusion.11), channel_id=1, source_target_pairs={{0,16},{1,17},{2,18},{3,19},{4,20},{5,21},{6,22},{7,23},{8,24},{9,... | collective-permute-start | bytes 884744 | tf_op jit(solution)/shard_map/ppermute | solution.py:578
  141.0 24.7 %collective-permute-start.26 = (bf16[384,768]{1,0:T(8,128)(2,1)S(1)}, bf16[384,768]{1,0:T(8,128)(2,1)}, u32[]{:S(2)}, u32[]{:S(2)}) collective-permute-start(bf16[384,768]{1,0:T(8,128)(2,1)S(1)} %add_convert_fusion), channel_id=1, source_target_pairs={{0,4},{1,5},{2,6},{3,7},{4,0},{5,1},{6,2},{7,3},{8,12},{9,13},{10,... | collective-permute-start | bytes 1769480 | tf_op jit(solution)/shard_map/ppermute | solution.py:578
  155.3 14.6 %collective-permute-start.17 = (bf16[512,768]{1,0:T(8,128)(2,1)S(1)}, bf16[512,768]{1,0:T(8,128)(2,1)}, u32[]{:S(2)}, u32[]{:S(2)}) collective-permute-start(bf16[512,768]{1,0:T(8,128)(2,1)S(1)} %copy-done.34), channel_id=1, source_target_pairs={{0,2},{1,3},{2,0},{3,1},{4,6},{5,7},{6,4},{7,5},{8,10},{9,11},{10,... | collective-permute-start | bytes 2359304 | tf_op jit(solution)/shard_map/ppermute | solution.py:578
  167.0 15.8 %collective-permute-start.38 = (bf16[192,768]{1,0:T(8,128)(2,1)S(1)}, bf16[192,768]{1,0:T(8,128)(2,1)S(1)}, u32[]{:S(2)}, u32[]{:S(2)}) collective-permute-start(bf16[192,768]{1,0:T(8,128)(2,1)S(1)} %add_convert_fusion.6), channel_id=1, source_target_pairs={{0,8},{1,9},{2,10},{3,11},{4,12},{5,13},{6,14},{7,15},{8,0},{9,1},... | collective-permute-start | bytes 884744 | tf_op jit(solution)/shard_map/ppermute | solution.py:578
  167.1 15.7 %collective-permute-start.39 = (bf16[192,768]{1,0:T(8,128)(2,1)S(1)}, bf16[192,768]{1,0:T(8,128)(2,1)S(1)}, u32[]{:S(2)}, u32[]{:S(2)}) collective-permute-start(bf16[192,768]{1,0:T(8,128)(2,1)S(1)} %add_convert_fusion.7), channel_id=1, source_target_pairs={{0,16},{1,17},{2,18},{3,19},{4,20},{5,21},{6,22},{7,23},{8,24},{9,... | collective-permute-start | bytes 884744 | tf_op jit(solution)/shard_map/ppermute | solution.py:578
  182.9 14.2 %collective-permute-start.41 = (bf16[192,768]{1,0:T(8,128)(2,1)S(1)}, bf16[192,768]{1,0:T(8,128)(2,1)S(1)}, u32[]{:S(2)}, u32[]{:S(2)}) collective-permute-start(bf16[192,768]{1,0:T(8,128)(2,1)S(1)} %add_convert_fusion.5.refs_8_), channel_id=1, source_target_pairs={{0,4},{1,5},{2,6},{3,7},{4,0},{5,1},{6,2},{7,3},{8,12},{9,13},{10,... | collective-permute-start | bytes 884744 | tf_op jit(solution)/shard_map/ppermute | solution.py:578
  187.8 17.6 %collective-permute-start.43 = (bf16[192,768]{1,0:T(8,128)(2,1)S(1)}, bf16[192,768]{1,0:T(8,128)(2,1)S(1)}, u32[]{:S(2)}, u32[]{:S(2)}) collective-permute-start(bf16[192,768]{1,0:T(8,128)(2,1)S(1)} %add_convert_fusion.5.refs_8_), channel_id=1, source_target_pairs={{0,12},{1,13},{2,14},{3,15},{4,8},{5,9},{6,10},{7,11},{8,4},{9,5},... | collective-permute-start | bytes 884744 | tf_op jit(solution)/shard_map/ppermute | solution.py:578
  188.9 16.5 %collective-permute-start.44 = (bf16[192,768]{1,0:T(8,128)(2,1)S(1)}, bf16[192,768]{1,0:T(8,128)(2,1)S(1)}, u32[]{:S(2)}, u32[]{:S(2)}) collective-permute-start(bf16[192,768]{1,0:T(8,128)(2,1)S(1)} %collective-permute-done.36.refs_2_), channel_id=1, source_target_pairs={{0,4},{1,5},{2,6},{3,7},{4,0},{5,1},{6,2},{7,3},{8,12},{9,13},{10,... | collective-permute-start | bytes 884744 | tf_op jit(solution)/shard_map/ppermute | solution.py:578
  (78 other events, 512.7 us)

commit v2 on v1

--- a/solution.py
+++ b/solution.py
@@ -290,15 +290,15 @@
             to = pl.ds(pl.multiple_of(half * tokens + step * piece, piece), piece)
             value, slope = gelu_parts(pre[at, :] + bias)
             act[to, :] = value.astype(BF16)
-            back = (dact[at, :] * slope).astype(BF16)
-            pg[to, :] = back
-            return total + jnp.sum(back.astype(F32), axis=0, keepdims=True)
+            back = dact[at, :] * slope
+            pg[to, :] = back.astype(BF16)
+            return total + jnp.sum(back.reshape(piece // 8, 8, hidden), axis=0)
 
         return lax.fori_loop(0, tokens // piece, elementwise, total)
 
     bias = biases[pl.ds((6 if own else 1 + core), 1), :]
-    bias_sum = lax.fori_loop(0, 2, half_step, jnp.zeros((1, hidden), F32))
-    bias_g[...] = bias_sum
+    bias_sum = lax.fori_loop(0, 2, half_step, jnp.zeros((8, hidden), F32))
+    bias_g[...] = jnp.sum(bias_sum, axis=0, keepdims=True)
     writes = []
     if own:
         dnm[...] = nt(pg[...], up[...]).astype(BF16)

time: 235 us -> 234 us (level)
  no operation moved by 1% of the time
where the time goes in v2:
time: 234 us; the launch traced here: 233 us
  Pallas kernels  98.4 us (42%)
  starting transfers between devices  56.9 us (24%)
  waiting for transfers between devices  53.4 us (23%)
  other arithmetic  12.5 us (5%)
  local copies, waits for them, and re-layouts  10.6 us (5%)
    ppermute x62, starting transfers between devices, swap(): lax.ppermute(value, ('dp', 'tp'), [(i, i ^ mask) for i in range(devices)])  56.9 us
    ppermute x62, waiting for transfers between devices, swap(): lax.ppermute(value, ('dp', 'tp'), [(i, i ^ mask) for i in range(devices)])  53.4 us
    pallas_call x1, Pallas kernels, on_device(): call(lambda *r: mlp_kernel(False, *r), [(one, F32), (one, BF16), (one, F3...  16.5 us
    pallas_call x1, Pallas kernels, on_device(): call(lambda *r: mlp_kernel(True, *r), [(both, BF16), (both, BF16), *[(pai...  16.3 us
    pallas_call x1, Pallas kernels, on_device(): call(other_back_kernel, [(one, F32), (acts, BF16), (grad_units, BF16), (g...  14.4 us
    pallas_call x1, Pallas kernels, on_device(): call(own_back_kernel, [(acts, BF16), (grad_units, BF16), (grad_units, BF1...  11.9 us
    convert_element_type x16, other arithmetic, total(): add(*[cut(term, part) for term, part in zip(turn(*terms), parts)])  11.9 us
    pallas_call x1, Pallas kernels, on_device(): call(other_fwd_kernel, [(acts, BF16), (head, BF16), (one, F32), (one, BF1...  10.3 us
  transfers between devices with their start and end apart: 62, of which 16 were waited for; matrix products, arithmetic and copies ran while one was open for 7% of the time, Pallas kernels for 41%

profile of v2, /device:TPU:1, one launch (start us, length us, event | category | flops | bytes accessed | tf_op | source)
XLA Modules:
  0.0 233.4 jit_solution(12545262105674186614)
XLA Ops:
  2.7 2.1 collective-permute-start.2
  6.2 7.1 %attn_own_fwd.1 = (bf16[512,768]{1,0:T(8,128)(2,1)}, bf16[512,1152]{1,0:T(8,128)(2,1)}, bf16[512,384]{1,0:T(8,128)(2,1)}) custom-call(s32[8,17]{1,0:T(8,128)} %lens.7, s32[3]{0:T(128)} %pad_add_fusion.ids.r_0_.refs_0_, bf16[512,768]{1,0:T(8,128)(2,1)} %x_hbm.5, f32[8,768]{1,0:T(8,128)} %stack.48.vecs.r_5_, bf16[3,768,384]{2,1,0:T(8,128)(2,1)} %bitcast.13, ...), custom_call_target="tpu_custom_call" | custom-call | flops 500000000 | bytes 8388608 | tf_op jit(solution)/shard_map/attn_own_fwd/pallas_call | solution.py:638
  18.8 10.0 %collective-permute-done.1.bias.r_5_ = f32[3,768]{1,0:T(4,128)S(1)} collective-permute-done((f32[3,768]{1,0:T(4,128)S(1)}, f32[3,768]{1,0:T(4,128)S(1)}, u32[]{:S(2)}, u32[]{:S(2)}) %collective-permute-start.1) | collective-permute-done | bytes 9248 | tf_op jit(solution)/shard_map/ppermute | solution.py:578
  35.8 10.3 %attn_other_fwd.1 = (bf16[512,1152]{1,0:T(8,128)(2,1)}, bf16[512,384]{1,0:T(8,128)(2,1)}, f32[512,768]{1,0:T(8,128)}, bf16[512,768]{1,0:T(8,128)(2,1)}) custom-call(s32[8,17]{1,0:T(8,128)} %lens.7, s32[3]{0:T(128)} %pad_add_fusion.ids.r_0_.refs_0_, bf16[512,768]{1,0:T(8,128)(2,1)} %x_hbm.5, bf16[512,768]{1,0:T(8,128)(2,1)} %get-tuple-element.175.nrm_hbm, ...), custom_call_target="tpu_custom_call" | custom-call | flops 6000000000 | bytes 8388608 | tf_op jit(solution)/shard_map/attn_other_fwd/pallas_call | solution.py:661
  52.6 16.3 %mlp_own.1 = (bf16[1024,768]{1,0:T(8,128)(2,1)}, bf16[1024,768]{1,0:T(8,128)(2,1)}, bf16[384,768]{1,0:T(8,128)(2,1)}, bf16[384,768]{1,0:T(8,128)(2,1)}, bf16[384...) custom-call(s32[3]{0:T(128)} %pad_add_fusion.ids.r_0_.refs_0_, ...), custom_call_target="tpu_custom_call" | custom-call | flops 1000000000 | bytes 8388608 | tf_op jit(solution)/shard_map/mlp_own/pallas_call | solution.py:693
  70.6 16.5 %mlp_other.1 = (f32[512,768]{1,0:T(8,128)}, bf16[512,768]{1,0:T(8,128)(2,1)}, f32[512,768]{1,0:T(8,128)}, bf16[512,768]{1,0:T(8,128)(2,1)}, bf16[384,768]{1,0:T(...) custom-call(s32[3]{0:T(128)} %pad_add_fusion.ids.r_0_.refs_0_, ...), custom_call_target="tpu_custom_call" | custom-call | flops 12000000000 | bytes 8388608 | tf_op jit(solution)/shard_map/mlp_other/pallas_call | solution.py:702
  91.6 14.4 %attn_other_back.1 = (f32[512,768]{1,0:T(8,128)}, bf16[512,1152]{1,0:T(8,128)(2,1)}, bf16[768,768]{1,0:T(8,128)(2,1)}, bf16[768,768]{1,0:T(8,128)(2,1)}, f32[8,768]{1,0:T(8,128)}) custom-call(s32[8,17]{1,0:T(8,128)} %lens.7, s32[3]{0:T(128)} %pad_add_fusion.ids.r_0_.refs_0_, f32[512,768]{1,0:T(8,128)} %get-tuple-element.195.dnm_own_hbm, ...), custom_call_target="tpu_custom_call" | custom-call | flops 10000000000 | bytes 8388608 | tf_op jit(solution)/shard_map/attn_other_back/pallas_call | solution.py:725
  112.7 11.9 %attn_own_back.1 = (bf16[512,1152]{1,0:T(8,128)(2,1)}, bf16[768,768]{1,0:T(8,128)(2,1)}, bf16[768,768]{1,0:T(8,128)(2,1)}) custom-call(s32[8,17]{1,0:T(8,128)} %lens.7, s32[3]{0:T(128)} %pad_add_fusion.ids.r_0_.refs_0_, f32[512,768]{1,0:T(8,128)} %get-tuple-element.246.mg_hbm, bf16[384,768]{1,0:T(8,128)(2,1)} %wo_hbm.1, ...), custom_call_target="tpu_custom_call" | custom-call | flops 10000000000 | bytes 8388608 | tf_op jit(solution)/shard_map/attn_own_back/pallas_call | solution.py:749
  124.6 2.0 collective-permute-done.23
  134.9 2.8 %collective-permute-done.28 = bf16[192,768]{1,0:T(8,128)(2,1)S(1)} collective-permute-done((bf16[192,768]{1,0:T(8,128)(2,1)S(1)}, bf16[192,768]{1,0:T(8,128)(2,1)S(1)}, u32[]{:S(2)}, u32[]{:S(2)}) %collective-permute-start.28) | collective-permute-done | bytes 294944 | tf_op jit(solution)/shard_map/ppermute | solution.py:578
  137.9 2.4 %collective-permute-start.34 = (bf16[192,768]{1,0:T(8,128)(2,1)S(1)}, bf16[192,768]{1,0:T(8,128)(2,1)S(1)}, u32[]{:S(2)}, u32[]{:S(2)}) collective-permute-start(bf16[192,768]{1,0:T(8,128)(2,1)S(1)} %add_convert_fusion.11), channel_id=1, source_target_pairs={{0,16},{1,17},{2,18},{3,19},{4,20},{5,21},{6,22},{7,23},{8,24},{9,... | collective-permute-start | bytes 884744 | tf_op jit(solution)/shard_map/ppermute | solution.py:578
  141.0 8.8 %input_grad.1 = (bf16[512,768]{1,0:T(8,128)(2,1)}, f32[16,768]{1,0:T(8,128)}) custom-call(s32[3]{0:T(128)} %pad_add_fusion.ids.r_0_.refs_0_, bf16[512,1152]{1,0:T(8,128)(2,1)} %get-tuple-element.222.dqkv_a_hbm, bf16[512,1152]{1,0:T(8,128)(2,1)} %get-tuple-element.240.dqkv_b_hbm, f32[512,768]{1,0:T(8,128)} %get-tuple-element.246.mg_hbm, ...), custom_call_target="tpu_custom_call" | custom-call | flops 10000000 | bytes 8388608 | tf_op jit(solution)/shard_map/input_grad/pallas_call | solution.py:770
  155.4 6.2 %collective-permute-done.33 = f32[16,768]{1,0:T(8,128)S(1)} collective-permute-done((f32[16,768]{1,0:T(8,128)S(1)}, f32[16,768]{1,0:T(8,128)S(1)}, u32[]{:S(2)}, u32[]{:S(2)}) %collective-permute-start.33) | collective-permute-done | bytes 49184 | tf_op jit(solution)/shard_map/ppermute | solution.py:578
  166.3 2.8 %collective-permute-start.39 = (bf16[192,768]{1,0:T(8,128)(2,1)S(1)}, bf16[192,768]{1,0:T(8,128)(2,1)S(1)}, u32[]{:S(2)}, u32[]{:S(2)}) collective-permute-start(bf16[192,768]{1,0:T(8,128)(2,1)S(1)} %add_convert_fusion.7), channel_id=1, source_target_pairs={{0,16},{1,17},{2,18},{3,19},{4,20},{5,21},{6,22},{7,23},{8,24},{9,... | collective-permute-start | bytes 884744 | tf_op jit(solution)/shard_map/ppermute | solution.py:578
  170.4 4.0 %layer_out.1 = bf16[512,768]{1,0:T(8,128)(2,1)} custom-call(f32[512,768]{1,0:T(8,128)} %get-tuple-element.179.mid_hbm, f32[512,768]{1,0:T(8,128)} %get-tuple-element.186.own_hbm, bf16[512,768]{1,0:T(8,128)(2,1)} %collective-permute-done.17.sib_hbm, f32[8,768]{1,0:T(8,128)} %stack.48.vecs.r_5_), custom_call_target="tpu_custom_call" | custom-call | flops 10000000 | bytes 8388608 | tf_op jit(solution)/shard_map/layer_out/pallas_call | solution.py:811
  174.4 7.7 %collective-permute-done.38 = bf16[192,768]{1,0:T(8,128)(2,1)S(1)} collective-permute-done((bf16[192,768]{1,0:T(8,128)(2,1)S(1)}, bf16[192,768]{1,0:T(8,128)(2,1)S(1)}, u32[]{:S(2)}, u32[]{:S(2)}) %collective-permute-start.38) | collective-permute-done | bytes 294944 | tf_op jit(solution)/shard_map/ppermute | solution.py:578
  184.2 2.0 collective-permute-start.45
  188.8 7.5 %collective-permute-done.45 = bf16[192,768]{1,0:T(8,128)(2,1)S(1)} collective-permute-done((bf16[192,768]{1,0:T(8,128)(2,1)S(1)}, bf16[192,768]{1,0:T(8,128)(2,1)S(1)}, u32[]{:S(2)}, u32[]{:S(2)}) %collective-permute-start.45) | collective-permute-done | bytes 294944 | tf_op jit(solution)/shard_map/ppermute | solution.py:578
  196.3 8.3 %collective-permute-done.43.refs_11_ = bf16[192,768]{1,0:T(8,128)(2,1)S(1)} collective-permute-done((bf16[192,768]{1,0:T(8,128)(2,1)S(1)}, bf16[192,768]{1,0:T(8,128)(2,1)S(1)}, u32[]{:S(2)}, u32[]{:S(2)}) %collective-permute-start.43) | collective-permute-done | bytes 294944 | tf_op jit(solution)/shard_map/ppermute | solution.py:578
  204.7 3.0 %collective-permute-start.50 = (bf16[192,768]{1,0:T(8,128)(2,1)S(1)}, bf16[192,768]{1,0:T(8,128)(2,1)S(1)}, u32[]{:S(2)}, u32[]{:S(2)}) collective-permute-start(bf16[192,768]{1,0:T(8,128)(2,1)S(1)} %add_convert_fusion.5.refs_8_), channel_id=1, source_target_pairs={{0,2},{1,3},{2,0},{3,1},{4,6},{5,7},{6,4},{7,5},{8,10},{9,11},{10,... | collective-permute-start | bytes 884744 | tf_op jit(solution)/shard_map/ppermute | solution.py:578
  213.7 5.7 %place_two.1 = (f32[768,1536]{1,0:T(8,128)}, f32[3,768,384]{2,1,0:T(8,128)}, f32[384,768]{1,0:T(8,128)}) custom-call(s32[3]{0:T(128)S(1)} %copy-done, bf16[192,768]{1,0:T(8,128)(2,1)S(1)} %add_convert_fusion.8.refs_0_, bf16[192,768]{1,0:T(8,128)(2,1)S(1)} %collective-permute-done.35.refs_1_, bf16[192,768]{1,0:T(8,128)(2,1)S(1)} %collective-permute-done.36.refs_2_, ...), custom_call_target="tpu_custom_call" | custom-call | flops 10000000 | bytes 8388608 | tf_op jit(solution)/shard_map/place_two/pallas_call | solution.py:834
  219.7 2.1 collective-permute-start.56
  223.5 2.2 collective-permute-done.60.refs_4_
  229.8 3.4 %place_down.1 = f32[1536,768]{1,0:T(8,128)} custom-call(s32[3]{0:T(128)S(1)} %copy-done, bf16[192,768]{1,0:T(8,128)(2,1)S(1)} %add_convert_fusion.3.refs_1_, bf16[192,768]{1,0:T(8,128)(2,1)S(1)} %collective-permute-done.54.refs_2_, bf16[192,768]{1,0:T(8,128)(2,1)S(1)} %collective-permute-done.55.refs_3_, ...), custom_call_target="tpu_custom_call" | custom-call | flops 1000000000 | bytes 8388608 | tf_op jit(solution)/shard_map/place_down/pallas_call | solution.py:857
  (234 shorter events, 72.3 us)
Async XLA Ops:
  14.6 17.1 %collective-permute-start = (bf16[384,768]{1,0:T(8,128)(2,1)S(1)}, bf16[384,768]{1,0:T(8,128)(2,1)}, u32[]{:S(2)}, u32[]{:S(2)}) collective-permute-start(bf16[384,768]{1,0:T(8,128)(2,1)S(1)} %pad_maximum_fusion), channel_id=1, source_target_pairs={{0,1},{1,0},{2,3},{3,2},{4,5},{5,4},{6,7},{7,6},{8,9},{9,8},{10,11... | collective-permute-start | bytes 1769480 | tf_op jit(solution)/shard_map/ppermute | solution.py:578
  14.7 16.0 %collective-permute-start.3 = (bf16[192,768]{1,0:T(8,128)(2,1)S(1)}, bf16[192,768]{1,0:T(8,128)(2,1)S(1)}, u32[]{:S(2)}, u32[]{:S(2)}) collective-permute-start(bf16[192,768]{1,0:T(8,128)(2,1)S(1)} %collective-permute-done.2.refs_0_), channel_id=1, source_target_pairs={{0,4},{1,5},{2,6},{3,7},{4,0},{5,1},{6,2},{7,3},{8,12},{9,13},{10,... | collective-permute-start | bytes 884744 | tf_op jit(solution)/shard_map/ppermute | solution.py:578
  16.1 14.7 %collective-permute-start.4 = (bf16[192,768]{1,0:T(8,128)(2,1)S(1)}, bf16[192,768]{1,0:T(8,128)(2,1)S(1)}, u32[]{:S(2)}, u32[]{:S(2)}) collective-permute-start(bf16[192,768]{1,0:T(8,128)(2,1)S(1)} %collective-permute-done.2.refs_0_), channel_id=1, source_target_pairs={{0,8},{1,9},{2,10},{3,11},{4,12},{5,13},{6,14},{7,15},{8,0},{9,1},... | collective-permute-start | bytes 884744 | tf_op jit(solution)/shard_map/ppermute | solution.py:578
  31.7 15.2 %collective-permute-start.10 = (bf16[384,768]{1,0:T(8,128)(2,1)}, bf16[384,768]{1,0:T(8,128)(2,1)S(1)}, u32[]{:S(2)}, u32[]{:S(2)}) collective-permute-start(bf16[384,768]{1,0:T(8,128)(2,1)} %collective-permute-done.r_6_), channel_id=1, source_target_pairs={{0,4},{1,5},{2,6},{3,7},{4,0},{5,1},{6,2},{7,3},{8,12},{9,13},{10,... | collective-permute-start | bytes 1769480 | tf_op jit(solution)/shard_map/ppermute | solution.py:578
  33.0 14.9 %collective-permute-start.11 = (bf16[384,768]{1,0:T(8,128)(2,1)}, bf16[384,768]{1,0:T(8,128)(2,1)}, u32[]{:S(2)}, u32[]{:S(2)}) collective-permute-start(bf16[384,768]{1,0:T(8,128)(2,1)} %collective-permute-done.r_6_), channel_id=1, source_target_pairs={{0,8},{1,9},{2,10},{3,11},{4,12},{5,13},{6,14},{7,15},{8,0},{9,1},... | collective-permute-start | bytes 1769480 | tf_op jit(solution)/shard_map/ppermute | solution.py:578
  34.3 16.5 %collective-permute-start.13 = (bf16[512,768]{1,0:T(8,128)(2,1)S(1)}, bf16[512,768]{1,0:T(8,128)(2,1)S(1)}, u32[]{:S(2)}, u32[]{:S(2)}) collective-permute-start(bf16[512,768]{1,0:T(8,128)(2,1)S(1)} %copy-done.4), channel_id=1, source_target_pairs={{0,2},{1,3},{2,0},{3,1},{4,6},{5,7},{6,4},{7,5},{8,10},{9,11},{10,... | collective-permute-start | bytes 2359304 | tf_op jit(solution)/shard_map/ppermute | solution.py:578
  49.1 20.7 %collective-permute-start.14 = (bf16[384,768]{1,0:T(8,128)(2,1)}, bf16[384,768]{1,0:T(8,128)(2,1)S(1)}, u32[]{:S(2)}, u32[]{:S(2)}) collective-permute-start(bf16[384,768]{1,0:T(8,128)(2,1)} %collective-permute-done.r_6_), channel_id=1, source_target_pairs={{0,12},{1,13},{2,14},{3,15},{4,8},{5,9},{6,10},{7,11},{8,4},{9,5},... | collective-permute-start | bytes 1769480 | tf_op jit(solution)/shard_map/ppermute | solution.py:578
  68.9 18.2 %collective-permute-start.15 = (bf16[384,768]{1,0:T(8,128)(2,1)}, bf16[384,768]{1,0:T(8,128)(2,1)S(1)}, u32[]{:S(2)}, u32[]{:S(2)}) collective-permute-start(bf16[384,768]{1,0:T(8,128)(2,1)} %get-tuple-element.187), channel_id=1, source_target_pairs={{0,4},{1,5},{2,6},{3,7},{4,0},{5,1},{6,2},{7,3},{8,12},{9,13},{10,... | collective-permute-start | bytes 1769480 | tf_op jit(solution)/shard_map/ppermute | solution.py:578
  87.8 18.2 %collective-permute-start.19 = (bf16[192,768]{1,0:T(8,128)(2,1)S(1)}, bf16[192,768]{1,0:T(8,128)(2,1)S(1)}, u32[]{:S(2)}, u32[]{:S(2)}) collective-permute-start(bf16[192,768]{1,0:T(8,128)(2,1)S(1)} %add_convert_fusion.15), channel_id=1, source_target_pairs={{0,8},{1,9},{2,10},{3,11},{4,12},{5,13},{6,14},{7,15},{8,0},{9,1},... | collective-permute-start | bytes 884744 | tf_op jit(solution)/shard_map/ppermute | solution.py:578
  88.7 17.4 %collective-permute-start.18 = (bf16[384,768]{1,0:T(8,128)(2,1)}, bf16[384,768]{1,0:T(8,128)(2,1)S(1)}, u32[]{:S(2)}, u32[]{:S(2)}) collective-permute-start(bf16[384,768]{1,0:T(8,128)(2,1)} %get-tuple-element.203), channel_id=1, source_target_pairs={{0,4},{1,5},{2,6},{3,7},{4,0},{5,1},{6,2},{7,3},{8,12},{9,13},{10,... | collective-permute-start | bytes 1769480 | tf_op jit(solution)/shard_map/ppermute | solution.py:578
  89.5 16.6 %collective-permute-start.20 = (bf16[384,768]{1,0:T(8,128)(2,1)}, bf16[384,768]{1,0:T(8,128)(2,1)S(1)}, u32[]{:S(2)}, u32[]{:S(2)}) collective-permute-start(bf16[384,768]{1,0:T(8,128)(2,1)} %get-tuple-element.208), channel_id=1, source_target_pairs={{0,1},{1,0},{2,3},{3,2},{4,5},{5,4},{6,7},{7,6},{8,9},{9,8},{10,11... | collective-permute-start | bytes 1769480 | tf_op jit(solution)/shard_map/ppermute | solution.py:578
  107.0 17.6 %collective-permute-start.24 = (bf16[384,768]{1,0:T(8,128)(2,1)}, bf16[384,768]{1,0:T(8,128)(2,1)}, u32[]{:S(2)}, u32[]{:S(2)}) collective-permute-start(bf16[384,768]{1,0:T(8,128)(2,1)} %get-tuple-element.217), channel_id=1, source_target_pairs={{0,1},{1,0},{2,3},{3,2},{4,5},{5,4},{6,7},{7,6},{8,9},{9,8},{10,11... | collective-permute-start | bytes 1769480 | tf_op jit(solution)/shard_map/ppermute | solution.py:578
  107.4 17.3 %collective-permute-start.21 = (bf16[192,768]{1,0:T(8,128)(2,1)S(1)}, bf16[192,768]{1,0:T(8,128)(2,1)}, u32[]{:S(2)}, u32[]{:S(2)}) collective-permute-start(bf16[192,768]{1,0:T(8,128)(2,1)S(1)} %add_convert_fusion.14), channel_id=1, source_target_pairs={{0,8},{1,9},{2,10},{3,11},{4,12},{5,13},{6,14},{7,15},{8,0},{9,1},... | collective-permute-start | bytes 884744 | tf_op jit(solution)/shard_map/ppermute | solution.py:578
  112.0 14.7 %collective-permute-start.23 = (bf16[384,768]{1,0:T(8,128)(2,1)S(1)}, bf16[384,768]{1,0:T(8,128)(2,1)}, u32[]{:S(2)}, u32[]{:S(2)}) collective-permute-start(bf16[384,768]{1,0:T(8,128)(2,1)S(1)} %add_convert_fusion.2), channel_id=1, source_target_pairs={{0,4},{1,5},{2,6},{3,7},{4,0},{5,1},{6,2},{7,3},{8,12},{9,13},{10,... | collective-permute-start | bytes 1769480 | tf_op jit(solution)/shard_map/ppermute | solution.py:578
  131.5 19.6 %collective-permute-start.27 = (bf16[384,768]{1,0:T(8,128)(2,1)}, bf16[384,768]{1,0:T(8,128)(2,1)}, u32[]{:S(2)}, u32[]{:S(2)}) collective-permute-start(bf16[384,768]{1,0:T(8,128)(2,1)} %add_convert_fusion.1), channel_id=1, source_target_pairs={{0,4},{1,5},{2,6},{3,7},{4,0},{5,1},{6,2},{7,3},{8,12},{9,13},{10,... | collective-permute-start | bytes 1769480 | tf_op jit(solution)/shard_map/ppermute | solution.py:578
  134.2 18.0 %collective-permute-start.30 = (bf16[192,768]{1,0:T(8,128)(2,1)}, bf16[192,768]{1,0:T(8,128)(2,1)}, u32[]{:S(2)}, u32[]{:S(2)}) collective-permute-start(bf16[192,768]{1,0:T(8,128)(2,1)} %add_convert_fusion.12), channel_id=1, source_target_pairs={{0,8},{1,9},{2,10},{3,11},{4,12},{5,13},{6,14},{7,15},{8,0},{9,1},... | collective-permute-start | bytes 884744 | tf_op jit(solution)/shard_map/ppermute | solution.py:578
  137.9 17.2 %collective-permute-start.34 = (bf16[192,768]{1,0:T(8,128)(2,1)S(1)}, bf16[192,768]{1,0:T(8,128)(2,1)S(1)}, u32[]{:S(2)}, u32[]{:S(2)}) collective-permute-start(bf16[192,768]{1,0:T(8,128)(2,1)S(1)} %add_convert_fusion.11), channel_id=1, source_target_pairs={{0,16},{1,17},{2,18},{3,19},{4,20},{5,21},{6,22},{7,23},{8,24},{9,... | collective-permute-start | bytes 884744 | tf_op jit(solution)/shard_map/ppermute | solution.py:578
  140.3 24.7 %collective-permute-start.26 = (bf16[384,768]{1,0:T(8,128)(2,1)S(1)}, bf16[384,768]{1,0:T(8,128)(2,1)}, u32[]{:S(2)}, u32[]{:S(2)}) collective-permute-start(bf16[384,768]{1,0:T(8,128)(2,1)S(1)} %add_convert_fusion), channel_id=1, source_target_pairs={{0,4},{1,5},{2,6},{3,7},{4,0},{5,1},{6,2},{7,3},{8,12},{9,13},{10,... | collective-permute-start | bytes 1769480 | tf_op jit(solution)/shard_map/ppermute | solution.py:578
  154.5 14.6 %collective-permute-start.17 = (bf16[512,768]{1,0:T(8,128)(2,1)S(1)}, bf16[512,768]{1,0:T(8,128)(2,1)}, u32[]{:S(2)}, u32[]{:S(2)}) collective-permute-start(bf16[512,768]{1,0:T(8,128)(2,1)S(1)} %copy-done.34), channel_id=1, source_target_pairs={{0,2},{1,3},{2,0},{3,1},{4,6},{5,7},{6,4},{7,5},{8,10},{9,11},{10,... | collective-permute-start | bytes 2359304 | tf_op jit(solution)/shard_map/ppermute | solution.py:578
  166.2 15.8 %collective-permute-start.38 = (bf16[192,768]{1,0:T(8,128)(2,1)S(1)}, bf16[192,768]{1,0:T(8,128)(2,1)S(1)}, u32[]{:S(2)}, u32[]{:S(2)}) collective-permute-start(bf16[192,768]{1,0:T(8,128)(2,1)S(1)} %add_convert_fusion.6), channel_id=1, source_target_pairs={{0,8},{1,9},{2,10},{3,11},{4,12},{5,13},{6,14},{7,15},{8,0},{9,1},... | collective-permute-start | bytes 884744 | tf_op jit(solution)/shard_map/ppermute | solution.py:578
  166.3 15.7 %collective-permute-start.39 = (bf16[192,768]{1,0:T(8,128)(2,1)S(1)}, bf16[192,768]{1,0:T(8,128)(2,1)S(1)}, u32[]{:S(2)}, u32[]{:S(2)}) collective-permute-start(bf16[192,768]{1,0:T(8,128)(2,1)S(1)} %add_convert_fusion.7), channel_id=1, source_target_pairs={{0,16},{1,17},{2,18},{3,19},{4,20},{5,21},{6,22},{7,23},{8,24},{9,... | collective-permute-start | bytes 884744 | tf_op jit(solution)/shard_map/ppermute | solution.py:578
  182.1 14.2 %collective-permute-start.41 = (bf16[192,768]{1,0:T(8,128)(2,1)S(1)}, bf16[192,768]{1,0:T(8,128)(2,1)S(1)}, u32[]{:S(2)}, u32[]{:S(2)}) collective-permute-start(bf16[192,768]{1,0:T(8,128)(2,1)S(1)} %add_convert_fusion.5.refs_8_), channel_id=1, source_target_pairs={{0,4},{1,5},{2,6},{3,7},{4,0},{5,1},{6,2},{7,3},{8,12},{9,13},{10,... | collective-permute-start | bytes 884744 | tf_op jit(solution)/shard_map/ppermute | solution.py:578
  187.0 17.6 %collective-permute-start.43 = (bf16[192,768]{1,0:T(8,128)(2,1)S(1)}, bf16[192,768]{1,0:T(8,128)(2,1)S(1)}, u32[]{:S(2)}, u32[]{:S(2)}) collective-permute-start(bf16[192,768]{1,0:T(8,128)(2,1)S(1)} %add_convert_fusion.5.refs_8_), channel_id=1, source_target_pairs={{0,12},{1,13},{2,14},{3,15},{4,8},{5,9},{6,10},{7,11},{8,4},{9,5},... | collective-permute-start | bytes 884744 | tf_op jit(solution)/shard_map/ppermute | solution.py:578
  188.1 16.5 %collective-permute-start.44 = (bf16[192,768]{1,0:T(8,128)(2,1)S(1)}, bf16[192,768]{1,0:T(8,128)(2,1)S(1)}, u32[]{:S(2)}, u32[]{:S(2)}) collective-permute-start(bf16[192,768]{1,0:T(8,128)(2,1)S(1)} %collective-permute-done.36.refs_2_), channel_id=1, source_target_pairs={{0,4},{1,5},{2,6},{3,7},{4,0},{5,1},{6,2},{7,3},{8,12},{9,13},{10,... | collective-permute-start | bytes 884744 | tf_op jit(solution)/shard_map/ppermute | solution.py:578
  (78 other events, 512.4 us)

commit v3 on v2

--- a/solution.py
+++ b/solution.py
@@ -557,7 +557,7 @@
     return [pltpu.VMEM(shape, dtype) for shape, dtype in buffers] + [pltpu.SemaphoreType.DMA((sems,))]
 
 
-def call(kernel, outs, in_specs, name, scratch=(), out_specs=None, limit=60, gflop=1.0):
+def call(kernel, outs, in_specs, name, scratch=(), out_specs=None, limit=61, gflop=1.0):
     return pl.pallas_call(
         kernel,
         out_shape=tuple(jax.ShapeDtypeStruct(shape, dtype) for shape, dtype in outs),

time: 234 us -> 234 us (level)
    ppermute x62, starting transfers between devices: 56.9 us -> 54.6 us  [swap(): lax.ppermute(value, ('dp', 'tp'), [(i, i ^ mask) for i in range(devices)])]
    unnamed x78 -> x76, local copies, waits for them, and re-layouts: 4.96 us -> 3.72 us
  transfers between devices with their start and end apart: 62 -> 62, of which waited for: 16 -> 16; matrix products, arithmetic and copies ran while one was open for 7% -> 8% of each run, Pallas kernels for 41% -> 41%
where the time goes in v3:
time: 234 us; the launch traced here: 233 us
  Pallas kernels  98.3 us (42%)
  waiting for transfers between devices  54.8 us (23%)
  starting transfers between devices  54.6 us (23%)
  other arithmetic  14.2 us (6%)
  local copies, waits for them, and re-layouts  9.4 us (4%)
    ppermute x62, waiting for transfers between devices, swap(): lax.ppermute(value, ('dp', 'tp'), [(i, i ^ mask) for i in range(devices)])  54.8 us
    ppermute x62, starting transfers between devices, swap(): lax.ppermute(value, ('dp', 'tp'), [(i, i ^ mask) for i in range(devices)])  54.6 us
    pallas_call x1, Pallas kernels, on_device(): call(lambda *r: mlp_kernel(False, *r), [(one, F32), (one, BF16), (one, F3...  16.4 us
    pallas_call x1, Pallas kernels, on_device(): call(lambda *r: mlp_kernel(True, *r), [(both, BF16), (both, BF16), *[(pai...  16.3 us
    pallas_call x1, Pallas kernels, on_device(): call(other_back_kernel, [(one, F32), (acts, BF16), (grad_units, BF16), (g...  14.4 us
    convert_element_type x16, other arithmetic, total(): add(*[cut(term, part) for term, part in zip(turn(*terms), parts)])  13.5 us
    pallas_call x1, Pallas kernels, on_device(): call(own_back_kernel, [(acts, BF16), (grad_units, BF16), (grad_units, BF1...  11.9 us
    pallas_call x1, Pallas kernels, on_device(): call(other_fwd_kernel, [(acts, BF16), (head, BF16), (one, F32), (one, BF1...  10.3 us
  transfers between devices with their start and end apart: 62, of which 16 were waited for; matrix products, arithmetic and copies ran while one was open for 8% of the time, Pallas kernels for 41%

profile of v3, /device:TPU:1, one launch (start us, length us, event | category | flops | bytes accessed | tf_op | source)
XLA Modules:
  0.0 232.8 jit_solution(4732142846837032832)
XLA Ops:
  2.7 2.1 collective-permute-start.2
  6.3 7.1 %attn_own_fwd.1 = (bf16[512,768]{1,0:T(8,128)(2,1)}, bf16[512,1152]{1,0:T(8,128)(2,1)}, bf16[512,384]{1,0:T(8,128)(2,1)}) custom-call(s32[8,17]{1,0:T(8,128)} %lens.7, s32[3]{0:T(128)} %pad_add_fusion.ids.r_0_.refs_0_, bf16[512,768]{1,0:T(8,128)(2,1)} %x_hbm.5, f32[8,768]{1,0:T(8,128)} %stack.48.vecs.r_5_, bf16[3,768,384]{2,1,0:T(8,128)(2,1)} %bitcast.13, ...), custom_call_target="tpu_custom_call" | custom-call | flops 500000000 | bytes 8388608 | tf_op jit(solution)/shard_map/attn_own_fwd/pallas_call | solution.py:638
  18.8 10.0 %collective-permute-done.1.bias.r_5_ = f32[3,768]{1,0:T(4,128)S(1)} collective-permute-done((f32[3,768]{1,0:T(4,128)S(1)}, f32[3,768]{1,0:T(4,128)S(1)}, u32[]{:S(2)}, u32[]{:S(2)}) %collective-permute-start.1) | collective-permute-done | bytes 9248 | tf_op jit(solution)/shard_map/ppermute | solution.py:578
  35.8 10.3 %attn_other_fwd.1 = (bf16[512,1152]{1,0:T(8,128)(2,1)}, bf16[512,384]{1,0:T(8,128)(2,1)}, f32[512,768]{1,0:T(8,128)}, bf16[512,768]{1,0:T(8,128)(2,1)}) custom-call(s32[8,17]{1,0:T(8,128)} %lens.7, s32[3]{0:T(128)} %pad_add_fusion.ids.r_0_.refs_0_, bf16[512,768]{1,0:T(8,128)(2,1)} %x_hbm.5, bf16[512,768]{1,0:T(8,128)(2,1)} %get-tuple-element.175.nrm_hbm, ...), custom_call_target="tpu_custom_call" | custom-call | flops 6000000000 | bytes 8388608 | tf_op jit(solution)/shard_map/attn_other_fwd/pallas_call | solution.py:661
  52.1 16.3 %mlp_own.1 = (bf16[1024,768]{1,0:T(8,128)(2,1)}, bf16[1024,768]{1,0:T(8,128)(2,1)}, bf16[384,768]{1,0:T(8,128)(2,1)}, bf16[384,768]{1,0:T(8,128)(2,1)}, bf16[384...) custom-call(s32[3]{0:T(128)} %pad_add_fusion.ids.r_0_.refs_0_, ...), custom_call_target="tpu_custom_call" | custom-call | flops 1000000000 | bytes 8388608 | tf_op jit(solution)/shard_map/mlp_own/pallas_call | solution.py:693
  69.8 16.4 %mlp_other.1 = (f32[512,768]{1,0:T(8,128)}, bf16[512,768]{1,0:T(8,128)(2,1)}, f32[512,768]{1,0:T(8,128)}, bf16[512,768]{1,0:T(8,128)(2,1)}, bf16[384,768]{1,0:T(...) custom-call(s32[3]{0:T(128)} %pad_add_fusion.ids.r_0_.refs_0_, ...), custom_call_target="tpu_custom_call" | custom-call | flops 12000000000 | bytes 8388608 | tf_op jit(solution)/shard_map/mlp_other/pallas_call | solution.py:702
  90.7 14.4 %attn_other_back.1 = (f32[512,768]{1,0:T(8,128)}, bf16[512,1152]{1,0:T(8,128)(2,1)}, bf16[768,768]{1,0:T(8,128)(2,1)}, bf16[768,768]{1,0:T(8,128)(2,1)}, f32[8,768]{1,0:T(8,128)}) custom-call(s32[8,17]{1,0:T(8,128)} %lens.7, s32[3]{0:T(128)} %pad_add_fusion.ids.r_0_.refs_0_, f32[512,768]{1,0:T(8,128)} %get-tuple-element.195.dnm_own_hbm, ...), custom_call_target="tpu_custom_call" | custom-call | flops 10000000000 | bytes 8388608 | tf_op jit(solution)/shard_map/attn_other_back/pallas_call | solution.py:725
  111.4 11.9 %attn_own_back.1 = (bf16[512,1152]{1,0:T(8,128)(2,1)}, bf16[768,768]{1,0:T(8,128)(2,1)}, bf16[768,768]{1,0:T(8,128)(2,1)}) custom-call(s32[8,17]{1,0:T(8,128)} %lens.7, s32[3]{0:T(128)} %pad_add_fusion.ids.r_0_.refs_0_, f32[512,768]{1,0:T(8,128)} %get-tuple-element.246.mg_hbm, bf16[384,768]{1,0:T(8,128)(2,1)} %wo_hbm.1, ...), custom_call_target="tpu_custom_call" | custom-call | flops 10000000000 | bytes 8388608 | tf_op jit(solution)/shard_map/attn_own_back/pallas_call | solution.py:749
  123.3 2.5 %collective-permute-done.23 = bf16[384,768]{1,0:T(8,128)(2,1)} collective-permute-done((bf16[384,768]{1,0:T(8,128)(2,1)S(1)}, bf16[384,768]{1,0:T(8,128)(2,1)}, u32[]{:S(2)}, u32[]{:S(2)}) %collective-permute-start.23) | collective-permute-done | bytes 589856 | tf_op jit(solution)/shard_map/ppermute | solution.py:578
  134.9 2.0 collective-permute-done.28
  137.1 2.4 %collective-permute-start.34 = (bf16[192,768]{1,0:T(8,128)(2,1)S(1)}, bf16[192,768]{1,0:T(8,128)(2,1)S(1)}, u32[]{:S(2)}, u32[]{:S(2)}) collective-permute-start(bf16[192,768]{1,0:T(8,128)(2,1)S(1)} %add_convert_fusion.11), channel_id=1, source_target_pairs={{0,16},{1,17},{2,18},{3,19},{4,20},{5,21},{6,22},{7,23},{8,24},{9,... | collective-permute-start | bytes 884744 | tf_op jit(solution)/shard_map/ppermute | solution.py:578
  139.8 8.8 %input_grad.1 = (bf16[512,768]{1,0:T(8,128)(2,1)}, f32[16,768]{1,0:T(8,128)}) custom-call(s32[3]{0:T(128)} %pad_add_fusion.ids.r_0_.refs_0_, bf16[512,1152]{1,0:T(8,128)(2,1)} %get-tuple-element.222.dqkv_a_hbm, bf16[512,1152]{1,0:T(8,128)(2,1)} %get-tuple-element.240.dqkv_b_hbm, f32[512,768]{1,0:T(8,128)} %get-tuple-element.246.mg_hbm, ...), custom_call_target="tpu_custom_call" | custom-call | flops 10000000 | bytes 8388608 | tf_op jit(solution)/shard_map/input_grad/pallas_call | solution.py:770
  154.6 6.2 %collective-permute-done.33 = f32[16,768]{1,0:T(8,128)S(1)} collective-permute-done((f32[16,768]{1,0:T(8,128)S(1)}, f32[16,768]{1,0:T(8,128)S(1)}, u32[]{:S(2)}, u32[]{:S(2)}) %collective-permute-start.33) | collective-permute-done | bytes 49184 | tf_op jit(solution)/shard_map/ppermute | solution.py:578
  165.8 2.8 %collective-permute-start.39 = (bf16[192,768]{1,0:T(8,128)(2,1)S(1)}, bf16[192,768]{1,0:T(8,128)(2,1)S(1)}, u32[]{:S(2)}, u32[]{:S(2)}) collective-permute-start(bf16[192,768]{1,0:T(8,128)(2,1)S(1)} %add_convert_fusion.7), channel_id=1, source_target_pairs={{0,16},{1,17},{2,18},{3,19},{4,20},{5,21},{6,22},{7,23},{8,24},{9,... | collective-permute-start | bytes 884744 | tf_op jit(solution)/shard_map/ppermute | solution.py:578
  169.2 4.0 %layer_out.1 = bf16[512,768]{1,0:T(8,128)(2,1)} custom-call(f32[512,768]{1,0:T(8,128)} %get-tuple-element.179.mid_hbm, f32[512,768]{1,0:T(8,128)} %get-tuple-element.186.own_hbm, bf16[512,768]{1,0:T(8,128)(2,1)} %collective-permute-done.17.sib_hbm, f32[8,768]{1,0:T(8,128)} %stack.48.vecs.r_5_), custom_call_target="tpu_custom_call" | custom-call | flops 10000000 | bytes 8388608 | tf_op jit(solution)/shard_map/layer_out/pallas_call | solution.py:811
  173.2 8.3 %collective-permute-done.38 = bf16[192,768]{1,0:T(8,128)(2,1)S(1)} collective-permute-done((bf16[192,768]{1,0:T(8,128)(2,1)S(1)}, bf16[192,768]{1,0:T(8,128)(2,1)S(1)}, u32[]{:S(2)}, u32[]{:S(2)}) %collective-permute-start.38) | collective-permute-done | bytes 294944 | tf_op jit(solution)/shard_map/ppermute | solution.py:578
  183.4 2.0 collective-permute-start.45
  188.1 7.5 %collective-permute-done.45 = bf16[192,768]{1,0:T(8,128)(2,1)S(1)} collective-permute-done((bf16[192,768]{1,0:T(8,128)(2,1)S(1)}, bf16[192,768]{1,0:T(8,128)(2,1)S(1)}, u32[]{:S(2)}, u32[]{:S(2)}) %collective-permute-start.45) | collective-permute-done | bytes 294944 | tf_op jit(solution)/shard_map/ppermute | solution.py:578
  195.6 8.9 %collective-permute-done.43.refs_11_ = bf16[192,768]{1,0:T(8,128)(2,1)S(1)} collective-permute-done((bf16[192,768]{1,0:T(8,128)(2,1)S(1)}, bf16[192,768]{1,0:T(8,128)(2,1)S(1)}, u32[]{:S(2)}, u32[]{:S(2)}) %collective-permute-start.43) | collective-permute-done | bytes 294944 | tf_op jit(solution)/shard_map/ppermute | solution.py:578
  204.5 2.7 %collective-permute-start.50 = (bf16[192,768]{1,0:T(8,128)(2,1)S(1)}, bf16[192,768]{1,0:T(8,128)(2,1)S(1)}, u32[]{:S(2)}, u32[]{:S(2)}) collective-permute-start(bf16[192,768]{1,0:T(8,128)(2,1)S(1)} %add_convert_fusion.5.refs_8_), channel_id=1, source_target_pairs={{0,2},{1,3},{2,0},{3,1},{4,6},{5,7},{6,4},{7,5},{8,10},{9,11},{10,... | collective-permute-start | bytes 884744 | tf_op jit(solution)/shard_map/ppermute | solution.py:578
  212.9 5.7 %place_two.1 = (f32[768,1536]{1,0:T(8,128)}, f32[3,768,384]{2,1,0:T(8,128)}, f32[384,768]{1,0:T(8,128)}) custom-call(s32[3]{0:T(128)S(1)} %copy-done, bf16[192,768]{1,0:T(8,128)(2,1)S(1)} %add_convert_fusion.8.refs_0_, bf16[192,768]{1,0:T(8,128)(2,1)S(1)} %collective-permute-done.35.refs_1_, bf16[192,768]{1,0:T(8,128)(2,1)S(1)} %collective-permute-done.36.refs_2_, ...), custom_call_target="tpu_custom_call" | custom-call | flops 10000000 | bytes 8388608 | tf_op jit(solution)/shard_map/place_two/pallas_call | solution.py:834
  219.2 2.1 collective-permute-start.56
  222.7 2.5 %collective-permute-done.60.refs_4_ = bf16[192,768]{1,0:T(8,128)(2,1)S(1)} collective-permute-done((bf16[192,768]{1,0:T(8,128)(2,1)S(1)}, bf16[192,768]{1,0:T(8,128)(2,1)S(1)}, u32[]{:S(2)}, u32[]{:S(2)}) %collective-permute-start.60) | collective-permute-done | bytes 294944 | tf_op jit(solution)/shard_map/ppermute | solution.py:578
  229.2 3.4 %place_down.1 = f32[1536,768]{1,0:T(8,128)} custom-call(s32[3]{0:T(128)S(1)} %copy-done, bf16[192,768]{1,0:T(8,128)(2,1)S(1)} %add_convert_fusion.3.refs_1_, bf16[192,768]{1,0:T(8,128)(2,1)S(1)} %collective-permute-done.54.refs_2_, bf16[192,768]{1,0:T(8,128)(2,1)S(1)} %collective-permute-done.55.refs_3_, ...), custom_call_target="tpu_custom_call" | custom-call | flops 1000000000 | bytes 8388608 | tf_op jit(solution)/shard_map/place_down/pallas_call | solution.py:857
  (232 shorter events, 70.9 us)
Async XLA Ops:
  14.6 17.1 %collective-permute-start = (bf16[384,768]{1,0:T(8,128)(2,1)S(1)}, bf16[384,768]{1,0:T(8,128)(2,1)}, u32[]{:S(2)}, u32[]{:S(2)}) collective-permute-start(bf16[384,768]{1,0:T(8,128)(2,1)S(1)} %pad_maximum_fusion), channel_id=1, source_target_pairs={{0,1},{1,0},{2,3},{3,2},{4,5},{5,4},{6,7},{7,6},{8,9},{9,8},{10,11... | collective-permute-start | bytes 1769480 | tf_op jit(solution)/shard_map/ppermute | solution.py:578
  14.7 16.0 %collective-permute-start.3 = (bf16[192,768]{1,0:T(8,128)(2,1)S(1)}, bf16[192,768]{1,0:T(8,128)(2,1)S(1)}, u32[]{:S(2)}, u32[]{:S(2)}) collective-permute-start(bf16[192,768]{1,0:T(8,128)(2,1)S(1)} %collective-permute-done.2.refs_0_), channel_id=1, source_target_pairs={{0,4},{1,5},{2,6},{3,7},{4,0},{5,1},{6,2},{7,3},{8,12},{9,13},{10,... | collective-permute-start | bytes 884744 | tf_op jit(solution)/shard_map/ppermute | solution.py:578
  16.1 14.7 %collective-permute-start.4 = (bf16[192,768]{1,0:T(8,128)(2,1)S(1)}, bf16[192,768]{1,0:T(8,128)(2,1)S(1)}, u32[]{:S(2)}, u32[]{:S(2)}) collective-permute-start(bf16[192,768]{1,0:T(8,128)(2,1)S(1)} %collective-permute-done.2.refs_0_), channel_id=1, source_target_pairs={{0,8},{1,9},{2,10},{3,11},{4,12},{5,13},{6,14},{7,15},{8,0},{9,1},... | collective-permute-start | bytes 884744 | tf_op jit(solution)/shard_map/ppermute | solution.py:578
  31.7 15.2 %collective-permute-start.10 = (bf16[384,768]{1,0:T(8,128)(2,1)}, bf16[384,768]{1,0:T(8,128)(2,1)}, u32[]{:S(2)}, u32[]{:S(2)}) collective-permute-start(bf16[384,768]{1,0:T(8,128)(2,1)} %collective-permute-done.r_6_), channel_id=1, source_target_pairs={{0,4},{1,5},{2,6},{3,7},{4,0},{5,1},{6,2},{7,3},{8,12},{9,13},{10,... | collective-permute-start | bytes 1769480 | tf_op jit(solution)/shard_map/ppermute | solution.py:578
  33.0 14.9 %collective-permute-start.11 = (bf16[384,768]{1,0:T(8,128)(2,1)}, bf16[384,768]{1,0:T(8,128)(2,1)}, u32[]{:S(2)}, u32[]{:S(2)}) collective-permute-start(bf16[384,768]{1,0:T(8,128)(2,1)} %collective-permute-done.r_6_), channel_id=1, source_target_pairs={{0,8},{1,9},{2,10},{3,11},{4,12},{5,13},{6,14},{7,15},{8,0},{9,1},... | collective-permute-start | bytes 1769480 | tf_op jit(solution)/shard_map/ppermute | solution.py:578
  34.3 16.0 %collective-permute-start.13 = (bf16[512,768]{1,0:T(8,128)(2,1)S(1)}, bf16[512,768]{1,0:T(8,128)(2,1)S(1)}, u32[]{:S(2)}, u32[]{:S(2)}) collective-permute-start(bf16[512,768]{1,0:T(8,128)(2,1)S(1)} %copy-done.4), channel_id=1, source_target_pairs={{0,2},{1,3},{2,0},{3,1},{4,6},{5,7},{6,4},{7,5},{8,10},{9,11},{10,... | collective-permute-start | bytes 2359304 | tf_op jit(solution)/shard_map/ppermute | solution.py:578
  49.1 20.7 %collective-permute-start.14 = (bf16[384,768]{1,0:T(8,128)(2,1)}, bf16[384,768]{1,0:T(8,128)(2,1)}, u32[]{:S(2)}, u32[]{:S(2)}) collective-permute-start(bf16[384,768]{1,0:T(8,128)(2,1)} %collective-permute-done.r_6_), channel_id=1, source_target_pairs={{0,12},{1,13},{2,14},{3,15},{4,8},{5,9},{6,10},{7,11},{8,4},{9,5},... | collective-permute-start | bytes 1769480 | tf_op jit(solution)/shard_map/ppermute | solution.py:578
  68.5 17.7 %collective-permute-start.15 = (bf16[384,768]{1,0:T(8,128)(2,1)}, bf16[384,768]{1,0:T(8,128)(2,1)S(1)}, u32[]{:S(2)}, u32[]{:S(2)}) collective-permute-start(bf16[384,768]{1,0:T(8,128)(2,1)} %get-tuple-element.187), channel_id=1, source_target_pairs={{0,4},{1,5},{2,6},{3,7},{4,0},{5,1},{6,2},{7,3},{8,12},{9,13},{10,... | collective-permute-start | bytes 1769480 | tf_op jit(solution)/shard_map/ppermute | solution.py:578
  86.9 18.2 %collective-permute-start.19 = (bf16[192,768]{1,0:T(8,128)(2,1)S(1)}, bf16[192,768]{1,0:T(8,128)(2,1)S(1)}, u32[]{:S(2)}, u32[]{:S(2)}) collective-permute-start(bf16[192,768]{1,0:T(8,128)(2,1)S(1)} %add_convert_fusion.15), channel_id=1, source_target_pairs={{0,8},{1,9},{2,10},{3,11},{4,12},{5,13},{6,14},{7,15},{8,0},{9,1},... | collective-permute-start | bytes 884744 | tf_op jit(solution)/shard_map/ppermute | solution.py:578
  87.4 17.8 %collective-permute-start.18 = (bf16[384,768]{1,0:T(8,128)(2,1)}, bf16[384,768]{1,0:T(8,128)(2,1)S(1)}, u32[]{:S(2)}, u32[]{:S(2)}) collective-permute-start(bf16[384,768]{1,0:T(8,128)(2,1)} %get-tuple-element.203), channel_id=1, source_target_pairs={{0,4},{1,5},{2,6},{3,7},{4,0},{5,1},{6,2},{7,3},{8,12},{9,13},{10,... | collective-permute-start | bytes 1769480 | tf_op jit(solution)/shard_map/ppermute | solution.py:578
  88.6 16.6 %collective-permute-start.20 = (bf16[384,768]{1,0:T(8,128)(2,1)}, bf16[384,768]{1,0:T(8,128)(2,1)S(1)}, u32[]{:S(2)}, u32[]{:S(2)}) collective-permute-start(bf16[384,768]{1,0:T(8,128)(2,1)} %get-tuple-element.208), channel_id=1, source_target_pairs={{0,1},{1,0},{2,3},{3,2},{4,5},{5,4},{6,7},{7,6},{8,9},{9,8},{10,11... | collective-permute-start | bytes 1769480 | tf_op jit(solution)/shard_map/ppermute | solution.py:578
  106.2 17.1 %collective-permute-start.24 = (bf16[384,768]{1,0:T(8,128)(2,1)}, bf16[384,768]{1,0:T(8,128)(2,1)}, u32[]{:S(2)}, u32[]{:S(2)}) collective-permute-start(bf16[384,768]{1,0:T(8,128)(2,1)} %get-tuple-element.217), channel_id=1, source_target_pairs={{0,1},{1,0},{2,3},{3,2},{4,5},{5,4},{6,7},{7,6},{8,9},{9,8},{10,11... | collective-permute-start | bytes 1769480 | tf_op jit(solution)/shard_map/ppermute | solution.py:578
  107.2 16.1 %collective-permute-start.21 = (bf16[192,768]{1,0:T(8,128)(2,1)}, bf16[192,768]{1,0:T(8,128)(2,1)}, u32[]{:S(2)}, u32[]{:S(2)}) collective-permute-start(bf16[192,768]{1,0:T(8,128)(2,1)} %add_convert_fusion.14), channel_id=1, source_target_pairs={{0,8},{1,9},{2,10},{3,11},{4,12},{5,13},{6,14},{7,15},{8,0},{9,1},... | collective-permute-start | bytes 884744 | tf_op jit(solution)/shard_map/ppermute | solution.py:578
  111.1 14.7 %collective-permute-start.23 = (bf16[384,768]{1,0:T(8,128)(2,1)S(1)}, bf16[384,768]{1,0:T(8,128)(2,1)}, u32[]{:S(2)}, u32[]{:S(2)}) collective-permute-start(bf16[384,768]{1,0:T(8,128)(2,1)S(1)} %add_convert_fusion.2), channel_id=1, source_target_pairs={{0,4},{1,5},{2,6},{3,7},{4,0},{5,1},{6,2},{7,3},{8,12},{9,13},{10,... | collective-permute-start | bytes 1769480 | tf_op jit(solution)/shard_map/ppermute | solution.py:578
  130.7 19.2 %collective-permute-start.27 = (bf16[384,768]{1,0:T(8,128)(2,1)}, bf16[384,768]{1,0:T(8,128)(2,1)}, u32[]{:S(2)}, u32[]{:S(2)}) collective-permute-start(bf16[384,768]{1,0:T(8,128)(2,1)} %add_convert_fusion.1), channel_id=1, source_target_pairs={{0,4},{1,5},{2,6},{3,7},{4,0},{5,1},{6,2},{7,3},{8,12},{9,13},{10,... | collective-permute-start | bytes 1769480 | tf_op jit(solution)/shard_map/ppermute | solution.py:578
  132.9 18.1 %collective-permute-start.30 = (bf16[192,768]{1,0:T(8,128)(2,1)}, bf16[192,768]{1,0:T(8,128)(2,1)}, u32[]{:S(2)}, u32[]{:S(2)}) collective-permute-start(bf16[192,768]{1,0:T(8,128)(2,1)} %add_convert_fusion.12), channel_id=1, source_target_pairs={{0,8},{1,9},{2,10},{3,11},{4,12},{5,13},{6,14},{7,15},{8,0},{9,1},... | collective-permute-start | bytes 884744 | tf_op jit(solution)/shard_map/ppermute | solution.py:578
  137.1 17.2 %collective-permute-start.34 = (bf16[192,768]{1,0:T(8,128)(2,1)S(1)}, bf16[192,768]{1,0:T(8,128)(2,1)S(1)}, u32[]{:S(2)}, u32[]{:S(2)}) collective-permute-start(bf16[192,768]{1,0:T(8,128)(2,1)S(1)} %add_convert_fusion.11), channel_id=1, source_target_pairs={{0,16},{1,17},{2,18},{3,19},{4,20},{5,21},{6,22},{7,23},{8,24},{9,... | collective-permute-start | bytes 884744 | tf_op jit(solution)/shard_map/ppermute | solution.py:578
  139.5 24.7 %collective-permute-start.26 = (bf16[384,768]{1,0:T(8,128)(2,1)}, bf16[384,768]{1,0:T(8,128)(2,1)}, u32[]{:S(2)}, u32[]{:S(2)}) collective-permute-start(bf16[384,768]{1,0:T(8,128)(2,1)} %add_convert_fusion), channel_id=1, source_target_pairs={{0,4},{1,5},{2,6},{3,7},{4,0},{5,1},{6,2},{7,3},{8,12},{9,13},{10,... | collective-permute-start | bytes 1769480 | tf_op jit(solution)/shard_map/ppermute | solution.py:578
  153.7 14.9 %collective-permute-start.17 = (bf16[512,768]{1,0:T(8,128)(2,1)S(1)}, bf16[512,768]{1,0:T(8,128)(2,1)}, u32[]{:S(2)}, u32[]{:S(2)}) collective-permute-start(bf16[512,768]{1,0:T(8,128)(2,1)S(1)} %copy-done.35), channel_id=1, source_target_pairs={{0,2},{1,3},{2,0},{3,1},{4,6},{5,7},{6,4},{7,5},{8,10},{9,11},{10,... | collective-permute-start | bytes 2359304 | tf_op jit(solution)/shard_map/ppermute | solution.py:578
  165.4 16.1 %collective-permute-start.38 = (bf16[192,768]{1,0:T(8,128)(2,1)S(1)}, bf16[192,768]{1,0:T(8,128)(2,1)S(1)}, u32[]{:S(2)}, u32[]{:S(2)}) collective-permute-start(bf16[192,768]{1,0:T(8,128)(2,1)S(1)} %add_convert_fusion.6), channel_id=1, source_target_pairs={{0,8},{1,9},{2,10},{3,11},{4,12},{5,13},{6,14},{7,15},{8,0},{9,1},... | collective-permute-start | bytes 884744 | tf_op jit(solution)/shard_map/ppermute | solution.py:578
  165.8 15.7 %collective-permute-start.39 = (bf16[192,768]{1,0:T(8,128)(2,1)S(1)}, bf16[192,768]{1,0:T(8,128)(2,1)S(1)}, u32[]{:S(2)}, u32[]{:S(2)}) collective-permute-start(bf16[192,768]{1,0:T(8,128)(2,1)S(1)} %add_convert_fusion.7), channel_id=1, source_target_pairs={{0,16},{1,17},{2,18},{3,19},{4,20},{5,21},{6,22},{7,23},{8,24},{9,... | collective-permute-start | bytes 884744 | tf_op jit(solution)/shard_map/ppermute | solution.py:578
  181.6 13.9 %collective-permute-start.41 = (bf16[192,768]{1,0:T(8,128)(2,1)S(1)}, bf16[192,768]{1,0:T(8,128)(2,1)S(1)}, u32[]{:S(2)}, u32[]{:S(2)}) collective-permute-start(bf16[192,768]{1,0:T(8,128)(2,1)S(1)} %add_convert_fusion.5.refs_8_), channel_id=1, source_target_pairs={{0,4},{1,5},{2,6},{3,7},{4,0},{5,1},{6,2},{7,3},{8,12},{9,13},{10,... | collective-permute-start | bytes 884744 | tf_op jit(solution)/shard_map/ppermute | solution.py:578
  186.3 18.2 %collective-permute-start.43 = (bf16[192,768]{1,0:T(8,128)(2,1)S(1)}, bf16[192,768]{1,0:T(8,128)(2,1)S(1)}, u32[]{:S(2)}, u32[]{:S(2)}) collective-permute-start(bf16[192,768]{1,0:T(8,128)(2,1)S(1)} %add_convert_fusion.5.refs_8_), channel_id=1, source_target_pairs={{0,12},{1,13},{2,14},{3,15},{4,8},{5,9},{6,10},{7,11},{8,4},{9,5},... | collective-permute-start | bytes 884744 | tf_op jit(solution)/shard_map/ppermute | solution.py:578
  187.4 17.1 %collective-permute-start.44 = (bf16[192,768]{1,0:T(8,128)(2,1)S(1)}, bf16[192,768]{1,0:T(8,128)(2,1)S(1)}, u32[]{:S(2)}, u32[]{:S(2)}) collective-permute-start(bf16[192,768]{1,0:T(8,128)(2,1)S(1)} %collective-permute-done.36.refs_2_), channel_id=1, source_target_pairs={{0,4},{1,5},{2,6},{3,7},{4,0},{5,1},{6,2},{7,3},{8,12},{9,13},{10,... | collective-permute-start | bytes 884744 | tf_op jit(solution)/shard_map/ppermute | solution.py:578
  (77 other events, 516.8 us)

commit v4 on v3

--- a/solution.py
+++ b/solution.py
@@ -221,7 +221,7 @@
 
 
 def gelu_parts(pre):
-    bell = jnp.exp(-0.5 * pre * pre)
+    bell = jnp.exp2(pre * pre * (-0.5 * math.log2(math.e)))
     t = 1.0 / (1.0 + (0.3275911 * math.sqrt(0.5)) * jnp.abs(pre))
     poly = 0.5307027145 * t - 0.7265760135
     poly = poly * t + 0.7107068705

time: 234 us -> 233 us (level)
  no operation moved by 1% of the time
where the time goes in v4:
time: 233 us
  Pallas kernels  98.1 us (42%)
  waiting for transfers between devices  54.8 us (24%)
  starting transfers between devices  54.6 us (23%)
  other arithmetic  14.2 us (6%)
  local copies, waits for them, and re-layouts  9.4 us (4%)
    ppermute x62, waiting for transfers between devices, swap(): lax.ppermute(value, ('dp', 'tp'), [(i, i ^ mask) for i in range(devices)])  54.8 us
    ppermute x62, starting transfers between devices, swap(): lax.ppermute(value, ('dp', 'tp'), [(i, i ^ mask) for i in range(devices)])  54.6 us
    pallas_call x1, Pallas kernels, on_device(): call(lambda *r: mlp_kernel(False, *r), [(one, F32), (one, BF16), (one, F3...  16.3 us
    pallas_call x1, Pallas kernels, on_device(): call(lambda *r: mlp_kernel(True, *r), [(both, BF16), (both, BF16), *[(pai...  16.2 us
    pallas_call x1, Pallas kernels, on_device(): call(other_back_kernel, [(one, F32), (acts, BF16), (grad_units, BF16), (g...  14.4 us
    convert_element_type x16, other arithmetic, total(): add(*[cut(term, part) for term, part in zip(turn(*terms), parts)])  13.5 us
    pallas_call x1, Pallas kernels, on_device(): call(own_back_kernel, [(acts, BF16), (grad_units, BF16), (grad_units, BF1...  11.9 us
    pallas_call x1, Pallas kernels, on_device(): call(other_fwd_kernel, [(acts, BF16), (head, BF16), (one, F32), (one, BF1...  10.3 us
  transfers between devices with their start and end apart: 62, of which 16 were waited for; matrix products, arithmetic and copies ran while one was open for 8% of the time, Pallas kernels for 41%

profile of v4, /device:TPU:1, one launch (start us, length us, event | category | flops | bytes accessed | tf_op | source)
XLA Modules:
  0.0 232.6 jit_solution(15133789280771504803)
XLA Ops:
  2.7 2.1 collective-permute-start.2
  6.3 7.1 %attn_own_fwd.1 = (bf16[512,768]{1,0:T(8,128)(2,1)}, bf16[512,1152]{1,0:T(8,128)(2,1)}, bf16[512,384]{1,0:T(8,128)(2,1)}) custom-call(s32[8,17]{1,0:T(8,128)} %lens.7, s32[3]{0:T(128)} %pad_add_fusion.ids.r_0_.refs_0_, bf16[512,768]{1,0:T(8,128)(2,1)} %x_hbm.5, f32[8,768]{1,0:T(8,128)} %stack.48.vecs.r_5_, bf16[3,768,384]{2,1,0:T(8,128)(2,1)} %bitcast.13, ...), custom_call_target="tpu_custom_call" | custom-call | flops 500000000 | bytes 8388608 | tf_op jit(solution)/shard_map/attn_own_fwd/pallas_call | solution.py:638
  18.8 10.0 %collective-permute-done.1.bias.r_5_ = f32[3,768]{1,0:T(4,128)S(1)} collective-permute-done((f32[3,768]{1,0:T(4,128)S(1)}, f32[3,768]{1,0:T(4,128)S(1)}, u32[]{:S(2)}, u32[]{:S(2)}) %collective-permute-start.1) | collective-permute-done | bytes 9248 | tf_op jit(solution)/shard_map/ppermute | solution.py:578
  35.8 10.3 %attn_other_fwd.1 = (bf16[512,1152]{1,0:T(8,128)(2,1)}, bf16[512,384]{1,0:T(8,128)(2,1)}, f32[512,768]{1,0:T(8,128)}, bf16[512,768]{1,0:T(8,128)(2,1)}) custom-call(s32[8,17]{1,0:T(8,128)} %lens.7, s32[3]{0:T(128)} %pad_add_fusion.ids.r_0_.refs_0_, bf16[512,768]{1,0:T(8,128)(2,1)} %x_hbm.5, bf16[512,768]{1,0:T(8,128)(2,1)} %get-tuple-element.175.nrm_hbm, ...), custom_call_target="tpu_custom_call" | custom-call | flops 6000000000 | bytes 8388608 | tf_op jit(solution)/shard_map/attn_other_fwd/pallas_call | solution.py:661
  52.1 16.2 %mlp_own.1 = (bf16[1024,768]{1,0:T(8,128)(2,1)}, bf16[1024,768]{1,0:T(8,128)(2,1)}, bf16[384,768]{1,0:T(8,128)(2,1)}, bf16[384,768]{1,0:T(8,128)(2,1)}, bf16[384...) custom-call(s32[3]{0:T(128)} %pad_add_fusion.ids.r_0_.refs_0_, ...), custom_call_target="tpu_custom_call" | custom-call | flops 1000000000 | bytes 8388608 | tf_op jit(solution)/shard_map/mlp_own/pallas_call | solution.py:693
  69.7 16.3 %mlp_other.1 = (f32[512,768]{1,0:T(8,128)}, bf16[512,768]{1,0:T(8,128)(2,1)}, f32[512,768]{1,0:T(8,128)}, bf16[512,768]{1,0:T(8,128)(2,1)}, bf16[384,768]{1,0:T(...) custom-call(s32[3]{0:T(128)} %pad_add_fusion.ids.r_0_.refs_0_, ...), custom_call_target="tpu_custom_call" | custom-call | flops 12000000000 | bytes 8388608 | tf_op jit(solution)/shard_map/mlp_other/pallas_call | solution.py:702
  90.5 14.4 %attn_other_back.1 = (f32[512,768]{1,0:T(8,128)}, bf16[512,1152]{1,0:T(8,128)(2,1)}, bf16[768,768]{1,0:T(8,128)(2,1)}, bf16[768,768]{1,0:T(8,128)(2,1)}, f32[8,768]{1,0:T(8,128)}) custom-call(s32[8,17]{1,0:T(8,128)} %lens.7, s32[3]{0:T(128)} %pad_add_fusion.ids.r_0_.refs_0_, f32[512,768]{1,0:T(8,128)} %get-tuple-element.195.dnm_own_hbm, ...), custom_call_target="tpu_custom_call" | custom-call | flops 10000000000 | bytes 8388608 | tf_op jit(solution)/shard_map/attn_other_back/pallas_call | solution.py:725
  111.2 11.9 %attn_own_back.1 = (bf16[512,1152]{1,0:T(8,128)(2,1)}, bf16[768,768]{1,0:T(8,128)(2,1)}, bf16[768,768]{1,0:T(8,128)(2,1)}) custom-call(s32[8,17]{1,0:T(8,128)} %lens.7, s32[3]{0:T(128)} %pad_add_fusion.ids.r_0_.refs_0_, f32[512,768]{1,0:T(8,128)} %get-tuple-element.246.mg_hbm, bf16[384,768]{1,0:T(8,128)(2,1)} %wo_hbm.1, ...), custom_call_target="tpu_custom_call" | custom-call | flops 10000000000 | bytes 8388608 | tf_op jit(solution)/shard_map/attn_own_back/pallas_call | solution.py:749
  123.1 2.5 %collective-permute-done.23 = bf16[384,768]{1,0:T(8,128)(2,1)} collective-permute-done((bf16[384,768]{1,0:T(8,128)(2,1)S(1)}, bf16[384,768]{1,0:T(8,128)(2,1)}, u32[]{:S(2)}, u32[]{:S(2)}) %collective-permute-start.23) | collective-permute-done | bytes 589856 | tf_op jit(solution)/shard_map/ppermute | solution.py:578
  134.7 2.0 collective-permute-done.28
  136.9 2.4 %collective-permute-start.34 = (bf16[192,768]{1,0:T(8,128)(2,1)S(1)}, bf16[192,768]{1,0:T(8,128)(2,1)S(1)}, u32[]{:S(2)}, u32[]{:S(2)}) collective-permute-start(bf16[192,768]{1,0:T(8,128)(2,1)S(1)} %add_convert_fusion.11), channel_id=1, source_target_pairs={{0,16},{1,17},{2,18},{3,19},{4,20},{5,21},{6,22},{7,23},{8,24},{9,... | collective-permute-start | bytes 884744 | tf_op jit(solution)/shard_map/ppermute | solution.py:578
  139.6 8.8 %input_grad.1 = (bf16[512,768]{1,0:T(8,128)(2,1)}, f32[16,768]{1,0:T(8,128)}) custom-call(s32[3]{0:T(128)} %pad_add_fusion.ids.r_0_.refs_0_, bf16[512,1152]{1,0:T(8,128)(2,1)} %get-tuple-element.222.dqkv_a_hbm, bf16[512,1152]{1,0:T(8,128)(2,1)} %get-tuple-element.240.dqkv_b_hbm, f32[512,768]{1,0:T(8,128)} %get-tuple-element.246.mg_hbm, ...), custom_call_target="tpu_custom_call" | custom-call | flops 10000000 | bytes 8388608 | tf_op jit(solution)/shard_map/input_grad/pallas_call | solution.py:770
  154.4 6.2 %collective-permute-done.33 = f32[16,768]{1,0:T(8,128)S(1)} collective-permute-done((f32[16,768]{1,0:T(8,128)S(1)}, f32[16,768]{1,0:T(8,128)S(1)}, u32[]{:S(2)}, u32[]{:S(2)}) %collective-permute-start.33) | collective-permute-done | bytes 49184 | tf_op jit(solution)/shard_map/ppermute | solution.py:578
  165.6 2.8 %collective-permute-start.39 = (bf16[192,768]{1,0:T(8,128)(2,1)S(1)}, bf16[192,768]{1,0:T(8,128)(2,1)S(1)}, u32[]{:S(2)}, u32[]{:S(2)}) collective-permute-start(bf16[192,768]{1,0:T(8,128)(2,1)S(1)} %add_convert_fusion.7), channel_id=1, source_target_pairs={{0,16},{1,17},{2,18},{3,19},{4,20},{5,21},{6,22},{7,23},{8,24},{9,... | collective-permute-start | bytes 884744 | tf_op jit(solution)/shard_map/ppermute | solution.py:578
  169.0 4.0 %layer_out.1 = bf16[512,768]{1,0:T(8,128)(2,1)} custom-call(f32[512,768]{1,0:T(8,128)} %get-tuple-element.179.mid_hbm, f32[512,768]{1,0:T(8,128)} %get-tuple-element.186.own_hbm, bf16[512,768]{1,0:T(8,128)(2,1)} %collective-permute-done.17.sib_hbm, f32[8,768]{1,0:T(8,128)} %stack.48.vecs.r_5_), custom_call_target="tpu_custom_call" | custom-call | flops 10000000 | bytes 8388608 | tf_op jit(solution)/shard_map/layer_out/pallas_call | solution.py:811
  173.0 8.3 %collective-permute-done.38 = bf16[192,768]{1,0:T(8,128)(2,1)S(1)} collective-permute-done((bf16[192,768]{1,0:T(8,128)(2,1)S(1)}, bf16[192,768]{1,0:T(8,128)(2,1)S(1)}, u32[]{:S(2)}, u32[]{:S(2)}) %collective-permute-start.38) | collective-permute-done | bytes 294944 | tf_op jit(solution)/shard_map/ppermute | solution.py:578
  183.2 2.0 collective-permute-start.45
  187.9 7.5 %collective-permute-done.45 = bf16[192,768]{1,0:T(8,128)(2,1)S(1)} collective-permute-done((bf16[192,768]{1,0:T(8,128)(2,1)S(1)}, bf16[192,768]{1,0:T(8,128)(2,1)S(1)}, u32[]{:S(2)}, u32[]{:S(2)}) %collective-permute-start.45) | collective-permute-done | bytes 294944 | tf_op jit(solution)/shard_map/ppermute | solution.py:578
  195.4 8.9 %collective-permute-done.43.refs_11_ = bf16[192,768]{1,0:T(8,128)(2,1)S(1)} collective-permute-done((bf16[192,768]{1,0:T(8,128)(2,1)S(1)}, bf16[192,768]{1,0:T(8,128)(2,1)S(1)}, u32[]{:S(2)}, u32[]{:S(2)}) %collective-permute-start.43) | collective-permute-done | bytes 294944 | tf_op jit(solution)/shard_map/ppermute | solution.py:578
  204.3 2.7 %collective-permute-start.50 = (bf16[192,768]{1,0:T(8,128)(2,1)S(1)}, bf16[192,768]{1,0:T(8,128)(2,1)S(1)}, u32[]{:S(2)}, u32[]{:S(2)}) collective-permute-start(bf16[192,768]{1,0:T(8,128)(2,1)S(1)} %add_convert_fusion.5.refs_8_), channel_id=1, source_target_pairs={{0,2},{1,3},{2,0},{3,1},{4,6},{5,7},{6,4},{7,5},{8,10},{9,11},{10,... | collective-permute-start | bytes 884744 | tf_op jit(solution)/shard_map/ppermute | solution.py:578
  212.7 5.7 %place_two.1 = (f32[768,1536]{1,0:T(8,128)}, f32[3,768,384]{2,1,0:T(8,128)}, f32[384,768]{1,0:T(8,128)}) custom-call(s32[3]{0:T(128)S(1)} %copy-done, bf16[192,768]{1,0:T(8,128)(2,1)S(1)} %add_convert_fusion.8.refs_0_, bf16[192,768]{1,0:T(8,128)(2,1)S(1)} %collective-permute-done.35.refs_1_, bf16[192,768]{1,0:T(8,128)(2,1)S(1)} %collective-permute-done.36.refs_2_, ...), custom_call_target="tpu_custom_call" | custom-call | flops 10000000 | bytes 8388608 | tf_op jit(solution)/shard_map/place_two/pallas_call | solution.py:834
  219.0 2.1 collective-permute-start.56
  222.5 2.5 %collective-permute-done.60.refs_4_ = bf16[192,768]{1,0:T(8,128)(2,1)S(1)} collective-permute-done((bf16[192,768]{1,0:T(8,128)(2,1)S(1)}, bf16[192,768]{1,0:T(8,128)(2,1)S(1)}, u32[]{:S(2)}, u32[]{:S(2)}) %collective-permute-start.60) | collective-permute-done | bytes 294944 | tf_op jit(solution)/shard_map/ppermute | solution.py:578
  229.0 3.4 %place_down.1 = f32[1536,768]{1,0:T(8,128)} custom-call(s32[3]{0:T(128)S(1)} %copy-done, bf16[192,768]{1,0:T(8,128)(2,1)S(1)} %add_convert_fusion.3.refs_1_, bf16[192,768]{1,0:T(8,128)(2,1)S(1)} %collective-permute-done.54.refs_2_, bf16[192,768]{1,0:T(8,128)(2,1)S(1)} %collective-permute-done.55.refs_3_, ...), custom_call_target="tpu_custom_call" | custom-call | flops 1000000000 | bytes 8388608 | tf_op jit(solution)/shard_map/place_down/pallas_call | solution.py:857
  (232 shorter events, 70.9 us)
Async XLA Ops:
  14.6 17.1 %collective-permute-start = (bf16[384,768]{1,0:T(8,128)(2,1)S(1)}, bf16[384,768]{1,0:T(8,128)(2,1)}, u32[]{:S(2)}, u32[]{:S(2)}) collective-permute-start(bf16[384,768]{1,0:T(8,128)(2,1)S(1)} %pad_maximum_fusion), channel_id=1, source_target_pairs={{0,1},{1,0},{2,3},{3,2},{4,5},{5,4},{6,7},{7,6},{8,9},{9,8},{10,11... | collective-permute-start | bytes 1769480 | tf_op jit(solution)/shard_map/ppermute | solution.py:578
  14.7 16.0 %collective-permute-start.3 = (bf16[192,768]{1,0:T(8,128)(2,1)S(1)}, bf16[192,768]{1,0:T(8,128)(2,1)S(1)}, u32[]{:S(2)}, u32[]{:S(2)}) collective-permute-start(bf16[192,768]{1,0:T(8,128)(2,1)S(1)} %collective-permute-done.2.refs_0_), channel_id=1, source_target_pairs={{0,4},{1,5},{2,6},{3,7},{4,0},{5,1},{6,2},{7,3},{8,12},{9,13},{10,... | collective-permute-start | bytes 884744 | tf_op jit(solution)/shard_map/ppermute | solution.py:578
  16.1 14.7 %collective-permute-start.4 = (bf16[192,768]{1,0:T(8,128)(2,1)S(1)}, bf16[192,768]{1,0:T(8,128)(2,1)S(1)}, u32[]{:S(2)}, u32[]{:S(2)}) collective-permute-start(bf16[192,768]{1,0:T(8,128)(2,1)S(1)} %collective-permute-done.2.refs_0_), channel_id=1, source_target_pairs={{0,8},{1,9},{2,10},{3,11},{4,12},{5,13},{6,14},{7,15},{8,0},{9,1},... | collective-permute-start | bytes 884744 | tf_op jit(solution)/shard_map/ppermute | solution.py:578
  31.7 15.2 %collective-permute-start.10 = (bf16[384,768]{1,0:T(8,128)(2,1)}, bf16[384,768]{1,0:T(8,128)(2,1)}, u32[]{:S(2)}, u32[]{:S(2)}) collective-permute-start(bf16[384,768]{1,0:T(8,128)(2,1)} %collective-permute-done.r_6_), channel_id=1, source_target_pairs={{0,4},{1,5},{2,6},{3,7},{4,0},{5,1},{6,2},{7,3},{8,12},{9,13},{10,... | collective-permute-start | bytes 1769480 | tf_op jit(solution)/shard_map/ppermute | solution.py:578
  33.0 14.9 %collective-permute-start.11 = (bf16[384,768]{1,0:T(8,128)(2,1)}, bf16[384,768]{1,0:T(8,128)(2,1)}, u32[]{:S(2)}, u32[]{:S(2)}) collective-permute-start(bf16[384,768]{1,0:T(8,128)(2,1)} %collective-permute-done.r_6_), channel_id=1, source_target_pairs={{0,8},{1,9},{2,10},{3,11},{4,12},{5,13},{6,14},{7,15},{8,0},{9,1},... | collective-permute-start | bytes 1769480 | tf_op jit(solution)/shard_map/ppermute | solution.py:578
  34.3 16.0 %collective-permute-start.13 = (bf16[512,768]{1,0:T(8,128)(2,1)S(1)}, bf16[512,768]{1,0:T(8,128)(2,1)S(1)}, u32[]{:S(2)}, u32[]{:S(2)}) collective-permute-start(bf16[512,768]{1,0:T(8,128)(2,1)S(1)} %copy-done.4), channel_id=1, source_target_pairs={{0,2},{1,3},{2,0},{3,1},{4,6},{5,7},{6,4},{7,5},{8,10},{9,11},{10,... | collective-permute-start | bytes 2359304 | tf_op jit(solution)/shard_map/ppermute | solution.py:578
  49.1 20.6 %collective-permute-start.14 = (bf16[384,768]{1,0:T(8,128)(2,1)}, bf16[384,768]{1,0:T(8,128)(2,1)}, u32[]{:S(2)}, u32[]{:S(2)}) collective-permute-start(bf16[384,768]{1,0:T(8,128)(2,1)} %collective-permute-done.r_6_), channel_id=1, source_target_pairs={{0,12},{1,13},{2,14},{3,15},{4,8},{5,9},{6,10},{7,11},{8,4},{9,5},... | collective-permute-start | bytes 1769480 | tf_op jit(solution)/shard_map/ppermute | solution.py:578
  68.4 17.6 %collective-permute-start.15 = (bf16[384,768]{1,0:T(8,128)(2,1)}, bf16[384,768]{1,0:T(8,128)(2,1)S(1)}, u32[]{:S(2)}, u32[]{:S(2)}) collective-permute-start(bf16[384,768]{1,0:T(8,128)(2,1)} %get-tuple-element.187), channel_id=1, source_target_pairs={{0,4},{1,5},{2,6},{3,7},{4,0},{5,1},{6,2},{7,3},{8,12},{9,13},{10,... | collective-permute-start | bytes 1769480 | tf_op jit(solution)/shard_map/ppermute | solution.py:578
  86.7 18.2 %collective-permute-start.19 = (bf16[192,768]{1,0:T(8,128)(2,1)S(1)}, bf16[192,768]{1,0:T(8,128)(2,1)S(1)}, u32[]{:S(2)}, u32[]{:S(2)}) collective-permute-start(bf16[192,768]{1,0:T(8,128)(2,1)S(1)} %add_convert_fusion.15), channel_id=1, source_target_pairs={{0,8},{1,9},{2,10},{3,11},{4,12},{5,13},{6,14},{7,15},{8,0},{9,1},... | collective-permute-start | bytes 884744 | tf_op jit(solution)/shard_map/ppermute | solution.py:578
  87.2 17.8 %collective-permute-start.18 = (bf16[384,768]{1,0:T(8,128)(2,1)}, bf16[384,768]{1,0:T(8,128)(2,1)S(1)}, u32[]{:S(2)}, u32[]{:S(2)}) collective-permute-start(bf16[384,768]{1,0:T(8,128)(2,1)} %get-tuple-element.203), channel_id=1, source_target_pairs={{0,4},{1,5},{2,6},{3,7},{4,0},{5,1},{6,2},{7,3},{8,12},{9,13},{10,... | collective-permute-start | bytes 1769480 | tf_op jit(solution)/shard_map/ppermute | solution.py:578
  88.4 16.6 %collective-permute-start.20 = (bf16[384,768]{1,0:T(8,128)(2,1)}, bf16[384,768]{1,0:T(8,128)(2,1)S(1)}, u32[]{:S(2)}, u32[]{:S(2)}) collective-permute-start(bf16[384,768]{1,0:T(8,128)(2,1)} %get-tuple-element.208), channel_id=1, source_target_pairs={{0,1},{1,0},{2,3},{3,2},{4,5},{5,4},{6,7},{7,6},{8,9},{9,8},{10,11... | collective-permute-start | bytes 1769480 | tf_op jit(solution)/shard_map/ppermute | solution.py:578
  106.0 17.1 %collective-permute-start.24 = (bf16[384,768]{1,0:T(8,128)(2,1)}, bf16[384,768]{1,0:T(8,128)(2,1)}, u32[]{:S(2)}, u32[]{:S(2)}) collective-permute-start(bf16[384,768]{1,0:T(8,128)(2,1)} %get-tuple-element.217), channel_id=1, source_target_pairs={{0,1},{1,0},{2,3},{3,2},{4,5},{5,4},{6,7},{7,6},{8,9},{9,8},{10,11... | collective-permute-start | bytes 1769480 | tf_op jit(solution)/shard_map/ppermute | solution.py:578
  107.0 16.1 %collective-permute-start.21 = (bf16[192,768]{1,0:T(8,128)(2,1)}, bf16[192,768]{1,0:T(8,128)(2,1)}, u32[]{:S(2)}, u32[]{:S(2)}) collective-permute-start(bf16[192,768]{1,0:T(8,128)(2,1)} %add_convert_fusion.14), channel_id=1, source_target_pairs={{0,8},{1,9},{2,10},{3,11},{4,12},{5,13},{6,14},{7,15},{8,0},{9,1},... | collective-permute-start | bytes 884744 | tf_op jit(solution)/shard_map/ppermute | solution.py:578
  110.9 14.7 %collective-permute-start.23 = (bf16[384,768]{1,0:T(8,128)(2,1)S(1)}, bf16[384,768]{1,0:T(8,128)(2,1)}, u32[]{:S(2)}, u32[]{:S(2)}) collective-permute-start(bf16[384,768]{1,0:T(8,128)(2,1)S(1)} %add_convert_fusion.2), channel_id=1, source_target_pairs={{0,4},{1,5},{2,6},{3,7},{4,0},{5,1},{6,2},{7,3},{8,12},{9,13},{10,... | collective-permute-start | bytes 1769480 | tf_op jit(solution)/shard_map/ppermute | solution.py:578
  130.5 19.2 %collective-permute-start.27 = (bf16[384,768]{1,0:T(8,128)(2,1)}, bf16[384,768]{1,0:T(8,128)(2,1)}, u32[]{:S(2)}, u32[]{:S(2)}) collective-permute-start(bf16[384,768]{1,0:T(8,128)(2,1)} %add_convert_fusion.1), channel_id=1, source_target_pairs={{0,4},{1,5},{2,6},{3,7},{4,0},{5,1},{6,2},{7,3},{8,12},{9,13},{10,... | collective-permute-start | bytes 1769480 | tf_op jit(solution)/shard_map/ppermute | solution.py:578
  132.7 18.1 %collective-permute-start.30 = (bf16[192,768]{1,0:T(8,128)(2,1)}, bf16[192,768]{1,0:T(8,128)(2,1)}, u32[]{:S(2)}, u32[]{:S(2)}) collective-permute-start(bf16[192,768]{1,0:T(8,128)(2,1)} %add_convert_fusion.12), channel_id=1, source_target_pairs={{0,8},{1,9},{2,10},{3,11},{4,12},{5,13},{6,14},{7,15},{8,0},{9,1},... | collective-permute-start | bytes 884744 | tf_op jit(solution)/shard_map/ppermute | solution.py:578
  136.9 17.2 %collective-permute-start.34 = (bf16[192,768]{1,0:T(8,128)(2,1)S(1)}, bf16[192,768]{1,0:T(8,128)(2,1)S(1)}, u32[]{:S(2)}, u32[]{:S(2)}) collective-permute-start(bf16[192,768]{1,0:T(8,128)(2,1)S(1)} %add_convert_fusion.11), channel_id=1, source_target_pairs={{0,16},{1,17},{2,18},{3,19},{4,20},{5,21},{6,22},{7,23},{8,24},{9,... | collective-permute-start | bytes 884744 | tf_op jit(solution)/shard_map/ppermute | solution.py:578
  139.3 24.7 %collective-permute-start.26 = (bf16[384,768]{1,0:T(8,128)(2,1)}, bf16[384,768]{1,0:T(8,128)(2,1)}, u32[]{:S(2)}, u32[]{:S(2)}) collective-permute-start(bf16[384,768]{1,0:T(8,128)(2,1)} %add_convert_fusion), channel_id=1, source_target_pairs={{0,4},{1,5},{2,6},{3,7},{4,0},{5,1},{6,2},{7,3},{8,12},{9,13},{10,... | collective-permute-start | bytes 1769480 | tf_op jit(solution)/shard_map/ppermute | solution.py:578
  153.5 14.9 %collective-permute-start.17 = (bf16[512,768]{1,0:T(8,128)(2,1)S(1)}, bf16[512,768]{1,0:T(8,128)(2,1)}, u32[]{:S(2)}, u32[]{:S(2)}) collective-permute-start(bf16[512,768]{1,0:T(8,128)(2,1)S(1)} %copy-done.35), channel_id=1, source_target_pairs={{0,2},{1,3},{2,0},{3,1},{4,6},{5,7},{6,4},{7,5},{8,10},{9,11},{10,... | collective-permute-start | bytes 2359304 | tf_op jit(solution)/shard_map/ppermute | solution.py:578
  165.2 16.1 %collective-permute-start.38 = (bf16[192,768]{1,0:T(8,128)(2,1)S(1)}, bf16[192,768]{1,0:T(8,128)(2,1)S(1)}, u32[]{:S(2)}, u32[]{:S(2)}) collective-permute-start(bf16[192,768]{1,0:T(8,128)(2,1)S(1)} %add_convert_fusion.6), channel_id=1, source_target_pairs={{0,8},{1,9},{2,10},{3,11},{4,12},{5,13},{6,14},{7,15},{8,0},{9,1},... | collective-permute-start | bytes 884744 | tf_op jit(solution)/shard_map/ppermute | solution.py:578
  165.6 15.7 %collective-permute-start.39 = (bf16[192,768]{1,0:T(8,128)(2,1)S(1)}, bf16[192,768]{1,0:T(8,128)(2,1)S(1)}, u32[]{:S(2)}, u32[]{:S(2)}) collective-permute-start(bf16[192,768]{1,0:T(8,128)(2,1)S(1)} %add_convert_fusion.7), channel_id=1, source_target_pairs={{0,16},{1,17},{2,18},{3,19},{4,20},{5,21},{6,22},{7,23},{8,24},{9,... | collective-permute-start | bytes 884744 | tf_op jit(solution)/shard_map/ppermute | solution.py:578
  181.4 13.9 %collective-permute-start.41 = (bf16[192,768]{1,0:T(8,128)(2,1)S(1)}, bf16[192,768]{1,0:T(8,128)(2,1)S(1)}, u32[]{:S(2)}, u32[]{:S(2)}) collective-permute-start(bf16[192,768]{1,0:T(8,128)(2,1)S(1)} %add_convert_fusion.5.refs_8_), channel_id=1, source_target_pairs={{0,4},{1,5},{2,6},{3,7},{4,0},{5,1},{6,2},{7,3},{8,12},{9,13},{10,... | collective-permute-start | bytes 884744 | tf_op jit(solution)/shard_map/ppermute | solution.py:578
  186.1 18.2 %collective-permute-start.43 = (bf16[192,768]{1,0:T(8,128)(2,1)S(1)}, bf16[192,768]{1,0:T(8,128)(2,1)S(1)}, u32[]{:S(2)}, u32[]{:S(2)}) collective-permute-start(bf16[192,768]{1,0:T(8,128)(2,1)S(1)} %add_convert_fusion.5.refs_8_), channel_id=1, source_target_pairs={{0,12},{1,13},{2,14},{3,15},{4,8},{5,9},{6,10},{7,11},{8,4},{9,5},... | collective-permute-start | bytes 884744 | tf_op jit(solution)/shard_map/ppermute | solution.py:578
  187.2 17.1 %collective-permute-start.44 = (bf16[192,768]{1,0:T(8,128)(2,1)S(1)}, bf16[192,768]{1,0:T(8,128)(2,1)S(1)}, u32[]{:S(2)}, u32[]{:S(2)}) collective-permute-start(bf16[192,768]{1,0:T(8,128)(2,1)S(1)} %collective-permute-done.36.refs_2_), channel_id=1, source_target_pairs={{0,4},{1,5},{2,6},{3,7},{4,0},{5,1},{6,2},{7,3},{8,12},{9,13},{10,... | collective-permute-start | bytes 884744 | tf_op jit(solution)/shard_map/ppermute | solution.py:578
  (77 other events, 516.7 us)

commit v5 on v4

--- a/solution.py
+++ b/solution.py
@@ -800,10 +800,10 @@
         s2 = swap(total((second, second, high_half), keep_s, s_sib, s1), FAR)
         o_back = swap(total((first, first, low_half, whole), keep_o, o_sib, o1, o2), TP)
         vec = step(vec, CORE_BIT)
+        for bit in range(FIRST_REST, bits):
+            vec = step(vec, bit)
         a_unit = rest(a_unit, a_more)
         a_near, a_far = swap(a_unit, NEAR), swap(a_unit, FAR)
-        for bit in range(FIRST_REST, bits):
-            vec = step(vec, bit)
         s_unit = total((first, first, low_half, whole, whole), keep_s, s_sib, s1, s2, o_back)
         s_more = swap(s_unit, 1 << FIRST_REST)
         vec_tp = swap(vec, TP)

time: 233 us -> 233 us (level)
  transfers between devices with their start and end apart: 62 -> 62, of which waited for: 16 -> 18; matrix products, arithmetic and copies ran while one was open for 8% -> 8% of each run, Pallas kernels for 41% -> 41%
where the time goes in v5:
time: 233 us; the launch traced here: 232 us
  Pallas kernels  98.1 us (42%)
  starting transfers between devices  54.7 us (23%)
  waiting for transfers between devices  54.3 us (23%)
  other arithmetic  14.2 us (6%)
  local copies, waits for them, and re-layouts  9.4 us (4%)
    ppermute x62, starting transfers between devices, swap(): lax.ppermute(value, ('dp', 'tp'), [(i, i ^ mask) for i in range(devices)])  54.7 us
    ppermute x62, waiting for transfers between devices, swap(): lax.ppermute(value, ('dp', 'tp'), [(i, i ^ mask) for i in range(devices)])  54.3 us
    pallas_call x1, Pallas kernels, on_device(): call(lambda *r: mlp_kernel(False, *r), [(one, F32), (one, BF16), (one, F3...  16.3 us
    pallas_call x1, Pallas kernels, on_device(): call(lambda *r: mlp_kernel(True, *r), [(both, BF16), (both, BF16), *[(pai...  16.2 us
    pallas_call x1, Pallas kernels, on_device(): call(other_back_kernel, [(one, F32), (acts, BF16), (grad_units, BF16), (g...  14.4 us
    convert_element_type x16, other arithmetic, total(): add(*[cut(term, part) for term, part in zip(turn(*terms), parts)])  13.5 us
    pallas_call x1, Pallas kernels, on_device(): call(own_back_kernel, [(acts, BF16), (grad_units, BF16), (grad_units, BF1...  11.9 us
    pallas_call x1, Pallas kernels, on_device(): call(other_fwd_kernel, [(acts, BF16), (head, BF16), (one, F32), (one, BF1...  10.3 us
  transfers between devices with their start and end apart: 62, of which 18 were waited for; matrix products, arithmetic and copies ran while one was open for 8% of the time, Pallas kernels for 41%

profile of v5, /device:TPU:1, one launch (start us, length us, event | category | flops | bytes accessed | tf_op | source)
XLA Modules:
  0.0 232.3 jit_solution(16166586598673701054)
XLA Ops:
  2.7 2.1 collective-permute-start.2
  6.3 7.1 %attn_own_fwd.1 = (bf16[512,768]{1,0:T(8,128)(2,1)}, bf16[512,1152]{1,0:T(8,128)(2,1)}, bf16[512,384]{1,0:T(8,128)(2,1)}) custom-call(s32[8,17]{1,0:T(8,128)} %lens.7, s32[3]{0:T(128)} %pad_add_fusion.ids.r_0_.refs_0_, bf16[512,768]{1,0:T(8,128)(2,1)} %x_hbm.5, f32[8,768]{1,0:T(8,128)} %stack.48.vecs.r_5_, bf16[3,768,384]{2,1,0:T(8,128)(2,1)} %bitcast.13, ...), custom_call_target="tpu_custom_call" | custom-call | flops 500000000 | bytes 8388608 | tf_op jit(solution)/shard_map/attn_own_fwd/pallas_call | solution.py:638
  18.8 10.0 %collective-permute-done.1.bias.r_5_ = f32[3,768]{1,0:T(4,128)S(1)} collective-permute-done((f32[3,768]{1,0:T(4,128)S(1)}, f32[3,768]{1,0:T(4,128)S(1)}, u32[]{:S(2)}, u32[]{:S(2)}) %collective-permute-start.1) | collective-permute-done | bytes 9248 | tf_op jit(solution)/shard_map/ppermute | solution.py:578
  35.8 10.3 %attn_other_fwd.1 = (bf16[512,1152]{1,0:T(8,128)(2,1)}, bf16[512,384]{1,0:T(8,128)(2,1)}, f32[512,768]{1,0:T(8,128)}, bf16[512,768]{1,0:T(8,128)(2,1)}) custom-call(s32[8,17]{1,0:T(8,128)} %lens.7, s32[3]{0:T(128)} %pad_add_fusion.ids.r_0_.refs_0_, bf16[512,768]{1,0:T(8,128)(2,1)} %x_hbm.5, bf16[512,768]{1,0:T(8,128)(2,1)} %get-tuple-element.175.nrm_hbm, ...), custom_call_target="tpu_custom_call" | custom-call | flops 6000000000 | bytes 8388608 | tf_op jit(solution)/shard_map/attn_other_fwd/pallas_call | solution.py:661
  52.1 16.2 %mlp_own.1 = (bf16[1024,768]{1,0:T(8,128)(2,1)}, bf16[1024,768]{1,0:T(8,128)(2,1)}, bf16[384,768]{1,0:T(8,128)(2,1)}, bf16[384,768]{1,0:T(8,128)(2,1)}, bf16[384...) custom-call(s32[3]{0:T(128)} %pad_add_fusion.ids.r_0_.refs_0_, ...), custom_call_target="tpu_custom_call" | custom-call | flops 1000000000 | bytes 8388608 | tf_op jit(solution)/shard_map/mlp_own/pallas_call | solution.py:693
  69.7 16.3 %mlp_other.1 = (f32[512,768]{1,0:T(8,128)}, bf16[512,768]{1,0:T(8,128)(2,1)}, f32[512,768]{1,0:T(8,128)}, bf16[512,768]{1,0:T(8,128)(2,1)}, bf16[384,768]{1,0:T(...) custom-call(s32[3]{0:T(128)} %pad_add_fusion.ids.r_0_.refs_0_, ...), custom_call_target="tpu_custom_call" | custom-call | flops 12000000000 | bytes 8388608 | tf_op jit(solution)/shard_map/mlp_other/pallas_call | solution.py:702
  90.5 14.4 %attn_other_back.1 = (f32[512,768]{1,0:T(8,128)}, bf16[512,1152]{1,0:T(8,128)(2,1)}, bf16[768,768]{1,0:T(8,128)(2,1)}, bf16[768,768]{1,0:T(8,128)(2,1)}, f32[8,768]{1,0:T(8,128)}) custom-call(s32[8,17]{1,0:T(8,128)} %lens.7, s32[3]{0:T(128)} %pad_add_fusion.ids.r_0_.refs_0_, f32[512,768]{1,0:T(8,128)} %get-tuple-element.195.dnm_own_hbm, ...), custom_call_target="tpu_custom_call" | custom-call | flops 10000000000 | bytes 8388608 | tf_op jit(solution)/shard_map/attn_other_back/pallas_call | solution.py:725
  111.2 11.9 %attn_own_back.1 = (bf16[512,1152]{1,0:T(8,128)(2,1)}, bf16[768,768]{1,0:T(8,128)(2,1)}, bf16[768,768]{1,0:T(8,128)(2,1)}) custom-call(s32[8,17]{1,0:T(8,128)} %lens.7, s32[3]{0:T(128)} %pad_add_fusion.ids.r_0_.refs_0_, f32[512,768]{1,0:T(8,128)} %get-tuple-element.246.mg_hbm, bf16[384,768]{1,0:T(8,128)(2,1)} %wo_hbm.1, ...), custom_call_target="tpu_custom_call" | custom-call | flops 10000000000 | bytes 8388608 | tf_op jit(solution)/shard_map/attn_own_back/pallas_call | solution.py:749
  123.1 2.5 %collective-permute-done.23 = bf16[384,768]{1,0:T(8,128)(2,1)} collective-permute-done((bf16[384,768]{1,0:T(8,128)(2,1)S(1)}, bf16[384,768]{1,0:T(8,128)(2,1)}, u32[]{:S(2)}, u32[]{:S(2)}) %collective-permute-start.23) | collective-permute-done | bytes 589856 | tf_op jit(solution)/shard_map/ppermute | solution.py:578
  130.7 2.0 add_convert_fusion.12
  134.7 2.0 collective-permute-done.28
  136.9 2.4 %collective-permute-start.32 = (bf16[192,768]{1,0:T(8,128)(2,1)S(1)}, bf16[192,768]{1,0:T(8,128)(2,1)S(1)}, u32[]{:S(2)}, u32[]{:S(2)}) collective-permute-start(bf16[192,768]{1,0:T(8,128)(2,1)S(1)} %add_convert_fusion.11), channel_id=1, source_target_pairs={{0,16},{1,17},{2,18},{3,19},{4,20},{5,21},{6,22},{7,23},{8,24},{9,... | collective-permute-start | bytes 884744 | tf_op jit(solution)/shard_map/ppermute | solution.py:578
  139.6 8.8 %input_grad.1 = (bf16[512,768]{1,0:T(8,128)(2,1)}, f32[16,768]{1,0:T(8,128)}) custom-call(s32[3]{0:T(128)} %pad_add_fusion.ids.r_0_.refs_0_, bf16[512,1152]{1,0:T(8,128)(2,1)} %get-tuple-element.222.dqkv_a_hbm, bf16[512,1152]{1,0:T(8,128)(2,1)} %get-tuple-element.240.dqkv_b_hbm, f32[512,768]{1,0:T(8,128)} %get-tuple-element.246.mg_hbm, ...), custom_call_target="tpu_custom_call" | custom-call | flops 10000000 | bytes 8388608 | tf_op jit(solution)/shard_map/input_grad/pallas_call | solution.py:770
  153.6 2.6 %collective-permute-done.34 = f32[16,768]{1,0:T(8,128)S(1)} collective-permute-done((f32[16,768]{1,0:T(8,128)S(1)}, f32[16,768]{1,0:T(8,128)S(1)}, u32[]{:S(2)}, u32[]{:S(2)}) %collective-permute-start.34) | collective-permute-done | bytes 49184 | tf_op jit(solution)/shard_map/ppermute | solution.py:578
  156.2 2.3 collective-permute-start.17
  167.6 4.0 %layer_out.1 = bf16[512,768]{1,0:T(8,128)(2,1)} custom-call(f32[512,768]{1,0:T(8,128)} %get-tuple-element.179.mid_hbm, f32[512,768]{1,0:T(8,128)} %get-tuple-element.186.own_hbm, bf16[512,768]{1,0:T(8,128)(2,1)} %collective-permute-done.17.sib_hbm, f32[8,768]{1,0:T(8,128)} %stack.48.vecs.r_5_), custom_call_target="tpu_custom_call" | custom-call | flops 10000000 | bytes 8388608 | tf_op jit(solution)/shard_map/layer_out/pallas_call | solution.py:811
  171.6 9.1 %collective-permute-done.38 = bf16[192,768]{1,0:T(8,128)(2,1)S(1)} collective-permute-done((bf16[192,768]{1,0:T(8,128)(2,1)S(1)}, bf16[192,768]{1,0:T(8,128)(2,1)S(1)}, u32[]{:S(2)}, u32[]{:S(2)}) %collective-permute-start.38) | collective-permute-done | bytes 294944 | tf_op jit(solution)/shard_map/ppermute | solution.py:578
  186.9 9.7 %collective-permute-done.45 = bf16[192,768]{1,0:T(8,128)(2,1)S(1)} collective-permute-done((bf16[192,768]{1,0:T(8,128)(2,1)S(1)}, bf16[192,768]{1,0:T(8,128)(2,1)S(1)}, u32[]{:S(2)}, u32[]{:S(2)}) %collective-permute-start.45) | collective-permute-done | bytes 294944 | tf_op jit(solution)/shard_map/ppermute | solution.py:578
  196.6 7.2 %collective-permute-done.43.refs_11_ = bf16[192,768]{1,0:T(8,128)(2,1)S(1)} collective-permute-done((bf16[192,768]{1,0:T(8,128)(2,1)S(1)}, bf16[192,768]{1,0:T(8,128)(2,1)S(1)}, u32[]{:S(2)}, u32[]{:S(2)}) %collective-permute-start.43) | collective-permute-done | bytes 294944 | tf_op jit(solution)/shard_map/ppermute | solution.py:578
  203.8 2.6 %collective-permute-start.50 = (bf16[192,768]{1,0:T(8,128)(2,1)S(1)}, bf16[192,768]{1,0:T(8,128)(2,1)S(1)}, u32[]{:S(2)}, u32[]{:S(2)}) collective-permute-start(bf16[192,768]{1,0:T(8,128)(2,1)S(1)} %add_convert_fusion.5.refs_8_), channel_id=1, source_target_pairs={{0,2},{1,3},{2,0},{3,1},{4,6},{5,7},{6,4},{7,5},{8,10},{9,11},{10,... | collective-permute-start | bytes 884744 | tf_op jit(solution)/shard_map/ppermute | solution.py:578
  212.6 5.7 %place_two.1 = (f32[768,1536]{1,0:T(8,128)}, f32[3,768,384]{2,1,0:T(8,128)}, f32[384,768]{1,0:T(8,128)}) custom-call(s32[3]{0:T(128)S(1)} %copy-done, bf16[192,768]{1,0:T(8,128)(2,1)S(1)} %add_convert_fusion.8.refs_0_, bf16[192,768]{1,0:T(8,128)(2,1)S(1)} %collective-permute-done.35.refs_1_, bf16[192,768]{1,0:T(8,128)(2,1)S(1)} %collective-permute-done.36.refs_2_, ...), custom_call_target="tpu_custom_call" | custom-call | flops 10000000 | bytes 8388608 | tf_op jit(solution)/shard_map/place_two/pallas_call | solution.py:834
  218.4 2.1 collective-permute-start.56
  221.9 2.4 %collective-permute-done.60.refs_4_ = bf16[192,768]{1,0:T(8,128)(2,1)S(1)} collective-permute-done((bf16[192,768]{1,0:T(8,128)(2,1)S(1)}, bf16[192,768]{1,0:T(8,128)(2,1)S(1)}, u32[]{:S(2)}, u32[]{:S(2)}) %collective-permute-start.60) | collective-permute-done | bytes 294944 | tf_op jit(solution)/shard_map/ppermute | solution.py:578
  228.7 3.4 %place_down.1 = f32[1536,768]{1,0:T(8,128)} custom-call(s32[3]{0:T(128)S(1)} %copy-done, bf16[192,768]{1,0:T(8,128)(2,1)S(1)} %add_convert_fusion.3.refs_1_, bf16[192,768]{1,0:T(8,128)(2,1)S(1)} %collective-permute-done.54.refs_2_, bf16[192,768]{1,0:T(8,128)(2,1)S(1)} %collective-permute-done.55.refs_3_, ...), custom_call_target="tpu_custom_call" | custom-call | flops 1000000000 | bytes 8388608 | tf_op jit(solution)/shard_map/place_down/pallas_call | solution.py:857
  (232 shorter events, 73.6 us)
Async XLA Ops:
  14.6 17.1 %collective-permute-start = (bf16[384,768]{1,0:T(8,128)(2,1)S(1)}, bf16[384,768]{1,0:T(8,128)(2,1)}, u32[]{:S(2)}, u32[]{:S(2)}) collective-permute-start(bf16[384,768]{1,0:T(8,128)(2,1)S(1)} %pad_maximum_fusion), channel_id=1, source_target_pairs={{0,1},{1,0},{2,3},{3,2},{4,5},{5,4},{6,7},{7,6},{8,9},{9,8},{10,11... | collective-permute-start | bytes 1769480 | tf_op jit(solution)/shard_map/ppermute | solution.py:578
  14.7 16.0 %collective-permute-start.3 = (bf16[192,768]{1,0:T(8,128)(2,1)S(1)}, bf16[192,768]{1,0:T(8,128)(2,1)S(1)}, u32[]{:S(2)}, u32[]{:S(2)}) collective-permute-start(bf16[192,768]{1,0:T(8,128)(2,1)S(1)} %collective-permute-done.2.refs_0_), channel_id=1, source_target_pairs={{0,4},{1,5},{2,6},{3,7},{4,0},{5,1},{6,2},{7,3},{8,12},{9,13},{10,... | collective-permute-start | bytes 884744 | tf_op jit(solution)/shard_map/ppermute | solution.py:578
  16.1 14.7 %collective-permute-start.4 = (bf16[192,768]{1,0:T(8,128)(2,1)S(1)}, bf16[192,768]{1,0:T(8,128)(2,1)S(1)}, u32[]{:S(2)}, u32[]{:S(2)}) collective-permute-start(bf16[192,768]{1,0:T(8,128)(2,1)S(1)} %collective-permute-done.2.refs_0_), channel_id=1, source_target_pairs={{0,8},{1,9},{2,10},{3,11},{4,12},{5,13},{6,14},{7,15},{8,0},{9,1},... | collective-permute-start | bytes 884744 | tf_op jit(solution)/shard_map/ppermute | solution.py:578
  17.4 13.8 %collective-permute-start.5 = (bf16[192,768]{1,0:T(8,128)(2,1)S(1)}, bf16[192,768]{1,0:T(8,128)(2,1)S(1)}, u32[]{:S(2)}, u32[]{:S(2)}) collective-permute-start(bf16[192,768]{1,0:T(8,128)(2,1)S(1)} %collective-permute-done.2.refs_0_), channel_id=1, source_target_pairs={{0,12},{1,13},{2,14},{3,15},{4,8},{5,9},{6,10},{7,11},{8,4},{9,5},... | collective-permute-start | bytes 884744 | tf_op jit(solution)/shard_map/ppermute | solution.py:578
  31.7 15.2 %collective-permute-start.10 = (bf16[384,768]{1,0:T(8,128)(2,1)}, bf16[384,768]{1,0:T(8,128)(2,1)}, u32[]{:S(2)}, u32[]{:S(2)}) collective-permute-start(bf16[384,768]{1,0:T(8,128)(2,1)} %collective-permute-done.r_6_), channel_id=1, source_target_pairs={{0,4},{1,5},{2,6},{3,7},{4,0},{5,1},{6,2},{7,3},{8,12},{9,13},{10,... | collective-permute-start | bytes 1769480 | tf_op jit(solution)/shard_map/ppermute | solution.py:578
  33.0 14.9 %collective-permute-start.11 = (bf16[384,768]{1,0:T(8,128)(2,1)}, bf16[384,768]{1,0:T(8,128)(2,1)}, u32[]{:S(2)}, u32[]{:S(2)}) collective-permute-start(bf16[384,768]{1,0:T(8,128)(2,1)} %collective-permute-done.r_6_), channel_id=1, source_target_pairs={{0,8},{1,9},{2,10},{3,11},{4,12},{5,13},{6,14},{7,15},{8,0},{9,1},... | collective-permute-start | bytes 1769480 | tf_op jit(solution)/shard_map/ppermute | solution.py:578
  34.3 16.0 %collective-permute-start.13 = (bf16[512,768]{1,0:T(8,128)(2,1)S(1)}, bf16[512,768]{1,0:T(8,128)(2,1)S(1)}, u32[]{:S(2)}, u32[]{:S(2)}) collective-permute-start(bf16[512,768]{1,0:T(8,128)(2,1)S(1)} %copy-done.4), channel_id=1, source_target_pairs={{0,2},{1,3},{2,0},{3,1},{4,6},{5,7},{6,4},{7,5},{8,10},{9,11},{10,... | collective-permute-start | bytes 2359304 | tf_op jit(solution)/shard_map/ppermute | solution.py:578
  49.1 20.6 %collective-permute-start.14 = (bf16[384,768]{1,0:T(8,128)(2,1)}, bf16[384,768]{1,0:T(8,128)(2,1)}, u32[]{:S(2)}, u32[]{:S(2)}) collective-permute-start(bf16[384,768]{1,0:T(8,128)(2,1)} %collective-permute-done.r_6_), channel_id=1, source_target_pairs={{0,12},{1,13},{2,14},{3,15},{4,8},{5,9},{6,10},{7,11},{8,4},{9,5},... | collective-permute-start | bytes 1769480 | tf_op jit(solution)/shard_map/ppermute | solution.py:578
  68.4 17.6 %collective-permute-start.15 = (bf16[384,768]{1,0:T(8,128)(2,1)}, bf16[384,768]{1,0:T(8,128)(2,1)S(1)}, u32[]{:S(2)}, u32[]{:S(2)}) collective-permute-start(bf16[384,768]{1,0:T(8,128)(2,1)} %get-tuple-element.187), channel_id=1, source_target_pairs={{0,4},{1,5},{2,6},{3,7},{4,0},{5,1},{6,2},{7,3},{8,12},{9,13},{10,... | collective-permute-start | bytes 1769480 | tf_op jit(solution)/shard_map/ppermute | solution.py:578
  86.7 18.2 %collective-permute-start.19 = (bf16[192,768]{1,0:T(8,128)(2,1)S(1)}, bf16[192,768]{1,0:T(8,128)(2,1)S(1)}, u32[]{:S(2)}, u32[]{:S(2)}) collective-permute-start(bf16[192,768]{1,0:T(8,128)(2,1)S(1)} %add_convert_fusion.15), channel_id=1, source_target_pairs={{0,8},{1,9},{2,10},{3,11},{4,12},{5,13},{6,14},{7,15},{8,0},{9,1},... | collective-permute-start | bytes 884744 | tf_op jit(solution)/shard_map/ppermute | solution.py:578
  87.2 17.8 %collective-permute-start.18 = (bf16[384,768]{1,0:T(8,128)(2,1)}, bf16[384,768]{1,0:T(8,128)(2,1)S(1)}, u32[]{:S(2)}, u32[]{:S(2)}) collective-permute-start(bf16[384,768]{1,0:T(8,128)(2,1)} %get-tuple-element.203), channel_id=1, source_target_pairs={{0,4},{1,5},{2,6},{3,7},{4,0},{5,1},{6,2},{7,3},{8,12},{9,13},{10,... | collective-permute-start | bytes 1769480 | tf_op jit(solution)/shard_map/ppermute | solution.py:578
  88.4 16.6 %collective-permute-start.20 = (bf16[384,768]{1,0:T(8,128)(2,1)}, bf16[384,768]{1,0:T(8,128)(2,1)S(1)}, u32[]{:S(2)}, u32[]{:S(2)}) collective-permute-start(bf16[384,768]{1,0:T(8,128)(2,1)} %get-tuple-element.208), channel_id=1, source_target_pairs={{0,1},{1,0},{2,3},{3,2},{4,5},{5,4},{6,7},{7,6},{8,9},{9,8},{10,11... | collective-permute-start | bytes 1769480 | tf_op jit(solution)/shard_map/ppermute | solution.py:578
  106.0 17.1 %collective-permute-start.24 = (bf16[384,768]{1,0:T(8,128)(2,1)}, bf16[384,768]{1,0:T(8,128)(2,1)}, u32[]{:S(2)}, u32[]{:S(2)}) collective-permute-start(bf16[384,768]{1,0:T(8,128)(2,1)} %get-tuple-element.217), channel_id=1, source_target_pairs={{0,1},{1,0},{2,3},{3,2},{4,5},{5,4},{6,7},{7,6},{8,9},{9,8},{10,11... | collective-permute-start | bytes 1769480 | tf_op jit(solution)/shard_map/ppermute | solution.py:578
  107.0 16.1 %collective-permute-start.21 = (bf16[192,768]{1,0:T(8,128)(2,1)}, bf16[192,768]{1,0:T(8,128)(2,1)}, u32[]{:S(2)}, u32[]{:S(2)}) collective-permute-start(bf16[192,768]{1,0:T(8,128)(2,1)} %add_convert_fusion.14), channel_id=1, source_target_pairs={{0,8},{1,9},{2,10},{3,11},{4,12},{5,13},{6,14},{7,15},{8,0},{9,1},... | collective-permute-start | bytes 884744 | tf_op jit(solution)/shard_map/ppermute | solution.py:578
  110.9 14.7 %collective-permute-start.23 = (bf16[384,768]{1,0:T(8,128)(2,1)S(1)}, bf16[384,768]{1,0:T(8,128)(2,1)}, u32[]{:S(2)}, u32[]{:S(2)}) collective-permute-start(bf16[384,768]{1,0:T(8,128)(2,1)S(1)} %add_convert_fusion.2), channel_id=1, source_target_pairs={{0,4},{1,5},{2,6},{3,7},{4,0},{5,1},{6,2},{7,3},{8,12},{9,13},{10,... | collective-permute-start | bytes 1769480 | tf_op jit(solution)/shard_map/ppermute | solution.py:578
  130.5 19.2 %collective-permute-start.27 = (bf16[384,768]{1,0:T(8,128)(2,1)}, bf16[384,768]{1,0:T(8,128)(2,1)}, u32[]{:S(2)}, u32[]{:S(2)}) collective-permute-start(bf16[384,768]{1,0:T(8,128)(2,1)} %add_convert_fusion.1), channel_id=1, source_target_pairs={{0,4},{1,5},{2,6},{3,7},{4,0},{5,1},{6,2},{7,3},{8,12},{9,13},{10,... | collective-permute-start | bytes 1769480 | tf_op jit(solution)/shard_map/ppermute | solution.py:578
  132.7 18.1 %collective-permute-start.30 = (bf16[192,768]{1,0:T(8,128)(2,1)}, bf16[192,768]{1,0:T(8,128)(2,1)}, u32[]{:S(2)}, u32[]{:S(2)}) collective-permute-start(bf16[192,768]{1,0:T(8,128)(2,1)} %add_convert_fusion.12), channel_id=1, source_target_pairs={{0,8},{1,9},{2,10},{3,11},{4,12},{5,13},{6,14},{7,15},{8,0},{9,1},... | collective-permute-start | bytes 884744 | tf_op jit(solution)/shard_map/ppermute | solution.py:578
  136.9 21.5 %collective-permute-start.32 = (bf16[192,768]{1,0:T(8,128)(2,1)S(1)}, bf16[192,768]{1,0:T(8,128)(2,1)S(1)}, u32[]{:S(2)}, u32[]{:S(2)}) collective-permute-start(bf16[192,768]{1,0:T(8,128)(2,1)S(1)} %add_convert_fusion.11), channel_id=1, source_target_pairs={{0,16},{1,17},{2,18},{3,19},{4,20},{5,21},{6,22},{7,23},{8,24},{9,... | collective-permute-start | bytes 884744 | tf_op jit(solution)/shard_map/ppermute | solution.py:578
  139.3 24.8 %collective-permute-start.26 = (bf16[384,768]{1,0:T(8,128)(2,1)}, bf16[384,768]{1,0:T(8,128)(2,1)}, u32[]{:S(2)}, u32[]{:S(2)}) collective-permute-start(bf16[384,768]{1,0:T(8,128)(2,1)} %add_convert_fusion), channel_id=1, source_target_pairs={{0,4},{1,5},{2,6},{3,7},{4,0},{5,1},{6,2},{7,3},{8,12},{9,13},{10,... | collective-permute-start | bytes 1769480 | tf_op jit(solution)/shard_map/ppermute | solution.py:578
  165.3 15.5 %collective-permute-start.38 = (bf16[192,768]{1,0:T(8,128)(2,1)S(1)}, bf16[192,768]{1,0:T(8,128)(2,1)S(1)}, u32[]{:S(2)}, u32[]{:S(2)}) collective-permute-start(bf16[192,768]{1,0:T(8,128)(2,1)S(1)} %add_convert_fusion.6), channel_id=1, source_target_pairs={{0,8},{1,9},{2,10},{3,11},{4,12},{5,13},{6,14},{7,15},{8,0},{9,1},... | collective-permute-start | bytes 884744 | tf_op jit(solution)/shard_map/ppermute | solution.py:578
  165.3 15.4 %collective-permute-start.39 = (bf16[192,768]{1,0:T(8,128)(2,1)S(1)}, bf16[192,768]{1,0:T(8,128)(2,1)S(1)}, u32[]{:S(2)}, u32[]{:S(2)}) collective-permute-start(bf16[192,768]{1,0:T(8,128)(2,1)S(1)} %add_convert_fusion.7), channel_id=1, source_target_pairs={{0,16},{1,17},{2,18},{3,19},{4,20},{5,21},{6,22},{7,23},{8,24},{9,... | collective-permute-start | bytes 884744 | tf_op jit(solution)/shard_map/ppermute | solution.py:578
  180.8 15.7 %collective-permute-start.41 = (bf16[192,768]{1,0:T(8,128)(2,1)S(1)}, bf16[192,768]{1,0:T(8,128)(2,1)S(1)}, u32[]{:S(2)}, u32[]{:S(2)}) collective-permute-start(bf16[192,768]{1,0:T(8,128)(2,1)S(1)} %add_convert_fusion.5.refs_8_), channel_id=1, source_target_pairs={{0,4},{1,5},{2,6},{3,7},{4,0},{5,1},{6,2},{7,3},{8,12},{9,13},{10,... | collective-permute-start | bytes 884744 | tf_op jit(solution)/shard_map/ppermute | solution.py:578
  185.6 18.1 %collective-permute-start.43 = (bf16[192,768]{1,0:T(8,128)(2,1)S(1)}, bf16[192,768]{1,0:T(8,128)(2,1)S(1)}, u32[]{:S(2)}, u32[]{:S(2)}) collective-permute-start(bf16[192,768]{1,0:T(8,128)(2,1)S(1)} %add_convert_fusion.5.refs_8_), channel_id=1, source_target_pairs={{0,12},{1,13},{2,14},{3,15},{4,8},{5,9},{6,10},{7,11},{8,4},{9,5},... | collective-permute-start | bytes 884744 | tf_op jit(solution)/shard_map/ppermute | solution.py:578
  186.6 17.2 %collective-permute-start.44 = (bf16[192,768]{1,0:T(8,128)(2,1)S(1)}, bf16[192,768]{1,0:T(8,128)(2,1)S(1)}, u32[]{:S(2)}, u32[]{:S(2)}) collective-permute-start(bf16[192,768]{1,0:T(8,128)(2,1)S(1)} %collective-permute-done.36.refs_2_), channel_id=1, source_target_pairs={{0,4},{1,5},{2,6},{3,7},{4,0},{5,1},{6,2},{7,3},{8,12},{9,13},{10,... | collective-permute-start | bytes 884744 | tf_op jit(solution)/shard_map/ppermute | solution.py:578
  (77 other events, 511.2 us)
